TPU v7x, 32 devices: a whole 2x2x4 slice. The times are simulated.
32 devices in a mesh: seq: 8 (over z, x), head: 4 (over y, core).
Axes of the slice: x: 2, y: 2, z: 4, core: 2. Of those that a mesh axis runs over, the one named last changes fastest.
Arguments:
- queries: bfloat16 [2048, 2048], P('seq', 'head'), may hold values from -1.75 to 1.75
- keys: bfloat16 [2048, 2048], P('seq', 'head'), may hold values from -1.75 to 1.75
- values: bfloat16 [2048, 2048], P('seq', 'head'), may hold values from -6 to 6
- level_table: float32 [16, 16], P(None, 'head'), may hold values from 0.05 to 1
- level_code: int32 [2048, 6], P('seq'), may hold values from 0 to 15
- out_weight: bfloat16 [2048, 2048], P('head'), may hold values from -0.125 to 0.125
- cotangent: bfloat16 [2048, 2048], P('seq', 'head'), may hold values from -8 to 8
Outputs:
- mixed: bfloat16 [2048, 2048], P('seq', 'head')
- out_weight_grad: float32 [2048, 2048], P('seq', 'head')
- query_grad: bfloat16 [2048, 2048], P('seq', 'head')
- key_grad: bfloat16 [2048, 2048], P('seq', 'head')
- value_grad: bfloat16 [2048, 2048], P('seq', 'head')
- table_grad: float32 [16, 16], P(None, 'head')
All inputs are finite; a program needn't handle non-finite values.
Results may differ from a plain program's by a relative error of at most 0.015.
Values may be sent and summed in bfloat16 or wider, within the bound.
No kernel may reach another device: no remote copies, remote signals or barrier semaphores. Data moves between devices by JAX's collectives and lax.ppermute only.
A program may use at most 128 MiB of HBM per device.

v0:
```python
import math

import jax
import jax.numpy as jnp
from jax import lax
from jax.sharding import PartitionSpec as P

SPAN = 64


HIGHEST_PRECISION = lax.Precision.HIGHEST


def partner_2(value, axis, apart):
    mask = 2**apart
    pairs = [(source, source ^ mask) for source in range(lax.axis_size(axis))]
    return lax.ppermute(value, axis, pairs)


def split_einsum(form, left, right):
    if left.dtype == jnp.float32:
        high = left.astype(jnp.bfloat16)
        rest = (left - high.astype(jnp.float32)).astype(jnp.bfloat16)
        return jnp.einsum(form, high, right, preferred_element_type=jnp.float32) + jnp.einsum(
            form, rest, right, preferred_element_type=jnp.float32
        )
    high = right.astype(jnp.bfloat16)
    rest = (right - high.astype(jnp.float32)).astype(jnp.bfloat16)
    return jnp.einsum(form, left, high, preferred_element_type=jnp.float32) + jnp.einsum(
        form, left, rest, preferred_element_type=jnp.float32
    )


def upper_half(array, bit_index):
    group_size = 2 ** (bit_index + 1)
    grouped = array.reshape((array.shape[0] // group_size, group_size) + array.shape[1:])
    return grouped[:, group_size // 2 :]


def lower_sum(array, bit_index):
    group_size = 2 ** (bit_index + 1)
    grouped = array.reshape((array.shape[0] // group_size, group_size) + array.shape[1:])
    return jnp.sum(grouped[:, : group_size // 2], axis=1)


def place_upper(piece_array, bit_index):
    group_size = 2 ** (bit_index + 1)
    joined = jnp.concatenate([jnp.zeros_like(piece_array), piece_array], axis=1)
    return joined.reshape((piece_array.shape[0] * group_size,) + piece_array.shape[2:])


def spread_lower(piece_array, bit_index):
    group_size = 2 ** (bit_index + 1)
    filled = jnp.broadcast_to(
        piece_array[:, None], (piece_array.shape[0], group_size // 2) + piece_array.shape[1:]
    )
    joined = jnp.concatenate([filled, jnp.zeros_like(filled)], axis=1)
    return joined.reshape((piece_array.shape[0] * group_size,) + piece_array.shape[1:])


def lower_blocks(device_state, position, seq_bits):
    block_state = device_state
    found_states = []
    for bit_index in range(seq_bits):
        partner = partner_2(block_state.astype(jnp.bfloat16), "seq", bit_index).astype(
            block_state.dtype
        )
        bit_owned = (position >> bit_index & 1).astype(jnp.float32)
        found_states.append(partner * bit_owned)
        block_state = block_state + partner
    return found_states


def upper_blocks(device_terms, position, seq_bits):
    stacked_terms = device_terms
    gathered = jnp.zeros_like(device_terms[0])
    for bit_index in range(seq_bits):
        partner = partner_2(stacked_terms.astype(jnp.bfloat16), "seq", bit_index).astype(
            stacked_terms.dtype
        )
        bit_owned = (position >> bit_index & 1).astype(jnp.float32)
        gathered = gathered + (1.0 - bit_owned) * partner[0]
        stacked_terms = stacked_terms[1:] + partner[1:]
    return gathered


def per_device(queries, keys, values, level_table, level_code, out_weight, cotangent):
    tok_rows = queries.shape[0]
    heads_here = level_table.shape[1]
    head_size = queries.shape[1] // heads_here
    span_len = SPAN
    spans_here = tok_rows // span_len
    local_bits = spans_here.bit_length() - 1
    seq_count = lax.axis_size("seq")
    seq_bits = seq_count.bit_length() - 1
    level_count = 1 + local_bits + seq_bits
    position = lax.axis_index("seq")
    four_shape = (spans_here, span_len, heads_here, head_size)
    scales = [
        1.0 / math.sqrt(span_len * 2 ** max(level_index - 1, 0))
        for level_index in range(level_count)
    ]
    code_count = level_table.shape[0]
    one_hot = (
        level_code[:, :, None] == jnp.arange(code_count, dtype=jnp.int32)[None, None, :]
    ).astype(jnp.float32)
    lookup = jnp.einsum("tlc,ch->tlh", one_hot, level_table, precision=HIGHEST_PRECISION)
    lookup = lookup.reshape(spans_here, span_len, level_count, heads_here)
    level_coef = lookup * jnp.asarray(scales, jnp.float32)[None, None, :, None]
    full_rows = lax.all_gather(cotangent, "head", axis=1, tiled=True)
    grad_attn = jnp.einsum(
        "tj,ij->ti", full_rows, out_weight, preferred_element_type=jnp.float32
    ).astype(jnp.bfloat16)
    q_half = queries.reshape(four_shape)
    k_half = keys.reshape(four_shape)
    v_half = values.reshape(four_shape)
    g_half = grad_attn.reshape(four_shape)
    causal = (jnp.arange(span_len)[:, None] >= jnp.arange(span_len)[None, :]).astype(jnp.float32)
    scores = (
        jnp.einsum("jchd,jshd->jhcs", q_half, k_half, preferred_element_type=jnp.float32) * causal
    )
    level_reads = [split_einsum("jhcs,jshe->jche", scores, v_half) * scales[0]]
    span_states = jnp.einsum("jchd,jche->jhde", k_half, v_half, preferred_element_type=jnp.float32)
    local_lower = []
    for bit_index in range(local_bits):
        lower_state = lower_sum(span_states, bit_index)
        local_lower.append(lower_state)
        upper_reads = split_einsum("gjchd,ghde->gjche", upper_half(q_half, bit_index), lower_state)
        level_reads.append(place_upper(upper_reads, bit_index) * scales[1 + bit_index])
    device_state = jnp.sum(span_states, axis=0)
    scaled_seq = g_half[:, :, None] * level_coef[:, :, 1 + local_bits :, :, None]
    device_terms = split_einsum("jchd,jclhe->lhde", q_half, scaled_seq)
    found_states = lower_blocks(device_state, position, seq_bits)
    gathered = upper_blocks(device_terms, position, seq_bits)
    for bit_index in range(seq_bits):
        level_reads.append(
            split_einsum("jchd,hde->jche", q_half, found_states[bit_index])
            * scales[1 + local_bits + bit_index]
        )
    attention = jnp.zeros(four_shape, jnp.float32)
    for level_index in range(level_count):
        attention = attention + lookup[:, :, level_index, :, None] * level_reads[level_index]
    attn_rows = attention.reshape(tok_rows, heads_here * head_size).astype(jnp.bfloat16)
    partial_value = jnp.dot(attn_rows, out_weight, preferred_element_type=jnp.float32)
    mixed = lax.psum_scatter(
        partial_value.astype(jnp.bfloat16), "head", scatter_dimension=1, tiled=True
    )
    weight_norm = 1.0 / math.sqrt(tok_rows * seq_count)
    out_weight_grad = lax.psum_scatter(
        jnp.einsum("tj,ti->ji", full_rows, attn_rows, preferred_element_type=jnp.float32)
        * weight_norm,
        "seq",
        scatter_dimension=0,
        tiled=True,
    )
    level_grads = jnp.stack(
        [jnp.sum(g_half * level_reads[level_index], axis=3) for level_index in range(level_count)],
        axis=2,
    )
    table_norm = 1.0 / math.sqrt(tok_rows * seq_count * level_count)
    table_part = (
        jnp.einsum(
            "tlc,tlh->ch",
            one_hot,
            level_grads.reshape(tok_rows, level_count, heads_here),
            precision=HIGHEST_PRECISION,
        )
        * table_norm
    )
    table_grad = lax.psum(table_part, "seq")
    within_coef = jnp.transpose(level_coef[:, :, 0, :], (0, 2, 1))[:, :, :, None]
    score_grads = (
        jnp.einsum("jche,jshe->jhcs", g_half, v_half, preferred_element_type=jnp.float32)
        * causal
        * within_coef
    )
    query_grad = split_einsum("jhcs,jshd->jchd", score_grads, k_half)
    key_grad = split_einsum("jhcs,jchd->jshd", score_grads, q_half)
    value_grad = split_einsum("jhcs,jche->jshe", scores * within_coef, g_half)
    upper_terms = jnp.zeros_like(span_states)
    for bit_index in range(local_bits):
        coef_here = level_coef[:, :, 1 + bit_index, :, None]
        query_part = upper_half(coef_here, bit_index) * split_einsum(
            "gjche,ghde->gjchd", upper_half(g_half, bit_index), local_lower[bit_index]
        )
        query_grad = query_grad + place_upper(query_part, bit_index)
        scaled_grads = upper_half(g_half * coef_here, bit_index)
        block_terms = split_einsum("gjchd,gjche->ghde", upper_half(q_half, bit_index), scaled_grads)
        upper_terms = upper_terms + spread_lower(block_terms, bit_index)
    for bit_index in range(seq_bits):
        coef_here = level_coef[:, :, 1 + local_bits + bit_index, :, None]
        query_grad = query_grad + coef_here * split_einsum(
            "jche,hde->jchd", g_half, found_states[bit_index]
        )
    states_back = upper_terms + gathered[None]
    key_grad = key_grad + split_einsum("jhde,jche->jchd", states_back, v_half)
    value_grad = value_grad + split_einsum("jhde,jchd->jche", states_back, k_half)
    flat_shape = (tok_rows, heads_here * head_size)
    return (
        mixed,
        out_weight_grad,
        query_grad.reshape(flat_shape).astype(jnp.bfloat16),
        key_grad.reshape(flat_shape).astype(jnp.bfloat16),
        value_grad.reshape(flat_shape).astype(jnp.bfloat16),
        table_grad,
    )


def solution(mesh):
    placed = (
        P("seq", "head"),
        P("seq", "head"),
        P("seq", "head"),
        P(None, "head"),
        P("seq", None),
        P("head", None),
        P("seq", "head"),
    )
    return jax.shard_map(
        per_device,
        mesh=mesh,
        in_specs=placed,
        out_specs=(
            P("seq", "head"),
            P("seq", "head"),
            P("seq", "head"),
            P("seq", "head"),
            P("seq", "head"),
            P(None, "head"),
        ),
        check_vma=False,
    )
```

profile of v0, /device:TPU:0, one launch (start us, length us, event | category | flops | bytes accessed | tf_op | source)
XLA Modules:
  0.0 191.6 jit_solution(12065787987830475894)
XLA Ops:
  7.2 1.9 reshape.213
  10.1 1.3 fusion.171
  12.8 3.0 %collective-permute-start = (bf16[4,128,128]{2,1,0:T(8,128)(2,1)}, bf16[4,128,128]{2,1,0:T(8,128)(2,1)S(1)}, u32[]{:S(2)}, u32[]{:S(2)}) collective-permute-start(bf16[4,128,128]{2,1,0:T(8,128)(2,1)} %convert_element_type.273), channel_id=1, source_target_pairs={{0,4},{4,0},{8,12},{12,8},{16,20},{20,16},{24,28},{28,24},{1,5},{5... | collective-permute-start | bytes 393224 | tf_op jit(solution)/shard_map/ppermute | solution.py:17
  15.8 1.7 reshape.212
  17.6 1.7 reshape_reshape.14
  19.3 1.7 reshape_reshape.15
  25.6 1.3 fusion.128
  26.9 2.0 %fusion.19 = f32[2,1,64,4,128]{4,2,3,1,0:T(8,128)} fusion(f32[2,4,128,64]{2,3,1,0:T(8,128)S(1)} %fusion.128, bf16[2,1,64,4,128]{4,3,2,1,0:T(4,128)(2,1)S(1)} %slice.119, f32[2,2,4,128,128]{4,3,2,1,0:T(8,128)} %bitcast.372), kind=kOutput, calls=%fused_computation.36 | convolution fusion | flops 17367040 | bytes 1179648 | tf_op jit(solution)/shard_map/gjchd,ghde->gjche/dot_general | solution.py:29
  28.9 1.3 convolution_multiply_fusion.1
  32.0 1.4 reshape.215
  33.5 1.8 concatenate.19.clone
  35.2 1.8 fusion.61
  37.0 1.5 broadcast_multiply_fusion
  39.2 1.6 collective-permute-start.1
  42.8 1.4 collective-permute-done.1
  44.2 2.7 %collective-permute-start.2 = (bf16[4,128,128]{2,1,0:T(8,128)(2,1)S(1)}, bf16[4,128,128]{2,1,0:T(8,128)(2,1)S(1)}, u32[]{:S(2)}, u32[]{:S(2)}) collective-permute-start(bf16[4,128,128]{2,1,0:T(8,128)(2,1)S(1)} %fusion.54), channel_id=1, source_target_pairs={{0,16},{4,20},{8,24},{12,28},{16,0},{20,4},{24,8},{28,12},{1,17},{... | collective-permute-start | bytes 393224 | tf_op jit(solution)/shard_map/ppermute | solution.py:17
  48.9 2.9 %collective-permute-done.2 = bf16[4,128,128]{2,1,0:T(8,128)(2,1)S(1)} collective-permute-done((bf16[4,128,128]{2,1,0:T(8,128)(2,1)S(1)}, bf16[4,128,128]{2,1,0:T(8,128)(2,1)S(1)}, u32[]{:S(2)}, u32[]{:S(2)}) %collective-permute-start.2) | collective-permute-done | bytes 131104 | tf_op jit(solution)/shard_map/ppermute | solution.py:17
  53.9 2.0 %convolution_convert_fusion.1 = bf16[256,512]{1,0:T(8,128)(2,1)S(1)} fusion(bf16[256,2048]{1,0:T(8,128)(2,1)} %all-gather.2.cloned.1.call-done, bf16[512,2048]{1,0:T(8,128)(2,1)S(1)} %copy-done), kind=kOutput, calls=%fused_computation.34 | convolution fusion | flops 537001984 | bytes 3407872 | tf_op jit(solution)/shard_map/tj,ij->ti/dot_general | solution.py:111
  55.9 4.5 %fusion.39 = (f32[4,64,4]{1,2,0:T(4,128)}, f32[4,64,4]{1,2,0:T(4,128)}, f32[4,64,4]{1,2,0:T(4,128)}, f32[4,64,4]{1,2,0:T(4,128)}, f32[4,64,4]{1,2,0:T(4,128)}, /...) fusion(f32[4,128,4,64]{1,3,2,0:T(8,128)} %bitcast.385, f32[4,128,4,64]{1,3,2,0:T(8,128)} %bitcast.384, ...), kind=kOutput, calls=%fused_computation.67 | convolution fusion | flops 21620736 | bytes 6078464 | tf_op jit(solution)/shard_map/jhcs,jshe->jche/dot_general | solution.py:24
  60.7 2.7 %multiply_bitcast_fusion = f32[2048,512]{0,1:T(8,128)} fusion(bf16[256,2048]{1,0:T(8,128)(2,1)S(1)} %copy-done.37, bf16[32,8,4,128]{3,2,1,0:T(4,128)(2,1)S(1)} %bitcast.378), kind=kOutput, calls=%fused_computation | convolution fusion | flops 537919488 | bytes 5505024 | tf_op jit(solution)/shard_map/tj,ti->ji/dot_general | solution.py:150
  65.0 1.4 slice_bitcast_fusion.5
  71.0 1.4 stack.21
  73.7 1.4 stack.22
  75.1 1.3 copy.250
  76.4 1.4 stack.23
  77.7 1.3 copy.251
  79.0 1.4 stack.24
  80.4 1.3 copy.252
  81.7 1.4 stack.25
  83.1 1.3 copy.253
  84.4 1.4 stack.26
  85.7 2.0 %convolution_bitcast_fusion = f32[4,3,128,128]{3,2,1,0:T(8,128)S(1)} fusion(f32[4,64,3,4]{1,0,2,3:T(4,128)} %copy.234, bf16[4,64,4,128,1]{3,2,1,0,4:T(4,128)(2,1)} %bitcast.375, bf16[4,64,4,128]{3,2,1,0:T(4,128)(2,1)S(1)} %reshape.222), kind=kOutput, calls=%fused_computation.5 | convolution fusion | flops 102760448 | bytes 1323008 | tf_op jit(solution)/shard_map/jchd,jclhe->lhde/dot_general | solution.py:29
  87.9 2.1 %fusion.172 = (bf16[3,4,128,128]{2,3,0,1:T(8,128)(2,1)}, f32[3,4,128,128]{2,3,0,1:T(8,128)}) fusion(f32[4,3,128,128]{3,2,1,0:T(8,128)S(1)} %convolution_bitcast_fusion, bf16[4,64,4,128,1]{3,2,1,0,4:T(4,128)(2,1)S(1)} %bitcast.376, f32[4,64,3,4]{1,0,2,3:T(4,128)S(1)} %copy-done.41, bf16[4,64,4,128]{3,2,1,0:T(4,128)(2,1)S(1)} %reshape.222), kind=kOutput, calls=%fused_computation.255 | convolution fusion | flops 101974016 | bytes 2502656 | tf_op jit(solution)/shard_map/jchd,jclhe->lhde/dot_general | solution.py:29
  93.1 1.4 fusion.83
  104.1 1.7 convolution_convert_fusion
  107.1 3.6 %fusion.16 = bf16[4,64,4,128]{3,1,2,0:T(8,128)(2,1)} fusion(f32[4,64,4,128]{3,1,2,0:T(8,128)S(1)} %bitcast.392, f32[4,4,64,128]{3,2,1,0:T(8,128)} %fusion.123, f32[4,128,4,64]{1,3,2,0:T(8,128)} %bitcast.387, f32[4,128,4,64]{1,3,2,0:T(8,128)} %bitcast.386, f32[4,128,4,64]{1,3,2,0:T(8,128)} %bitcast.389, f32[4,128,4,64]{1,3,2,0:T(8,128)} %bitcast.388, ...), kind=kOutput, calls=%fused_computation.31 | convolution fusion | flops 18743296 | bytes 5255168 | tf_op jit(solution)/shard_map/jhcs,jshd->jchd/dot_general | solution.py:24
  113.9 1.3 fusion.3
  115.3 2.1 %copy.275 = f32[2,1,4,128,128]{4,3,2,1,0:T(8,128)} copy(f32[2,1,4,128,128]{3,4,2,0,1:T(8,128)} %fusion.3) | data formatting | bytes 1048576
  117.4 2.1 %concatenate.23.clone = f32[2,2,4,128,128]{4,3,2,1,0:T(8,128)} pad(f32[2,1,4,128,128]{4,3,2,1,0:T(8,128)} %copy.275, f32[]{:T(128)} %constant.16.clone.1), padding=0_0x0_1x0_0x0_0x0_0 | pad | bytes 1572868 | tf_op jit(solution)/shard_map/concatenate | solution.py:57
  119.5 1.8 copy.231
  123.2 21.9 %psum.7 = f32[16,4]{0,1:T(4,128)} all-reduce(f32[16,4]{0,1:T(4,128)S(1)} %fusion.26), channel_id=1, replica_groups=mesh['seq'=8,'head'=4] {'seq'}, use_global_device_ids=true, to_apply=%region_10.0 | all-reduce | flops 64 | bytes 512 | tf_op jit(solution)/shard_map/psum | solution.py:170
  145.1 2.3 %fusion.47 = f32[4,4,128,64]{2,3,1,0:T(8,128)} fusion(f32[4,4,64,64]{3,2,1,0:T(8,128)S(1)} %convolution_multiply_fusion.1, f32[4,4,64]{2,1,0:T(4,128)S(1)} %get-tuple-element.41, bf16[4,64,4,128]{3,2,1,0:T(4,128)(2,1)} %copy-done.3), kind=kOutput, calls=%fused_computation.101 | convolution fusion | flops 16908288 | bytes 1052672 | tf_op jit(solution)/shard_map/jhcs,jche->jshe/dot_general | solution.py:24
  149.6 7.5 %collective-permute-done.5 = bf16[1,4,128,128]{2,3,0,1:T(8,128)(2,1)S(1)} collective-permute-done((bf16[1,4,128,128]{2,3,0,1:T(8,128)(2,1)S(1)}, bf16[1,4,128,128]{2,3,0,1:T(8,128)(2,1)S(1)}, u32[]{:S(2)}, u32[]{:S(2)}) %collective-permute-start.5) | collective-permute-done | bytes 131104 | tf_op jit(solution)/shard_map/ppermute | solution.py:17
  157.1 1.7 fusion.60
  158.9 1.8 copy.237
  161.7 1.6 subtract_convert_fusion
  167.4 2.1 %copy.254 = f32[256,512]{1,0:T(8,128)} copy(f32[256,512]{0,1:T(8,128)} %reduce-scatter.5.cloned.1.call-done) | data formatting | bytes 1048576
  169.5 15.6 %reduce-scatter.3.cloned.1.call-done = bf16[256,512]{1,0:T(8,128)(2,1)} async-done(((bf16[256,2048]{1,0:T(8,128)(2,1)}), bf16[256,512]{1,0:T(8,128)(2,1)}) %reduce-scatter.3.cloned.1.call-update) | async-done | bytes 262160 | tf_op jit(solution)/shard_map/reduce_scatter | solution.py:145
  (211 shorter events, 49.7 us)
Async XLA Ops:
  7.2 46.7 %copy-start = (bf16[512,2048]{1,0:T(8,128)(2,1)S(1)}, bf16[512,2048]{1,0:T(8,128)(2,1)}, u32[]{:S(2)}) copy-start(bf16[512,2048]{1,0:T(8,128)(2,1)} %param.13) | copy-start | bytes 6291460
  7.2 46.7 %all-gather.2.cloned.1.call-start = ((), (), s32[]{:S(2)}) async-start(), calls=%async_computation.3 | async-start | bytes 1310720 | tf_op jit(solution)/shard_map/all_gather | solution.py:110
  11.4 11.6 %copy-start.1 = (f32[4,4,128,128]{3,2,1,0:T(8,128)}, f32[4,4,128,128]{3,2,1,0:T(8,128)S(1)}, u32[]{:S(2)}) copy-start(f32[4,4,128,128]{3,2,1,0:T(8,128)S(1)} %get-tuple-element.51) | copy-start | bytes 3145732
  12.8 26.3 %collective-permute-start = (bf16[4,128,128]{2,1,0:T(8,128)(2,1)}, bf16[4,128,128]{2,1,0:T(8,128)(2,1)S(1)}, u32[]{:S(2)}, u32[]{:S(2)}) collective-permute-start(bf16[4,128,128]{2,1,0:T(8,128)(2,1)} %convert_element_type.273), channel_id=1, source_target_pairs={{0,4},{4,0},{8,12},{12,8},{16,20},{20,16},{24,28},{28,24},{1,5},{5... | collective-permute-start | bytes 393224 | tf_op jit(solution)/shard_map/ppermute | solution.py:17
  15.8 151.6 %reduce-scatter.5.cloned.1.call-start = ((), (), s32[]{:S(2)}) async-start(), calls=%async_computation.4 | async-start | bytes 4718592 | tf_op jit(solution)/shard_map/reduce_scatter | solution.py:149
  21.0 3.5 %copy-start.8 = (bf16[4,64,4,128]{3,2,1,0:T(4,128)(2,1)S(1)}, bf16[4,64,4,128]{3,2,1,0:T(4,128)(2,1)}, u32[]{:S(2)}) copy-start(bf16[4,64,4,128]{3,2,1,0:T(4,128)(2,1)} %reshape.212) | copy-start | bytes 786436
  25.6 3.3 %copy-start.18 = (bf16[2,1,64,4,128]{4,3,2,1,0:T(4,128)(2,1)}, bf16[2,1,64,4,128]{4,3,2,1,0:T(4,128)(2,1)S(1)}, u32[]{:S(2)}) copy-start(bf16[2,1,64,4,128]{4,3,2,1,0:T(4,128)(2,1)S(1)} %slice.119) | copy-start | bytes 393220
  25.6 5.7 %copy-start.54 = (s32[256,6]{0,1:T(8,128)S(1)}, s32[256,6]{0,1:T(8,128)}, u32[]{:S(2)}) copy-start(s32[256,6]{0,1:T(8,128)} %param.12) | copy-start | bytes 18436
  25.6 5.7 %copy-start.56 = (f32[16,4]{0,1:T(4,128)S(1)}, f32[16,4]{0,1:T(4,128)}, u32[]{:S(2)}) copy-start(f32[16,4]{0,1:T(4,128)} %param.11) | copy-start | bytes 772
  28.9 8.2 %copy-start.59 = (f32[6]{0:T(128)S(1)}, f32[6]{0:T(128)}, u32[]{:S(2)}) copy-start(f32[6]{0:T(128)} %constant.13.clone) | copy-start | bytes 76
  28.9 10.3 %copy-start.15 = (f32[4,128,128]{2,1,0:T(8,128)S(1)}, f32[4,128,128]{2,1,0:T(8,128)}, u32[]{:S(2)}) copy-start(f32[4,128,128]{2,1,0:T(8,128)} %copy-done.14) | copy-start | bytes 786436
  39.2 5.0 %collective-permute-start.1 = (bf16[4,128,128]{2,1,0:T(8,128)(2,1)S(1)}, bf16[4,128,128]{2,1,0:T(8,128)(2,1)S(1)}, u32[]{:S(2)}, u32[]{:S(2)}) collective-permute-start(bf16[4,128,128]{2,1,0:T(8,128)(2,1)S(1)} %fusion.77), channel_id=1, source_target_pairs={{0,8},{4,12},{8,0},{12,4},{16,24},{20,28},{24,16},{28,20},{1,9},{5... | collective-permute-start | bytes 393224 | tf_op jit(solution)/shard_map/ppermute | solution.py:17
  44.2 3.7 %copy-start.16 = (bf16[4,128,128]{2,1,0:T(8,128)(2,1)}, bf16[4,128,128]{2,1,0:T(8,128)(2,1)S(1)}, u32[]{:S(2)}) copy-start(bf16[4,128,128]{2,1,0:T(8,128)(2,1)S(1)} %collective-permute-done.1) | copy-start | bytes 393220
  44.2 7.6 %collective-permute-start.2 = (bf16[4,128,128]{2,1,0:T(8,128)(2,1)S(1)}, bf16[4,128,128]{2,1,0:T(8,128)(2,1)S(1)}, u32[]{:S(2)}, u32[]{:S(2)}) collective-permute-start(bf16[4,128,128]{2,1,0:T(8,128)(2,1)S(1)} %fusion.54), channel_id=1, source_target_pairs={{0,16},{4,20},{8,24},{12,28},{16,0},{20,4},{24,8},{28,12},{1,17},{... | collective-permute-start | bytes 393224 | tf_op jit(solution)/shard_map/ppermute | solution.py:17
  55.8 4.6 %copy-start.26 = (bf16[256,512]{1,0:T(8,128)(2,1)}, bf16[256,512]{1,0:T(8,128)(2,1)S(1)}, u32[]{:S(2)}) copy-start(bf16[256,512]{1,0:T(8,128)(2,1)S(1)} %convolution_convert_fusion.1) | copy-start | bytes 786436
  55.9 31.9 %copy-start.3 = (bf16[4,64,4,128]{3,2,1,0:T(4,128)(2,1)}, bf16[4,64,4,128]{3,2,1,0:T(4,128)(2,1)S(1)}, u32[]{:S(2)}) copy-start(bf16[4,64,4,128]{3,2,1,0:T(4,128)(2,1)S(1)} %reshape.222) | copy-start | bytes 786436
  55.9 4.7 %copy-start.37 = (bf16[256,2048]{1,0:T(8,128)(2,1)S(1)}, bf16[256,2048]{1,0:T(8,128)(2,1)}, u32[]{:S(2)}) copy-start(bf16[256,2048]{1,0:T(8,128)(2,1)} %all-gather.2.cloned.1.call-done) | copy-start | bytes 3145732
  63.4 4.8 %copy-start.27 = (bf16[256,512]{1,0:T(8,128)(2,1)S(1)}, bf16[256,512]{1,0:T(8,128)(2,1)}, u32[]{:S(2)}) copy-start(bf16[256,512]{1,0:T(8,128)(2,1)} %copy-done.26) | copy-start | bytes 786436
  63.4 121.6 %reduce-scatter.3.cloned.1.call-start = ((), (), s32[]{:S(2)}) async-start(), calls=%async_computation.2 | async-start | bytes 1310720 | tf_op jit(solution)/shard_map/reduce_scatter | solution.py:145
  85.7 5.2 %copy-start.39 = (bf16[2,2,64,4,128]{4,3,2,1,0:T(4,128)(2,1)S(1)}, bf16[2,2,64,4,128]{4,3,2,1,0:T(4,128)(2,1)}, u32[]{:S(2)}) copy-start(bf16[2,2,64,4,128]{4,3,2,1,0:T(4,128)(2,1)} %reshape_reshape.16) | copy-start | bytes 786436
  85.7 5.2 %copy-start.38 = (bf16[1,4,64,4,128]{4,3,2,1,0:T(4,128)(2,1)S(1)}, bf16[1,4,64,4,128]{4,3,2,1,0:T(4,128)(2,1)}, u32[]{:S(2)}) copy-start(bf16[1,4,64,4,128]{4,3,2,1,0:T(4,128)(2,1)} %reshape_reshape.17) | copy-start | bytes 786436
  87.8 3.3 %copy-start.49 = (f32[256,1,4]{0,2,1:T(4,128)S(1)}, f32[256,1,4]{0,2,1:T(4,128)}, u32[]{:S(2)}) copy-start(f32[256,1,4]{0,2,1:T(4,128)} %stack.22) | copy-start | bytes 12292
  87.8 3.3 %copy-start.50 = (f32[256,1,4]{0,2,1:T(4,128)S(1)}, f32[256,1,4]{0,2,1:T(4,128)}, u32[]{:S(2)}) copy-start(f32[256,1,4]{0,2,1:T(4,128)} %stack.23) | copy-start | bytes 12292
  87.8 3.3 %copy-start.51 = (f32[256,1,4]{0,2,1:T(4,128)S(1)}, f32[256,1,4]{0,2,1:T(4,128)}, u32[]{:S(2)}) copy-start(f32[256,1,4]{0,2,1:T(4,128)} %stack.24) | copy-start | bytes 12292
  87.9 3.3 %copy-start.52 = (f32[256,1,4]{0,2,1:T(4,128)S(1)}, f32[256,1,4]{0,2,1:T(4,128)}, u32[]{:S(2)}) copy-start(f32[256,1,4]{0,2,1:T(4,128)} %stack.25) | copy-start | bytes 12292
  87.9 3.3 %copy-start.53 = (f32[256,1,4]{0,2,1:T(4,128)S(1)}, f32[256,1,4]{0,2,1:T(4,128)}, u32[]{:S(2)}) copy-start(f32[256,1,4]{0,2,1:T(4,128)} %stack.26) | copy-start | bytes 12292
  87.9 3.3 %copy-start.36 = (bf16[1,2,64,4,128]{4,3,2,1,0:T(4,128)(2,1)S(1)}, bf16[1,2,64,4,128]{4,3,2,1,0:T(4,128)(2,1)}, u32[]{:S(2)}) copy-start(bf16[1,2,64,4,128]{4,3,2,1,0:T(4,128)(2,1)} %copy-done.35) | copy-start | bytes 393220
  87.9 3.3 %copy-start.47 = (f32[2,64,4]{1,0,2:T(2,128)S(1)}, f32[2,64,4]{1,0,2:T(2,128)}, u32[]{:S(2)}) copy-start(f32[2,64,4]{1,0,2:T(2,128)} %copy.430) | copy-start | bytes 6148
  87.9 3.7 %copy-start.13 = (f32[4,128,128]{2,1,0:T(8,128)S(1)}, f32[4,128,128]{2,1,0:T(8,128)}, u32[]{:S(2)}) copy-start(f32[4,128,128]{2,1,0:T(8,128)} %copy-done.12) | copy-start | bytes 786436
  90.0 4.4 %copy-start.46 = (f32[2,64,4]{1,2,0:T(4,128)S(1)}, f32[2,64,4]{1,2,0:T(4,128)}, u32[]{:S(2)}) copy-start(f32[2,64,4]{1,2,0:T(4,128)} %slice_bitcast_fusion.7) | copy-start | bytes 6148
  90.0 20.6 %collective-permute-start.3 = (bf16[3,4,128,128]{2,3,0,1:T(8,128)(2,1)}, bf16[3,4,128,128]{2,3,0,1:T(8,128)(2,1)}, u32[]{:S(2)}, u32[]{:S(2)}) collective-permute-start(bf16[3,4,128,128]{2,3,0,1:T(8,128)(2,1)} %get-tuple-element.52), channel_id=1, source_target_pairs={{0,4},{4,0},{8,12},{12,8},{16,20},{20,16},{24,28},{28,24},{1,5},{5... | collective-permute-start | bytes 1179656 | tf_op jit(solution)/shard_map/ppermute | solution.py:17
  91.0 11.1 %copy-start.21 = (bf16[2,1,64,4,128]{4,3,2,1,0:T(4,128)(2,1)}, bf16[2,1,64,4,128]{4,3,2,1,0:T(4,128)(2,1)S(1)}, u32[]{:S(2)}) copy-start(bf16[2,1,64,4,128]{4,3,2,1,0:T(4,128)(2,1)S(1)} %slice.131) | copy-start | bytes 393220
  91.2 4.0 %copy-start.57 = (f32[256,6,4]{0,2,1:T(4,128)}, f32[256,6,4]{0,2,1:T(4,128)S(1)}, u32[]{:S(2)}) copy-start(f32[256,6,4]{0,2,1:T(4,128)S(1)} %constant_dynamic-update-slice_fusion) | copy-start | bytes 73732
  91.2 4.0 %copy-start.2 = (f32[4,4,128,128]{3,2,1,0:T(8,128)S(1)}, f32[4,4,128,128]{3,2,1,0:T(8,128)}, u32[]{:S(2)}) copy-start(f32[4,4,128,128]{3,2,1,0:T(8,128)} %copy-done.1) | copy-start | bytes 3145732
  91.8 3.7 %copy-start.30 = (bf16[4,128,128]{2,1,0:T(8,128)(2,1)S(1)}, bf16[4,128,128]{2,1,0:T(8,128)(2,1)}, u32[]{:S(2)}) copy-start(bf16[4,128,128]{2,1,0:T(8,128)(2,1)} %copy-done.29) | copy-start | bytes 393220
  93.1 4.6 %copy-start.17 = (bf16[4,128,128]{2,1,0:T(8,128)(2,1)S(1)}, bf16[4,128,128]{2,1,0:T(8,128)(2,1)}, u32[]{:S(2)}) copy-start(bf16[4,128,128]{2,1,0:T(8,128)(2,1)} %copy-done.16) | copy-start | bytes 393220
  96.6 5.2 %copy-start.4 = (bf16[4,64,4,128]{3,2,1,0:T(4,128)(2,1)S(1)}, bf16[4,64,4,128]{3,2,1,0:T(4,128)(2,1)}, u32[]{:S(2)}) copy-start(bf16[4,64,4,128]{3,2,1,0:T(4,128)(2,1)} %copy-done.3) | copy-start | bytes 786436
  96.6 5.2 %copy-start.40 = (f32[64,64]{1,0:T(8,128)S(1)}, f32[64,64]{1,0:T(8,128)}, u32[]{:S(2)}) copy-start(f32[64,64]{1,0:T(8,128)} %fusion.145) | copy-start | bytes 49156
  98.6 3.4 %copy-start.45 = (f32[2,64,4]{1,2,0:T(4,128)S(1)}, f32[2,64,4]{1,2,0:T(4,128)}, u32[]{:S(2)}) copy-start(f32[2,64,4]{1,2,0:T(4,128)} %slice_bitcast_fusion.8) | copy-start | bytes 6148
  99.7 3.4 %copy-start.6 = (bf16[4,64,4,128]{3,2,1,0:T(4,128)(2,1)S(1)}, bf16[4,64,4,128]{3,2,1,0:T(4,128)(2,1)}, u32[]{:S(2)}) copy-start(bf16[4,64,4,128]{3,2,1,0:T(4,128)(2,1)} %reshape.213) | copy-start | bytes 786436
  100.8 3.3 %copy-start.24 = (bf16[4,64,4,128]{3,2,1,0:T(4,128)(2,1)S(1)}, bf16[4,64,4,128]{3,2,1,0:T(4,128)(2,1)}, u32[]{:S(2)}) copy-start(bf16[4,64,4,128]{3,2,1,0:T(4,128)(2,1)} %copy-done.23) | copy-start | bytes 786436
  107.1 5.6 %copy-start.28 = (f32[3,4,128,128]{2,3,0,1:T(8,128)S(1)}, f32[3,4,128,128]{2,3,0,1:T(8,128)}, u32[]{:S(2)}) copy-start(f32[3,4,128,128]{2,3,0,1:T(8,128)} %get-tuple-element.53) | copy-start | bytes 2359300
  110.6 3.3 %copy-start.20 = (bf16[2,1,64,4,128]{4,3,2,1,0:T(4,128)(2,1)S(1)}, bf16[2,1,64,4,128]{4,3,2,1,0:T(4,128)(2,1)}, u32[]{:S(2)}) copy-start(bf16[2,1,64,4,128]{4,3,2,1,0:T(4,128)(2,1)} %copy-done.18) | copy-start | bytes 393220
  110.6 3.3 %copy-start.22 = (bf16[2,1,64,4,128]{4,3,2,1,0:T(4,128)(2,1)S(1)}, bf16[2,1,64,4,128]{4,3,2,1,0:T(4,128)(2,1)}, u32[]{:S(2)}) copy-start(bf16[2,1,64,4,128]{4,3,2,1,0:T(4,128)(2,1)} %copy-done.21) | copy-start | bytes 393220
  110.6 3.3 %copy-start.31 = (f32[2,4,128,128]{3,2,1,0:T(8,128)S(1)}, f32[2,4,128,128]{3,2,1,0:T(8,128)}, u32[]{:S(2)}) copy-start(f32[2,4,128,128]{3,2,1,0:T(8,128)} %fusion.83) | copy-start | bytes 1572868
  113.7 33.7 %collective-permute-start.4 = (bf16[2,4,128,128]{2,3,0,1:T(8,128)(2,1)}, bf16[2,4,128,128]{2,3,0,1:T(8,128)(2,1)}, u32[]{:S(2)}, u32[]{:S(2)}) collective-permute-start(bf16[2,4,128,128]{2,3,0,1:T(8,128)(2,1)} %get-tuple-element.30), channel_id=1, source_target_pairs={{0,8},{4,12},{8,0},{12,4},{16,24},{20,28},{24,16},{28,20},{1,9},{5... | collective-permute-start | bytes 786440 | tf_op jit(solution)/shard_map/ppermute | solution.py:17
  145.1 3.4 %copy-start.10 = (bf16[4,64,4,128]{3,2,1,0:T(4,128)(2,1)S(1)}, bf16[4,64,4,128]{3,2,1,0:T(4,128)(2,1)}, u32[]{:S(2)}) copy-start(bf16[4,64,4,128]{3,2,1,0:T(4,128)(2,1)} %reshape.212) | copy-start | bytes 786436
  148.4 8.7 %collective-permute-start.5 = (bf16[1,4,128,128]{2,3,0,1:T(8,128)(2,1)S(1)}, bf16[1,4,128,128]{2,3,0,1:T(8,128)(2,1)S(1)}, u32[]{:S(2)}, u32[]{:S(2)}) collective-permute-start(bf16[1,4,128,128]{2,3,0,1:T(8,128)(2,1)S(1)} %fusion.57), channel_id=1, source_target_pairs={{0,16},{4,20},{8,24},{12,28},{16,0},{20,4},{24,8},{28,12},{1,17},{... | collective-permute-start | bytes 393224 | tf_op jit(solution)/shard_map/ppermute | solution.py:17
  (21 other events, 45.2 us)
Sparse Core Ops, SparseCore 0:
  15.9 17.0 all-gather.1
  63.5 93.6 reduce-scatter.4
  160.3 24.6 reduce-scatter.2
where the time goes:
time: 193 us; the launch traced here: 192 us
  local copies, waits for them, and re-layouts  53.3 us (28%)
  matrix products  53.1 us (28%)
  waiting for transfers between devices  27.4 us (14%)
  blocking collectives  21.9 us (11%)
  between operations  14.5 us (8%)
  other arithmetic  12.5 us (6%)
  starting transfers between devices  8.79 us (5%)
    psum x1, blocking collectives, per_device(): table_grad = lax.psum(table_part, 'seq')  21.9 us
    reduce_scatter x1, waiting for transfers between devices, per_device(): lax.psum_scatter(partial_value.astype(jnp.bfloat16), 'head', scatter_dime...  15.6 us
    unnamed x16, matrix products  14.5 us
    ppermute x6, waiting for transfers between devices, partner_2(): return lax.ppermute(value, axis, pairs)  11.8 us
    dot_general x6, matrix products, split_einsum(): jnp.einsum(form, rest, right, preferred_element_type=jnp.float32)  9.52 us
    ppermute x6, starting transfers between devices, partner_2(): return lax.ppermute(value, axis, pairs)  8.49 us
    another operation x7, local copies, waits for them, and re-layouts, per_device(): jnp.stack([jnp.sum(g_half * level_reads[level_index], axis=3) for level_i...  8.22 us
    unnamed x131, local copies, waits for them, and re-layouts  7.97 us
  transfers between devices with their start and end apart: 9, of which 4 were waited for; matrix products, arithmetic and copies ran while one was open for 53% of the time, Pallas kernels for 0%

commit v1 on v0

v1 whole, which is shorter than its diff:
```python
import functools
import math

import jax
import jax.numpy as jnp
from jax import lax
from jax.experimental import pallas as pl
from jax.experimental.pallas import tpu as pltpu
from jax.sharding import PartitionSpec as P

SPAN = 64
F32 = jnp.float32
BF16 = jnp.bfloat16
VMEM_LIMIT = 24 * 1024 * 1024

VMEM_SPEC = pl.BlockSpec(memory_space=pltpu.VMEM)
SMEM_SPEC = pl.BlockSpec(memory_space=pltpu.SMEM)


def nn(left, right):
    return lax.dot_general(left, right, (((1,), (0,)), ((), ())), preferred_element_type=F32)


def nt(left, right):
    return lax.dot_general(left, right, (((1,), (1,)), ((), ())), preferred_element_type=F32)


def tn(left, right):
    return lax.dot_general(left, right, (((0,), (0,)), ((), ())), preferred_element_type=F32)


def local_call(body, outs, ins, scalars=0, flops=0, scratch=(), name=None):
    moved = sum(math.prod(o.shape) * o.dtype.itemsize for o in outs)
    moved += sum(math.prod(a.shape) * a.dtype.itemsize for a in ins)
    return pl.pallas_call(
        body,
        out_shape=tuple(outs),
        in_specs=[SMEM_SPEC] * scalars + [VMEM_SPEC] * (len(ins) - scalars),
        out_specs=tuple(VMEM_SPEC for _ in outs),
        scratch_shapes=scratch,
        compiler_params=pltpu.CompilerParams(vmem_limit_bytes=VMEM_LIMIT),
        cost_estimate=pl.CostEstimate(flops=flops, bytes_accessed=moved, transcendentals=0),
        name=name,
    )(*ins)


def shaped(shape, dtype):
    return jax.ShapeDtypeStruct(shape, dtype)


def state_body(heads, k_ref, v_ref, d_ref):
    size = k_ref.shape[1] // heads
    for h in range(heads):
        cols = slice(h * size, (h + 1) * size)
        d_ref[h * size : (h + 1) * size, :] = tn(k_ref[:, cols], v_ref[:, cols]).astype(BF16)


def coef_body(levels, scales, code_ref, table_ref, coef_ref, hot_ref):
    heads, codes = table_ref.shape
    table = table_ref[...]
    high = table.astype(BF16)
    low = (table - high.astype(F32)).astype(BF16)
    tokens = code_ref.shape[1]
    row = lax.broadcasted_iota(jnp.int32, (codes, tokens), 0)
    for l in range(levels):
        hot = jnp.where(row == code_ref[l : l + 1, :], 1.0, 0.0).astype(BF16)
        hot_ref[l * codes : (l + 1) * codes, :] = hot
        lam = lax.dot_general(hot, high, (((0,), (1,)), ((), ())), preferred_element_type=F32)
        lam = lam + lax.dot_general(hot, low, (((0,), (1,)), ((), ())), preferred_element_type=F32)
        coef_ref[:, l * heads : (l + 1) * heads] = lam * scales[l]


def grad_body(heads, local_levels, levels, count, *refs):
    head_ref = refs[0]
    blocks = refs[1 : 1 + count]
    w_ref, q_ref, coef_ref, g_ref, full_ref, t_ref = refs[1 + count :]
    me = head_ref[0]
    width = blocks[0].shape[1]
    size = q_ref.shape[1] // heads
    total = None
    for m in range(count):
        start = pl.multiple_of((me ^ m) * width, width)
        block = blocks[m][...]
        full_ref[:, pl.ds(start, width)] = block
        part = nt(block, w_ref[:, pl.ds(start, width)])
        total = part if total is None else total + part
    g = total.astype(BF16)
    g_ref[...] = g
    for l in range(local_levels, levels):
        for h in range(heads):
            cols = slice(h * size, (h + 1) * size)
            scaled = (g[:, cols].astype(F32) * coef_ref[:, l * heads + h : l * heads + h + 1]).astype(BF16)
            t_ref[l - local_levels, h * size : (h + 1) * size, :] = tn(q_ref[:, cols], scaled).astype(BF16)


def level_masks(tokens, local_levels):
    row = lax.broadcasted_iota(jnp.int32, (tokens, tokens), 0)
    col = lax.broadcasted_iota(jnp.int32, (tokens, tokens), 1)
    apart = (row // SPAN) ^ (col // SPAN)
    causal = col <= row
    masks = [causal & (apart == 0)]
    for l in range(1, local_levels):
        masks.append(causal & ((apart >> (l - 1)) == 1))
    return masks


def inner_body(heads, local_levels, scales, q_ref, k_ref, v_ref, g_ref, coef_ref,
               attn_ref, dq_ref, dk_ref, dv_ref, lev_ref):
    tokens = q_ref.shape[0]
    size = q_ref.shape[1] // heads
    masks = level_masks(tokens, local_levels)
    lane = lax.broadcasted_iota(jnp.int32, lev_ref.shape, 1)
    lev = jnp.zeros(lev_ref.shape, F32)
    for h in range(heads):
        cols = slice(h * size, (h + 1) * size)
        q, k, v, g = q_ref[:, cols], k_ref[:, cols], v_ref[:, cols], g_ref[:, cols]
        weight = jnp.zeros((tokens, tokens), F32)
        for l in range(local_levels):
            weight = jnp.where(masks[l], coef_ref[:, l * heads + h : l * heads + h + 1], weight)
        scores = nt(q, k)
        grads = nt(g, v)
        both = scores * grads
        for l in range(local_levels):
            part = jnp.sum(jnp.where(masks[l], both, 0.0), axis=1, keepdims=True) * scales[l]
            lev = jnp.where(lane == l * heads + h, part, lev)
        scores = (scores * weight).astype(BF16)
        grads = (grads * weight).astype(BF16)
        attn_ref[:, cols] = nn(scores, v)
        dq_ref[:, cols] = nn(grads, k)
        dk_ref[:, cols] = tn(grads, q)
        dv_ref[:, cols] = tn(scores, g)
    lev_ref[...] = lev


def outer_body(heads, local_levels, levels, scales, norm, seq_ref, q_ref, g_ref, coef_ref, hot_ref,
               attn_in, dq_in, lev_ref, *rest):
    states = rest[: levels - local_levels]
    attn_ref, dq_ref, table_ref = rest[levels - local_levels :]
    me = seq_ref[0]
    size = q_ref.shape[1] // heads
    codes = table_ref.shape[0]
    lane = lax.broadcasted_iota(jnp.int32, lev_ref.shape, 1)
    lev = lev_ref[...]
    for h in range(heads):
        cols = slice(h * size, (h + 1) * size)
        q, g = q_ref[:, cols], g_ref[:, cols]
        qf = q.astype(F32)
        attn = attn_in[:, cols]
        dq = dq_in[:, cols]
        for l in range(local_levels, levels):
            b = l - local_levels
            owned = ((me >> b) & 1).astype(F32)
            state = states[b][h * size : (h + 1) * size, :]
            coef = coef_ref[:, l * heads + h : l * heads + h + 1] * owned
            attn = attn + coef * nn(q, state)
            back = nt(g, state)
            dq = dq + coef * back
            part = jnp.sum(qf * back, axis=1, keepdims=True) * (owned * scales[l])
            lev = jnp.where(lane == l * heads + h, part, lev)
        attn_ref[:, cols] = attn.astype(BF16)
        dq_ref[:, cols] = dq.astype(BF16)
    high = lev.astype(BF16)
    low = (lev - high.astype(F32)).astype(BF16)
    total = jnp.zeros((codes, heads), F32)
    for l in range(levels):
        hot = hot_ref[l * codes : (l + 1) * codes, :]
        pick = slice(l * heads, (l + 1) * heads)
        total = total + nn(hot, high[:, pick]) + nn(hot, low[:, pick])
    table_ref[...] = total * norm


def weight_body(masks_a, masks_b, scale, seq_ref, full_ref, attn_ref, a_ref, b_ref, *scratch):
    me = seq_ref[0]
    rows, half = a_ref.shape[1:]
    for masks, out_ref, cols in ((masks_a, a_ref, slice(0, half)), (masks_b, b_ref, slice(half, 2 * half))):
        if scratch:
            scratch[0][...] = tn(full_ref[...], attn_ref[:, cols]) * scale
        for n, m in enumerate(masks):
            start = pl.multiple_of((me ^ m) * rows, rows)
            if scratch:
                out_ref[n] = scratch[0][pl.ds(start, rows), :].astype(out_ref.dtype)
            else:
                part = tn(full_ref[:, pl.ds(start, rows)], attn_ref[:, cols])
                out_ref[n] = (part * scale).astype(out_ref.dtype)


def mixed_body(masks, head_ref, attn_ref, w_ref, o_ref):
    me = head_ref[0]
    width = o_ref.shape[2]
    for n, m in enumerate(masks):
        start = pl.multiple_of((me ^ m) * width, width)
        o_ref[n] = nn(attn_ref[...], w_ref[:, pl.ds(start, width)]).astype(BF16)


def final_body(heads, k_ref, v_ref, u_ref, dk_in, dv_in, dk_ref, dv_ref):
    size = k_ref.shape[1] // heads
    for h in range(heads):
        cols = slice(h * size, (h + 1) * size)
        u = u_ref[h * size : (h + 1) * size, :]
        dk_ref[:, cols] = (dk_in[:, cols] + nt(v_ref[:, cols], u)).astype(BF16)
        dv_ref[:, cols] = (dv_in[:, cols] + nn(k_ref[:, cols], u)).astype(BF16)


def swap(value, axis, bit):
    pairs = [(i, i ^ (1 << bit)) for i in range(lax.axis_size(axis))]
    return lax.ppermute(value, axis, pairs)


def one_way(value, axis, bit, up):
    n = lax.axis_size(axis)
    pairs = [(i, i ^ (1 << bit)) for i in range(n) if ((i >> bit) & 1) == (0 if up else 1)]
    return lax.ppermute(value, axis, pairs)


def bit_order(bits, order):
    masks = [0]
    for bit in order:
        masks = [m for m in masks] + [m | (1 << bit) for m in masks]
    return masks


def reduce_blocks(order, send, keep):
    for n, bit in enumerate(order):
        got = swap(send, "seq", bit).astype(F32)
        total = keep.astype(F32) + got
        if n + 1 == len(order):
            return total[0]
        half = total.shape[0] // 2
        keep = total[:half]
        send = total[half:].astype(BF16)


def per_device(queries, keys, values, level_table, level_code, out_weight, cotangent):
    tokens, cols = queries.shape
    heads = level_table.shape[1]
    codes = level_table.shape[0]
    size = cols // heads
    width = out_weight.shape[1]
    spans = tokens // SPAN
    local_bits = spans.bit_length() - 1
    seq_count = lax.axis_size("seq")
    seq_bits = seq_count.bit_length() - 1
    head_count = lax.axis_size("head")
    head_bits = head_count.bit_length() - 1
    local_levels = 1 + local_bits
    levels = local_levels + seq_bits
    scales = [1.0 / math.sqrt(SPAN * 2 ** max(l - 1, 0)) for l in range(levels)]
    seq_me = lax.axis_index("seq").astype(jnp.int32)
    head_me = lax.axis_index("head").astype(jnp.int32)
    seq_one = seq_me.reshape(1)
    head_one = head_me.reshape(1)

    blocks = {0: cotangent}
    for bit in reversed(range(head_bits)):
        for m in list(blocks):
            blocks[m | (1 << bit)] = swap(blocks[m], "head", bit)

    (state,) = local_call(
        functools.partial(state_body, heads),
        [shaped((cols, size), BF16)],
        [keys, values],
        flops=2 * tokens * cols * size,
        name="state",
    )
    coef, hot = local_call(
        functools.partial(coef_body, levels, scales),
        [shaped((tokens, levels * heads), F32), shaped((levels * codes, tokens), BF16)],
        [level_code.T, level_table.T],
        flops=4 * tokens * levels * codes * heads,
        name="coef",
    )
    found = []
    block_state = state
    for bit in range(seq_bits):
        if bit == seq_bits - 1:
            found.append(one_way(block_state, "seq", bit, True))
        else:
            got = swap(block_state, "seq", bit)
            found.append(got)
            block_state = (block_state.astype(F32) + got.astype(F32)).astype(BF16)

    g, full, terms = local_call(
        functools.partial(grad_body, heads, local_levels, levels, head_count),
        [
            shaped((tokens, cols), BF16),
            shaped((tokens, width), BF16),
            shaped((seq_bits, cols, size), BF16),
        ],
        [head_one] + [blocks[m] for m in range(head_count)] + [out_weight, queries, coef],
        scalars=1,
        flops=2 * tokens * cols * width,
        name="grad",
    )
    gathered = None
    for bit in range(seq_bits):
        if bit == seq_bits - 1:
            got = one_way(terms, "seq", bit, False)
            first = got[0].astype(F32)
        else:
            got = swap(terms, "seq", bit)
            first = got[0].astype(F32) * (1 - ((seq_me >> bit) & 1)).astype(F32)
            terms = (terms[1:].astype(F32) + got[1:].astype(F32)).astype(BF16)
        gathered = first if gathered is None else gathered + first
    gathered = gathered.astype(BF16)

    attn_in, dq_in, dk_in, dv_in, lev = local_call(
        functools.partial(inner_body, heads, local_levels, scales),
        [shaped((tokens, cols), F32)] * 4 + [shaped((tokens, 128 * pl.cdiv(levels * heads, 128)), F32)],
        [queries, keys, values, g, coef],
        flops=12 * tokens * tokens * cols,
        name="inner",
    )
    table_norm = 1.0 / math.sqrt(tokens * seq_count * levels)
    attn, query_grad, table_part = local_call(
        functools.partial(outer_body, heads, local_levels, levels, scales, table_norm),
        [shaped((tokens, cols), BF16), shaped((tokens, cols), BF16), shaped((codes, heads), F32)],
        [seq_one, queries, g, coef, hot, attn_in, dq_in, lev] + found,
        scalars=1,
        flops=4 * tokens * cols * size * seq_bits,
        name="outer",
    )

    weight_norm = 1.0 / math.sqrt(tokens * seq_count)
    order_a = list(range(seq_bits))
    order_b = order_a[1:] + order_a[:1]
    masks_a = bit_order(seq_bits, reversed(order_a))
    masks_b = bit_order(seq_bits, reversed(order_b))
    half = seq_count // 2
    rows = width // seq_count

    def weight_part(low, high, dtype, name):
        return local_call(
            functools.partial(weight_body, masks_a[low:high], masks_b[low:high], weight_norm),
            [shaped((high - low, rows, cols // 2), dtype)] * 2,
            [seq_one, full, attn],
            scalars=1,
            flops=tokens * cols * width,
            scratch=[pltpu.VMEM((width, cols // 2), F32)] if rows % 128 else [],
            name=name,
        )

    a_send, b_send = weight_part(half, seq_count, BF16, "weight_send")
    a_keep, b_keep = weight_part(0, half, BF16, "weight_keep")
    weight_a = reduce_blocks(order_a, a_send, a_keep)
    weight_b = reduce_blocks(order_b, b_send, b_keep)
    out_weight_grad = jnp.concatenate([weight_a, weight_b], axis=1)

    masks_m = bit_order(head_bits, reversed(range(head_bits)))
    (partial_value,) = local_call(
        functools.partial(mixed_body, masks_m),
        [shaped((head_count, tokens, width // head_count), BF16)],
        [head_one, attn, out_weight],
        scalars=1,
        flops=2 * tokens * cols * width,
        name="mixed",
    )
    keep, send = partial_value[: head_count // 2], partial_value[head_count // 2 :]
    for bit in range(head_bits):
        total = keep.astype(F32) + swap(send, "head", bit).astype(F32)
        if bit + 1 < head_bits:
            part = total.shape[0] // 2
            keep, send = total[:part], total[part:].astype(BF16)
    mixed = total[0].astype(BF16)

    table_grad = table_part
    for bit in range(seq_bits):
        table_grad = table_grad + swap(table_grad, "seq", bit)

    key_grad, value_grad = local_call(
        functools.partial(final_body, heads),
        [shaped((tokens, cols), BF16)] * 2,
        [keys, values, gathered, dk_in, dv_in],
        flops=4 * tokens * cols * size,
        name="final",
    )
    return mixed, out_weight_grad, query_grad, key_grad, value_grad, table_grad


def solution(mesh):
    placed = (
        P("seq", "head"),
        P("seq", "head"),
        P("seq", "head"),
        P(None, "head"),
        P("seq", None),
        P("head", None),
        P("seq", "head"),
    )
    return jax.shard_map(
        per_device,
        mesh=mesh,
        in_specs=placed,
        out_specs=(
            P("seq", "head"),
            P("seq", "head"),
            P("seq", "head"),
            P("seq", "head"),
            P("seq", "head"),
            P(None, "head"),
        ),
        check_vma=False,
    )
```

time: 193 us -> 101 us (0.52)
  matrix products: 53.1 us -> 0 us
  local copies, waits for them, and re-layouts: 53.3 us -> 21 us
  starting transfers between devices: 8.79 us -> 35.7 us
  blocking collectives: 21.9 us -> 0 us
  between operations: 14.5 us -> 0.93 us
  Pallas kernels: 0 us -> 11.6 us
  other arithmetic: 12.5 us -> 7.09 us
  waiting for transfers between devices: 27.4 us -> 24.3 us
    dot_general x30 -> x0, matrix products: 38.6 us -> none  [the longest x6 9.52 us: split_einsum(): jnp.einsum(form, rest, right, preferred_element_type=jnp.float32)]
    ppermute x6 -> x20, starting transfers between devices: 8.49 us -> 35.7 us  [the longest x18 29.1 us: swap(): return lax.ppermute(value, axis, pairs)]
    psum x1 -> x0, blocking collectives: 21.9 us -> none  [per_device(): table_grad = lax.psum(table_part, 'seq')]
    reduce_scatter x2 -> x0, waiting for transfers between devices: 15.6 us -> none  [the longest x1 15.6 us: per_device(): lax.psum_scatter(partial_value.astype(jnp.bfloat16), 'head', scatter_dime...]
    unnamed x16 -> x0, matrix products: 14.5 us -> none
    another operation x11 -> x0, local copies, waits for them, and re-layouts: 13.2 us -> none  [the longest x7 8.22 us: per_device(): jnp.stack([jnp.sum(g_half * level_reads[level_index], axis=3) for level_i...]
    ppermute x6 -> x20, waiting for transfers between devices: 11.8 us -> 24.3 us  [the longest x18 23.4 us: swap(): return lax.ppermute(value, axis, pairs)]
    unnamed x131 -> x59, local copies, waits for them, and re-layouts: 7.97 us -> 20 us
  transfers between devices with their start and end apart: 9 -> 20, of which waited for: 4 -> 11; matrix products, arithmetic and copies ran while one was open for 53% -> 8% of each run, Pallas kernels for 0% -> 11%
where the time goes in v1:
time: 101 us
  starting transfers between devices  35.7 us (35%)
  waiting for transfers between devices  24.3 us (24%)
  local copies, waits for them, and re-layouts  21 us (21%)
  Pallas kernels  11.6 us (11%)
  other arithmetic  7.09 us (7%)
    ppermute x18, starting transfers between devices, swap(): return lax.ppermute(value, axis, pairs)  29.1 us
    ppermute x18, waiting for transfers between devices, swap(): return lax.ppermute(value, axis, pairs)  23.4 us
    unnamed x59, local copies, waits for them, and re-layouts  20 us
    pallas_call x9, Pallas kernels, local_call(): pl.pallas_call(body, out_shape=tuple(outs), in_specs=[SMEM_SPEC] * scalar...  11.6 us
    ppermute x2, starting transfers between devices, one_way(): return lax.ppermute(value, axis, pairs)  6.69 us
  transfers between devices with their start and end apart: 20, of which 11 were waited for; matrix products, arithmetic and copies ran while one was open for 8% of the time, Pallas kernels for 11%

profile of v1, /device:TPU:0, one launch (start us, length us, event | category | flops | bytes accessed | tf_op | source)
XLA Modules:
  0.0 100.7 jit_solution(17579150555399313913)
XLA Ops:
  0.6 0.9 copy-done.4
  1.6 0.9 copy-done.7
  2.8 3.0 %collective-permute-start.3 = (bf16[512,128]{1,0:T(8,128)(2,1)S(1)}, bf16[512,128]{1,0:T(8,128)(2,1)S(1)}, u32[]{:S(2)}, u32[]{:S(2)}) collective-permute-start(bf16[512,128]{1,0:T(8,128)(2,1)S(1)} %state.1), channel_id=1, source_target_pairs={{0,4},{4,0},{8,12},{12,8},{16,20},{20,16},{24,28},{28,24},{1,5},{5... | collective-permute-start | bytes 393224 | tf_op jit(solution)/shard_map/ppermute | solution.py:206
  5.9 1.5 %collective-permute-start.1 = (bf16[256,512]{1,0:T(8,128)(2,1)}, bf16[256,512]{1,0:T(8,128)(2,1)S(1)}, u32[]{:S(2)}, u32[]{:S(2)}) collective-permute-start(bf16[256,512]{1,0:T(8,128)(2,1)} %refs_1_.1), channel_id=1, source_target_pairs={{0,2},{1,3},{2,0},{3,1},{4,6},{5,7},{6,4},{7,5},{8,10},{9,11},{10,... | collective-permute-start | bytes 786440 | tf_op jit(solution)/shard_map/ppermute | solution.py:206
  7.4 2.0 %collective-permute-done.3.rest_0_ = bf16[512,128]{1,0:T(8,128)(2,1)S(1)} collective-permute-done((bf16[512,128]{1,0:T(8,128)(2,1)S(1)}, bf16[512,128]{1,0:T(8,128)(2,1)S(1)}, u32[]{:S(2)}, u32[]{:S(2)}) %collective-permute-start.3) | collective-permute-done | bytes 131104 | tf_op jit(solution)/shard_map/ppermute | solution.py:206
  9.4 1.9 %collective-permute-start.4 = (bf16[512,128]{1,0:T(8,128)(2,1)S(1)}, bf16[512,128]{1,0:T(8,128)(2,1)S(1)}, u32[]{:S(2)}, u32[]{:S(2)}) collective-permute-start(bf16[512,128]{1,0:T(8,128)(2,1)S(1)} %add_convert_fusion.4), channel_id=1, source_target_pairs={{0,8},{4,12},{8,0},{12,4},{16,24},{20,28},{24,16},{28,20},{1,9},{5... | collective-permute-start | bytes 393224 | tf_op jit(solution)/shard_map/ppermute | solution.py:206
  11.3 2.5 %collective-permute-done.1.refs_3_ = bf16[256,512]{1,0:T(8,128)(2,1)S(1)} collective-permute-done((bf16[256,512]{1,0:T(8,128)(2,1)}, bf16[256,512]{1,0:T(8,128)(2,1)S(1)}, u32[]{:S(2)}, u32[]{:S(2)}) %collective-permute-start.1) | collective-permute-done | bytes 262176 | tf_op jit(solution)/shard_map/ppermute | solution.py:206
  15.8 5.4 %collective-permute-start.5 = (bf16[512,128]{1,0:T(8,128)(2,1)}, bf16[512,128]{1,0:T(8,128)(2,1)}, u32[]{:S(2)}, u32[]{:S(2)}) collective-permute-start(bf16[512,128]{1,0:T(8,128)(2,1)} %add_convert_fusion.3), channel_id=1, source_target_pairs={{0,16},{4,20},{8,24},{12,28},{1,17},{5,21},{9,25},{13,29},{2,18},{... | collective-permute-start | bytes 393224 | tf_op jit(solution)/shard_map/ppermute | solution.py:212
  23.7 1.6 %copy-done = bf16[512,2048]{1,0:T(8,128)(2,1)S(1)} copy-done((bf16[512,2048]{1,0:T(8,128)(2,1)S(1)}, bf16[512,2048]{1,0:T(8,128)(2,1)}, u32[]{:S(2)}) %copy-start) | copy-done | bytes 2097176
  25.3 0.9 copy-done.10
  26.2 0.9 copy-done.24
  27.2 2.0 %grad.1 = (bf16[256,512]{1,0:T(8,128)(2,1)S(1)}, bf16[256,2048]{1,0:T(8,128)(2,1)S(1)}, bf16[3,512,128]{2,1,0:T(8,128)(2,1)}) custom-call(s32[1]{0:T(128)} %bitcast.refs_0_.head_ref, bf16[256,512]{1,0:T(8,128)(2,1)S(1)} %copy-done.24, bf16[256,512]{1,0:T(8,128)(2,1)S(1)} %collective-permute-done.refs_2_, ...), custom_call_target="tpu_custom_call" | custom-call | flops 536870912 | bytes 5136388 | tf_op jit(solution)/shard_map/grad/pallas_call | solution.py:35
  30.5 1.5 %collective-permute-start.14 = (bf16[3,512,128]{2,1,0:T(8,128)(2,1)}, bf16[3,512,128]{2,1,0:T(8,128)(2,1)}, u32[]{:S(2)}, u32[]{:S(2)}) collective-permute-start(bf16[3,512,128]{2,1,0:T(8,128)(2,1)} %get-tuple-element.38), channel_id=1, source_target_pairs={{0,4},{4,0},{8,12},{12,8},{16,20},{20,16},{24,28},{28,24},{1,5},{5... | collective-permute-start | bytes 1179656 | tf_op jit(solution)/shard_map/ppermute | solution.py:206
  32.0 0.9 copy-done.8
  33.0 0.9 copy-done.11
  33.9 0.9 copy-done.20
  34.8 0.9 copy-done.22
  35.8 2.0 %inner.1 = (f32[256,512]{1,0:T(8,128)S(1)}, f32[256,512]{1,0:T(8,128)S(1)}, f32[256,512]{1,0:T(8,128)S(1)}, f32[256,512]{1,0:T(8,128)S(1)}, f32[256,128]{1,0:T(8,128)S(1)}) custom-call(bf16[256,512]{1,0:T(8,128)(2,1)S(1)} %copy-done.11, bf16[256,512]{1,0:T(8,128)(2,1)S(1)} %copy-done.5, bf16[256,512]{1,0:T(8,128)(2,1)S(1)} %copy-done.8, ...), custom_call_target="tpu_custom_call" | custom-call | flops 402653184 | bytes 3301376 | tf_op jit(solution)/shard_map/inner/pallas_call | solution.py:35
  37.8 0.8 copy-done.15
  39.4 0.9 copy-done.12
  40.4 0.9 copy-done.14
  41.3 0.9 copy-done.23
  42.2 0.8 copy-done.26
  43.0 3.2 %outer.1 = (bf16[256,512]{1,0:T(8,128)(2,1)S(1)}, bf16[256,512]{1,0:T(8,128)(2,1)}, f32[16,4]{1,0:T(8,128)S(1)}) custom-call(s32[1]{0:T(128)} %bitcast.1.seq_ref, bf16[256,512]{1,0:T(8,128)(2,1)S(1)} %copy-done.12, bf16[256,512]{1,0:T(8,128)(2,1)S(1)} %copy-done.23, f32[256,24]{1,0:T(8,128)S(1)} %copy-done.20, bf16[96,256]{1,0:T(8,128)(2,1)S(1)} %copy-done.26, ...), custom_call_target="tpu_custom_call" | custom-call | flops 201326592 | bytes 2695428 | tf_op jit(solution)/shard_map/outer/pallas_call | solution.py:35
  47.0 1.0 copy-done.2
  48.0 0.8 slice.78
  49.4 3.0 %collective-permute-done.17 = f32[16,4]{1,0:T(8,128)S(1)} collective-permute-done((f32[16,4]{1,0:T(8,128)S(1)}, f32[16,4]{1,0:T(8,128)S(1)}, u32[]{:S(2)}, u32[]{:S(2)}) %collective-permute-start.17) | collective-permute-done | bytes 288 | tf_op jit(solution)/shard_map/ppermute | solution.py:206
  52.4 1.6 %collective-permute-start.18 = (f32[16,4]{1,0:T(8,128)S(1)}, f32[16,4]{1,0:T(8,128)S(1)}, u32[]{:S(2)}, u32[]{:S(2)}) collective-permute-start(f32[16,4]{1,0:T(8,128)S(1)} %add.70), channel_id=1, source_target_pairs={{0,8},{4,12},{8,0},{12,4},{16,24},{20,28},{24,16},{28,20},{1,9},{5... | collective-permute-start | bytes 776 | tf_op jit(solution)/shard_map/ppermute | solution.py:206
  54.0 1.4 %weight_send.1 = (bf16[4,256,256]{2,1,0:T(8,128)(2,1)}, bf16[4,256,256]{2,1,0:T(8,128)(2,1)}) custom-call(s32[1]{0:T(128)} %bitcast.1.seq_ref, bf16[256,2048]{1,0:T(8,128)(2,1)S(1)} %get-tuple-element.32.full_ref, bf16[256,512]{1,0:T(8,128)(2,1)S(1)} %get-tuple-element.31.attn_ref), custom_call_target="tpu_custom_call" | custom-call | flops 268435456 | bytes 2359300 | tf_op jit(solution)/shard_map/weight_send/pallas_call | solution.py:35
  56.6 1.7 %collective-permute-start.11 = (bf16[4,256,256]{2,1,0:T(8,128)(2,1)}, bf16[4,256,256]{2,1,0:T(8,128)(2,1)S(1)}, u32[]{:S(2)}, u32[]{:S(2)}) collective-permute-start(bf16[4,256,256]{2,1,0:T(8,128)(2,1)} %get-tuple-element.36), channel_id=1, source_target_pairs={{0,8},{4,12},{8,0},{12,4},{16,24},{20,28},{24,16},{28,20},{1,9},{5... | collective-permute-start | bytes 1572872 | tf_op jit(solution)/shard_map/ppermute | solution.py:206
  58.3 2.5 %collective-permute-done.19 = f32[16,4]{1,0:T(8,128)S(1)} collective-permute-done((f32[16,4]{1,0:T(8,128)S(1)}, f32[16,4]{1,0:T(8,128)S(1)}, u32[]{:S(2)}, u32[]{:S(2)}) %collective-permute-start.19) | collective-permute-done | bytes 288 | tf_op jit(solution)/shard_map/ppermute | solution.py:206
  61.4 1.1 %add_convert_fusion = bf16[2,512,128]{2,1,0:T(8,128)(2,1)S(1)} fusion(bf16[3,512,128]{2,1,0:T(8,128)(2,1)} %collective-permute-done.14, bf16[3,512,128]{2,1,0:T(8,128)(2,1)} %get-tuple-element.38), kind=kLoop, calls=%fused_computation.11 | loop fusion | flops 524288 | bytes 786432 | tf_op jit(solution)/shard_map/convert_element_type | solution.py:302
  62.5 1.6 %collective-permute-start.15 = (bf16[2,512,128]{2,1,0:T(8,128)(2,1)S(1)}, bf16[2,512,128]{2,1,0:T(8,128)(2,1)S(1)}, u32[]{:S(2)}, u32[]{:S(2)}) collective-permute-start(bf16[2,512,128]{2,1,0:T(8,128)(2,1)S(1)} %add_convert_fusion), channel_id=1, source_target_pairs={{0,8},{4,12},{8,0},{12,4},{16,24},{20,28},{24,16},{28,20},{1,9},{5... | collective-permute-start | bytes 786440 | tf_op jit(solution)/shard_map/ppermute | solution.py:206
  64.2 1.2 %convert_add_fusion.2 = f32[2,256,512]{2,1,0:T(8,128)S(1)} fusion(bf16[2,256,512]{2,1,0:T(8,128)(2,1)} %collective-permute-done.6, bf16[4,256,512]{2,1,0:T(8,128)(2,1)S(1)} %copy-done.3), kind=kLoop, calls=%fused_computation.2 | loop fusion | flops 786432 | bytes 2097152 | tf_op jit(solution)/shard_map/add | solution.py:359
  65.4 1.6 %collective-permute-start.7 = (bf16[1,256,512]{2,1,0:T(8,128)(2,1)S(1)}, bf16[1,256,512]{2,1,0:T(8,128)(2,1)S(1)}, u32[]{:S(2)}, u32[]{:S(2)}) collective-permute-start(bf16[1,256,512]{2,1,0:T(8,128)(2,1)S(1)} %slice.121), channel_id=1, source_target_pairs={{0,2},{1,3},{2,0},{3,1},{4,6},{5,7},{6,4},{7,5},{8,10},{9,11},{10,... | collective-permute-start | bytes 786440 | tf_op jit(solution)/shard_map/ppermute | solution.py:206
  67.0 1.6 %collective-permute-done.8 = bf16[4,256,256]{2,1,0:T(8,128)(2,1)} collective-permute-done((bf16[4,256,256]{2,1,0:T(8,128)(2,1)}, bf16[4,256,256]{2,1,0:T(8,128)(2,1)}, u32[]{:S(2)}, u32[]{:S(2)}) %collective-permute-start.8) | collective-permute-done | bytes 524320 | tf_op jit(solution)/shard_map/ppermute | solution.py:206
  68.6 1.1 %convert_add_fusion.1 = f32[4,256,256]{2,1,0:T(8,128)S(1)} fusion(bf16[4,256,256]{2,1,0:T(8,128)(2,1)} %collective-permute-done.8, bf16[4,256,256]{2,1,0:T(8,128)(2,1)S(1)} %get-tuple-element.33), kind=kLoop, calls=%fused_computation.1 | loop fusion | flops 786432 | bytes 2097152 | tf_op jit(solution)/shard_map/add | solution.py:225
  70.3 1.5 %collective-permute-done.11 = bf16[4,256,256]{2,1,0:T(8,128)(2,1)S(1)} collective-permute-done((bf16[4,256,256]{2,1,0:T(8,128)(2,1)}, bf16[4,256,256]{2,1,0:T(8,128)(2,1)S(1)}, u32[]{:S(2)}, u32[]{:S(2)}) %collective-permute-start.11) | collective-permute-done | bytes 524320 | tf_op jit(solution)/shard_map/ppermute | solution.py:206
  72.0 4.9 %collective-permute-start.12 = (bf16[2,256,256]{2,1,0:T(8,128)(2,1)S(1)}, bf16[2,256,256]{2,1,0:T(8,128)(2,1)S(1)}, u32[]{:S(2)}, u32[]{:S(2)}) collective-permute-start(bf16[2,256,256]{2,1,0:T(8,128)(2,1)S(1)} %slice.119), channel_id=1, source_target_pairs={{0,16},{4,20},{8,24},{12,28},{16,0},{20,4},{24,8},{28,12},{1,17},{... | collective-permute-start | bytes 786440 | tf_op jit(solution)/shard_map/ppermute | solution.py:206
  76.9 6.9 %collective-permute-done.15 = bf16[2,512,128]{2,1,0:T(8,128)(2,1)S(1)} collective-permute-done((bf16[2,512,128]{2,1,0:T(8,128)(2,1)S(1)}, bf16[2,512,128]{2,1,0:T(8,128)(2,1)S(1)}, u32[]{:S(2)}, u32[]{:S(2)}) %collective-permute-start.15) | collective-permute-done | bytes 262176 | tf_op jit(solution)/shard_map/ppermute | solution.py:206
  83.9 1.3 %collective-permute-start.16 = (bf16[1,512,128]{2,1,0:T(8,128)(2,1)S(1)}, bf16[1,512,128]{2,1,0:T(8,128)(2,1)S(1)}, u32[]{:S(2)}, u32[]{:S(2)}) collective-permute-start(bf16[1,512,128]{2,1,0:T(8,128)(2,1)S(1)} %add_convert_fusion.2), channel_id=1, source_target_pairs={{16,0},{20,4},{24,8},{28,12},{17,1},{21,5},{25,9},{29,13},{18,2},{... | collective-permute-start | bytes 393224 | tf_op jit(solution)/shard_map/ppermute | solution.py:212
  85.2 2.7 %collective-permute-done.9 = bf16[2,256,256]{2,1,0:T(8,128)(2,1)S(1)} collective-permute-done((bf16[2,256,256]{2,1,0:T(8,128)(2,1)S(1)}, bf16[2,256,256]{2,1,0:T(8,128)(2,1)S(1)}, u32[]{:S(2)}, u32[]{:S(2)}) %collective-permute-start.9) | collective-permute-done | bytes 262176 | tf_op jit(solution)/shard_map/ppermute | solution.py:206
  88.0 0.9 collective-permute-start.10
  89.0 7.1 %collective-permute-start.13 = (bf16[1,256,256]{2,1,0:T(8,128)(2,1)S(1)}, bf16[1,256,256]{2,1,0:T(8,128)(2,1)S(1)}, u32[]{:S(2)}, u32[]{:S(2)}) collective-permute-start(bf16[1,256,256]{2,1,0:T(8,128)(2,1)S(1)} %slice.122), channel_id=1, source_target_pairs={{0,4},{4,0},{8,12},{12,8},{16,20},{20,16},{24,28},{28,24},{1,5},{5... | collective-permute-start | bytes 393224 | tf_op jit(solution)/shard_map/ppermute | solution.py:206
  96.0 0.9 collective-permute-done.16
  96.9 1.0 fusion.4.u_ref
  97.9 1.1 %final.1 = (bf16[256,512]{1,0:T(8,128)(2,1)}, bf16[256,512]{1,0:T(8,128)(2,1)}) custom-call(bf16[256,512]{1,0:T(8,128)(2,1)S(1)} %copy-done.6, bf16[256,512]{1,0:T(8,128)(2,1)S(1)} %copy-done.9, bf16[512,128]{1,0:T(8,128)(2,1)S(1)} %fusion.4.u_ref, f32[256,512]{1,0:T(8,128)S(1)} %copy-done.16, f32[256,512]{1,0:T(8,128)S(1)} %copy-done.18), custom_call_target="tpu_custom_call" | custom-call | flops 67108864 | bytes 2228224 | tf_op jit(solution)/shard_map/final/pallas_call | solution.py:35
  99.8 0.9 pad_maximum_fusion
  (83 shorter events, 11.9 us)
Async XLA Ops:
  0.6 1.0 copy-start.4
  1.6 0.9 copy-start.7
  2.8 29.2 %copy-start.5 = (bf16[256,512]{1,0:T(8,128)(2,1)S(1)}, bf16[256,512]{1,0:T(8,128)(2,1)}, u32[]{:S(2)}) copy-start(bf16[256,512]{1,0:T(8,128)(2,1)} %k_ref.5) | copy-start | bytes 786436
  2.8 6.5 %collective-permute-start.3 = (bf16[512,128]{1,0:T(8,128)(2,1)S(1)}, bf16[512,128]{1,0:T(8,128)(2,1)S(1)}, u32[]{:S(2)}, u32[]{:S(2)}) collective-permute-start(bf16[512,128]{1,0:T(8,128)(2,1)S(1)} %state.1), channel_id=1, source_target_pairs={{0,4},{4,0},{8,12},{12,8},{16,20},{20,16},{24,28},{28,24},{1,5},{5... | collective-permute-start | bytes 393224 | tf_op jit(solution)/shard_map/ppermute | solution.py:206
  5.9 8.0 %collective-permute-start.1 = (bf16[256,512]{1,0:T(8,128)(2,1)}, bf16[256,512]{1,0:T(8,128)(2,1)S(1)}, u32[]{:S(2)}, u32[]{:S(2)}) collective-permute-start(bf16[256,512]{1,0:T(8,128)(2,1)} %refs_1_.1), channel_id=1, source_target_pairs={{0,2},{1,3},{2,0},{3,1},{4,6},{5,7},{6,4},{7,5},{8,10},{9,11},{10,... | collective-permute-start | bytes 786440 | tf_op jit(solution)/shard_map/ppermute | solution.py:206
  9.4 5.0 %collective-permute-start.4 = (bf16[512,128]{1,0:T(8,128)(2,1)S(1)}, bf16[512,128]{1,0:T(8,128)(2,1)S(1)}, u32[]{:S(2)}, u32[]{:S(2)}) collective-permute-start(bf16[512,128]{1,0:T(8,128)(2,1)S(1)} %add_convert_fusion.4), channel_id=1, source_target_pairs={{0,8},{4,12},{8,0},{12,4},{16,24},{20,28},{24,16},{28,20},{1,9},{5... | collective-permute-start | bytes 393224 | tf_op jit(solution)/shard_map/ppermute | solution.py:206
  11.3 12.4 %collective-permute-start = (bf16[256,512]{1,0:T(8,128)(2,1)}, bf16[256,512]{1,0:T(8,128)(2,1)S(1)}, u32[]{:S(2)}, u32[]{:S(2)}) collective-permute-start(bf16[256,512]{1,0:T(8,128)(2,1)} %refs_1_.1), channel_id=1, source_target_pairs={{0,1},{1,0},{2,3},{3,2},{4,5},{5,4},{6,7},{7,6},{8,9},{9,8},{10,11... | collective-permute-start | bytes 786440 | tf_op jit(solution)/shard_map/ppermute | solution.py:206
  13.8 9.9 %collective-permute-start.2 = (bf16[256,512]{1,0:T(8,128)(2,1)S(1)}, bf16[256,512]{1,0:T(8,128)(2,1)S(1)}, u32[]{:S(2)}, u32[]{:S(2)}) collective-permute-start(bf16[256,512]{1,0:T(8,128)(2,1)S(1)} %collective-permute-done.1.refs_3_), channel_id=1, source_target_pairs={{0,1},{1,0},{2,3},{3,2},{4,5},{5,4},{6,7},{7,6},{8,9},{9,8},{10,11... | collective-permute-start | bytes 786440 | tf_op jit(solution)/shard_map/ppermute | solution.py:206
  15.1 0.7 copy-start.13
  15.8 23.7 %collective-permute-start.5 = (bf16[512,128]{1,0:T(8,128)(2,1)}, bf16[512,128]{1,0:T(8,128)(2,1)}, u32[]{:S(2)}, u32[]{:S(2)}) collective-permute-start(bf16[512,128]{1,0:T(8,128)(2,1)} %add_convert_fusion.3), channel_id=1, source_target_pairs={{0,16},{4,20},{8,24},{12,28},{1,17},{5,21},{9,25},{13,29},{2,18},{... | collective-permute-start | bytes 393224 | tf_op jit(solution)/shard_map/ppermute | solution.py:212
  21.2 0.7 copy-start.27
  21.9 0.7 copy-start.28
  23.7 1.6 %copy-start = (bf16[512,2048]{1,0:T(8,128)(2,1)S(1)}, bf16[512,2048]{1,0:T(8,128)(2,1)}, u32[]{:S(2)}) copy-start(bf16[512,2048]{1,0:T(8,128)(2,1)} %w_ref.1) | copy-start | bytes 6291460
  25.3 0.9 copy-start.10
  26.2 0.9 copy-start.24
  29.2 0.7 copy-start.19
  29.8 0.7 copy-start.21
  30.5 15.7 %copy-start.1 = (bf16[512,2048]{1,0:T(8,128)(2,1)S(1)}, bf16[512,2048]{1,0:T(8,128)(2,1)}, u32[]{:S(2)}) copy-start(bf16[512,2048]{1,0:T(8,128)(2,1)} %w_ref.1) | copy-start | bytes 6291460
  30.5 30.9 %collective-permute-start.14 = (bf16[3,512,128]{2,1,0:T(8,128)(2,1)}, bf16[3,512,128]{2,1,0:T(8,128)(2,1)}, u32[]{:S(2)}, u32[]{:S(2)}) collective-permute-start(bf16[3,512,128]{2,1,0:T(8,128)(2,1)} %get-tuple-element.38), channel_id=1, source_target_pairs={{0,4},{4,0},{8,12},{12,8},{16,20},{20,16},{24,28},{28,24},{1,5},{5... | collective-permute-start | bytes 1179656 | tf_op jit(solution)/shard_map/ppermute | solution.py:206
  32.0 1.0 copy-start.8
  33.0 0.9 copy-start.11
  33.9 0.9 copy-start.20
  34.8 0.9 copy-start.22
  37.8 0.8 copy-start.15
  38.6 0.8 copy-start.17
  39.4 1.0 copy-start.12
  40.4 0.9 copy-start.14
  41.3 0.9 copy-start.23
  42.2 0.8 copy-start.26
  46.9 1.0 copy-start.2
  48.8 15.4 %copy-start.3 = (bf16[4,256,512]{2,1,0:T(8,128)(2,1)S(1)}, bf16[4,256,512]{2,1,0:T(8,128)(2,1)}, u32[]{:S(2)}) copy-start(bf16[4,256,512]{2,1,0:T(8,128)(2,1)} %copy-done.2) | copy-start | bytes 3145732
  48.8 15.4 %collective-permute-start.6 = (bf16[2,256,512]{2,1,0:T(8,128)(2,1)}, bf16[2,256,512]{2,1,0:T(8,128)(2,1)}, u32[]{:S(2)}, u32[]{:S(2)}) collective-permute-start(bf16[2,256,512]{2,1,0:T(8,128)(2,1)} %slice.78), channel_id=1, source_target_pairs={{0,1},{1,0},{2,3},{3,2},{4,5},{5,4},{6,7},{7,6},{8,9},{9,8},{10,11... | collective-permute-start | bytes 1572872 | tf_op jit(solution)/shard_map/ppermute | solution.py:206
  48.8 3.7 %collective-permute-start.17 = (f32[16,4]{1,0:T(8,128)S(1)}, f32[16,4]{1,0:T(8,128)S(1)}, u32[]{:S(2)}, u32[]{:S(2)}) collective-permute-start(f32[16,4]{1,0:T(8,128)S(1)} %get-tuple-element.43), channel_id=1, source_target_pairs={{0,4},{4,0},{8,12},{12,8},{16,20},{20,16},{24,28},{28,24},{1,5},{5... | collective-permute-start | bytes 776 | tf_op jit(solution)/shard_map/ppermute | solution.py:206
  52.4 3.7 %collective-permute-start.18 = (f32[16,4]{1,0:T(8,128)S(1)}, f32[16,4]{1,0:T(8,128)S(1)}, u32[]{:S(2)}, u32[]{:S(2)}) collective-permute-start(f32[16,4]{1,0:T(8,128)S(1)} %add.70), channel_id=1, source_target_pairs={{0,8},{4,12},{8,0},{12,4},{16,24},{20,28},{24,16},{28,20},{1,9},{5... | collective-permute-start | bytes 776 | tf_op jit(solution)/shard_map/ppermute | solution.py:206
  55.4 13.2 %collective-permute-start.8 = (bf16[4,256,256]{2,1,0:T(8,128)(2,1)}, bf16[4,256,256]{2,1,0:T(8,128)(2,1)}, u32[]{:S(2)}, u32[]{:S(2)}) collective-permute-start(bf16[4,256,256]{2,1,0:T(8,128)(2,1)} %get-tuple-element.34), channel_id=1, source_target_pairs={{0,4},{4,0},{8,12},{12,8},{16,20},{20,16},{24,28},{28,24},{1,5},{5... | collective-permute-start | bytes 1572872 | tf_op jit(solution)/shard_map/ppermute | solution.py:206
  56.1 4.6 %collective-permute-start.19 = (f32[16,4]{1,0:T(8,128)S(1)}, f32[16,4]{1,0:T(8,128)S(1)}, u32[]{:S(2)}, u32[]{:S(2)}) collective-permute-start(f32[16,4]{1,0:T(8,128)S(1)} %add.71), channel_id=1, source_target_pairs={{0,16},{4,20},{8,24},{12,28},{16,0},{20,4},{24,8},{28,12},{1,17},{... | collective-permute-start | bytes 776 | tf_op jit(solution)/shard_map/ppermute | solution.py:206
  56.6 15.2 %collective-permute-start.11 = (bf16[4,256,256]{2,1,0:T(8,128)(2,1)}, bf16[4,256,256]{2,1,0:T(8,128)(2,1)S(1)}, u32[]{:S(2)}, u32[]{:S(2)}) collective-permute-start(bf16[4,256,256]{2,1,0:T(8,128)(2,1)} %get-tuple-element.36), channel_id=1, source_target_pairs={{0,8},{4,12},{8,0},{12,4},{16,24},{20,28},{24,16},{28,20},{1,9},{5... | collective-permute-start | bytes 1572872 | tf_op jit(solution)/shard_map/ppermute | solution.py:206
  62.5 21.3 %collective-permute-start.15 = (bf16[2,512,128]{2,1,0:T(8,128)(2,1)S(1)}, bf16[2,512,128]{2,1,0:T(8,128)(2,1)S(1)}, u32[]{:S(2)}, u32[]{:S(2)}) collective-permute-start(bf16[2,512,128]{2,1,0:T(8,128)(2,1)S(1)} %add_convert_fusion), channel_id=1, source_target_pairs={{0,8},{4,12},{8,0},{12,4},{16,24},{20,28},{24,16},{28,20},{1,9},{5... | collective-permute-start | bytes 786440 | tf_op jit(solution)/shard_map/ppermute | solution.py:206
  65.4 33.6 %collective-permute-start.7 = (bf16[1,256,512]{2,1,0:T(8,128)(2,1)S(1)}, bf16[1,256,512]{2,1,0:T(8,128)(2,1)S(1)}, u32[]{:S(2)}, u32[]{:S(2)}) collective-permute-start(bf16[1,256,512]{2,1,0:T(8,128)(2,1)S(1)} %slice.121), channel_id=1, source_target_pairs={{0,2},{1,3},{2,0},{3,1},{4,6},{5,7},{6,4},{7,5},{8,10},{9,11},{10,... | collective-permute-start | bytes 786440 | tf_op jit(solution)/shard_map/ppermute | solution.py:206
  69.8 18.1 %collective-permute-start.9 = (bf16[2,256,256]{2,1,0:T(8,128)(2,1)S(1)}, bf16[2,256,256]{2,1,0:T(8,128)(2,1)S(1)}, u32[]{:S(2)}, u32[]{:S(2)}) collective-permute-start(bf16[2,256,256]{2,1,0:T(8,128)(2,1)S(1)} %slice.120), channel_id=1, source_target_pairs={{0,8},{4,12},{8,0},{12,4},{16,24},{20,28},{24,16},{28,20},{1,9},{5... | collective-permute-start | bytes 786440 | tf_op jit(solution)/shard_map/ppermute | solution.py:206
  72.0 25.9 %copy-start.6 = (bf16[256,512]{1,0:T(8,128)(2,1)S(1)}, bf16[256,512]{1,0:T(8,128)(2,1)}, u32[]{:S(2)}) copy-start(bf16[256,512]{1,0:T(8,128)(2,1)} %k_ref.5) | copy-start | bytes 786436
  72.0 25.9 %copy-start.9 = (bf16[256,512]{1,0:T(8,128)(2,1)S(1)}, bf16[256,512]{1,0:T(8,128)(2,1)}, u32[]{:S(2)}) copy-start(bf16[256,512]{1,0:T(8,128)(2,1)} %v_ref.5) | copy-start | bytes 786436
  72.0 25.9 %copy-start.16 = (f32[256,512]{1,0:T(8,128)S(1)}, f32[256,512]{1,0:T(8,128)}, u32[]{:S(2)}) copy-start(f32[256,512]{1,0:T(8,128)} %copy-done.15) | copy-start | bytes 1572868
  72.0 25.9 %copy-start.18 = (f32[256,512]{1,0:T(8,128)S(1)}, f32[256,512]{1,0:T(8,128)}, u32[]{:S(2)}) copy-start(f32[256,512]{1,0:T(8,128)} %copy-done.17) | copy-start | bytes 1572868
  72.0 16.9 %collective-permute-start.12 = (bf16[2,256,256]{2,1,0:T(8,128)(2,1)S(1)}, bf16[2,256,256]{2,1,0:T(8,128)(2,1)S(1)}, u32[]{:S(2)}, u32[]{:S(2)}) collective-permute-start(bf16[2,256,256]{2,1,0:T(8,128)(2,1)S(1)} %slice.119), channel_id=1, source_target_pairs={{0,16},{4,20},{8,24},{12,28},{16,0},{20,4},{24,8},{28,12},{1,17},{... | collective-permute-start | bytes 786440 | tf_op jit(solution)/shard_map/ppermute | solution.py:206
  83.9 13.0 %collective-permute-start.16 = (bf16[1,512,128]{2,1,0:T(8,128)(2,1)S(1)}, bf16[1,512,128]{2,1,0:T(8,128)(2,1)S(1)}, u32[]{:S(2)}, u32[]{:S(2)}) collective-permute-start(bf16[1,512,128]{2,1,0:T(8,128)(2,1)S(1)} %add_convert_fusion.2), channel_id=1, source_target_pairs={{16,0},{20,4},{24,8},{28,12},{17,1},{21,5},{25,9},{29,13},{18,2},{... | collective-permute-start | bytes 393224 | tf_op jit(solution)/shard_map/ppermute | solution.py:212
  88.0 11.8 %collective-permute-start.10 = (bf16[1,256,256]{2,1,0:T(8,128)(2,1)S(1)}, bf16[1,256,256]{2,1,0:T(8,128)(2,1)S(1)}, u32[]{:S(2)}, u32[]{:S(2)}) collective-permute-start(bf16[1,256,256]{2,1,0:T(8,128)(2,1)S(1)} %slice.123), channel_id=1, source_target_pairs={{0,16},{4,20},{8,24},{12,28},{16,0},{20,4},{24,8},{28,12},{1,17},{... | collective-permute-start | bytes 393224 | tf_op jit(solution)/shard_map/ppermute | solution.py:206
  89.0 10.8 %collective-permute-start.13 = (bf16[1,256,256]{2,1,0:T(8,128)(2,1)S(1)}, bf16[1,256,256]{2,1,0:T(8,128)(2,1)S(1)}, u32[]{:S(2)}, u32[]{:S(2)}) collective-permute-start(bf16[1,256,256]{2,1,0:T(8,128)(2,1)S(1)} %slice.122), channel_id=1, source_target_pairs={{0,4},{4,0},{8,12},{12,8},{16,20},{20,16},{24,28},{28,24},{1,5},{5... | collective-permute-start | bytes 393224 | tf_op jit(solution)/shard_map/ppermute | solution.py:206
  (1 other events, 0.6 us)

commit v2 on v1

v2 whole, which is shorter than its diff:
```python
import functools
import math

import jax
import jax.numpy as jnp
from jax import lax
from jax.experimental import pallas as pl
from jax.experimental.pallas import tpu as pltpu
from jax.sharding import PartitionSpec as P

SPAN = 64
F32 = jnp.float32
BF16 = jnp.bfloat16
VMEM_LIMIT = None

VMEM_SPEC = pl.BlockSpec(memory_space=pltpu.VMEM)
SMEM_SPEC = pl.BlockSpec(memory_space=pltpu.SMEM)


def nn(left, right):
    return lax.dot_general(left, right, (((1,), (0,)), ((), ())), preferred_element_type=F32)


def nt(left, right):
    return lax.dot_general(left, right, (((1,), (1,)), ((), ())), preferred_element_type=F32)


def tn(left, right):
    return lax.dot_general(left, right, (((0,), (0,)), ((), ())), preferred_element_type=F32)


def local_call(body, outs, ins, scalars=0, flops=0, scratch=(), name=None):
    moved = sum(math.prod(o.shape) * o.dtype.itemsize for o in outs)
    moved += sum(math.prod(a.shape) * a.dtype.itemsize for a in ins)
    return pl.pallas_call(
        body,
        out_shape=tuple(outs),
        in_specs=[SMEM_SPEC] * scalars + [VMEM_SPEC] * (len(ins) - scalars),
        out_specs=tuple(VMEM_SPEC for _ in outs),
        scratch_shapes=scratch,
        compiler_params=pltpu.CompilerParams(vmem_limit_bytes=VMEM_LIMIT),
        cost_estimate=pl.CostEstimate(flops=flops, bytes_accessed=moved, transcendentals=0),
        name=name,
    )(*ins)


def shaped(shape, dtype):
    return jax.ShapeDtypeStruct(shape, dtype)


def state_body(heads, k_ref, v_ref, d_ref):
    size = k_ref.shape[1] // heads
    for h in range(heads):
        cols = slice(h * size, (h + 1) * size)
        d_ref[h * size : (h + 1) * size, :] = tn(k_ref[:, cols], v_ref[:, cols]).astype(BF16)


def coef_body(levels, scales, code_ref, table_ref, coef_ref, hot_ref):
    heads, codes = table_ref.shape
    table = table_ref[...]
    high = table.astype(BF16)
    low = (table - high.astype(F32)).astype(BF16)
    tokens = code_ref.shape[1]
    row = lax.broadcasted_iota(jnp.int32, (codes, tokens), 0)
    for l in range(levels):
        hot = jnp.where(row == code_ref[l : l + 1, :], 1.0, 0.0).astype(BF16)
        hot_ref[l * codes : (l + 1) * codes, :] = hot
        lam = lax.dot_general(hot, high, (((0,), (1,)), ((), ())), preferred_element_type=F32)
        lam = lam + lax.dot_general(hot, low, (((0,), (1,)), ((), ())), preferred_element_type=F32)
        coef_ref[:, l * heads : (l + 1) * heads] = lam * scales[l]


def grad_body(heads, local_levels, levels, count, group, rows, *refs):
    head_ref, seq_ref = refs[:2]
    blocks = refs[2 : 2 + count]
    w_ref, q_ref, coef_ref, g_ref, t_ref = refs[2 + count : 7 + count]
    picked = refs[7 + count : -1]
    full_ref = refs[-1]
    me = head_ref[0]
    width = blocks[0].shape[1]
    size = q_ref.shape[1] // heads
    total = None
    for m in range(count):
        start = pl.multiple_of((me ^ m) * width, width)
        block = blocks[m][...]
        full_ref[:, pl.ds(start, width)] = block
        part = nt(block, w_ref[:, pl.ds(start, width)])
        total = part if total is None else total + part
    g = total.astype(BF16)
    g_ref[...] = g
    for l in range(local_levels, levels):
        for h in range(heads):
            cols = slice(h * size, (h + 1) * size)
            scaled = (g[:, cols].astype(F32) * coef_ref[:, l * heads + h : l * heads + h + 1]).astype(BF16)
            t_ref[l - local_levels, h * size : (h + 1) * size, :] = tn(q_ref[:, cols], scaled).astype(BF16)
    if len(picked) == 1:
        picked[0][...] = full_ref[...]
        return
    low = seq_ref[0] & (group - 1)
    for m in range(group):
        for n in range(picked[m].shape[1] // rows):
            start = pl.multiple_of((n * group + (low ^ m)) * rows, rows)
            picked[m][:, n * rows : (n + 1) * rows] = full_ref[:, pl.ds(start, rows)]


def level_masks(tokens, local_levels):
    row = lax.broadcasted_iota(jnp.int32, (tokens, tokens), 0)
    col = lax.broadcasted_iota(jnp.int32, (tokens, tokens), 1)
    apart = (row // SPAN) ^ (col // SPAN)
    causal = col <= row
    masks = [causal & (apart == 0)]
    for l in range(1, local_levels):
        masks.append(causal & ((apart >> (l - 1)) == 1))
    return masks


def inner_body(heads, local_levels, scales, q_ref, k_ref, v_ref, g_ref, coef_ref,
               attn_ref, dq_ref, dk_ref, dv_ref, lev_ref):
    tokens = q_ref.shape[0]
    size = q_ref.shape[1] // heads
    masks = level_masks(tokens, local_levels)
    lane = lax.broadcasted_iota(jnp.int32, lev_ref.shape, 1)
    lev = jnp.zeros(lev_ref.shape, F32)
    for h in range(heads):
        cols = slice(h * size, (h + 1) * size)
        q, k, v, g = q_ref[:, cols], k_ref[:, cols], v_ref[:, cols], g_ref[:, cols]
        weight = jnp.zeros((tokens, tokens), F32)
        for l in range(local_levels):
            weight = jnp.where(masks[l], coef_ref[:, l * heads + h : l * heads + h + 1], weight)
        scores = nt(q, k)
        grads = nt(g, v)
        both = scores * grads
        for l in range(local_levels):
            part = jnp.sum(jnp.where(masks[l], both, 0.0), axis=1, keepdims=True) * scales[l]
            lev = jnp.where(lane == l * heads + h, part, lev)
        scores = (scores * weight).astype(BF16)
        grads = (grads * weight).astype(BF16)
        attn_ref[:, cols] = nn(scores, v)
        dq_ref[:, cols] = nn(grads, k)
        dk_ref[:, cols] = tn(grads, q)
        dv_ref[:, cols] = tn(scores, g)
    lev_ref[...] = lev


def outer_body(heads, local_levels, which, levels, scales, norm, seq_ref, q_ref, g_ref, coef_ref,
               attn_in, dq_in, lev_in, *rest):
    states = rest[: len(which)]
    rest = rest[len(which) :]
    me = seq_ref[0]
    tokens = q_ref.shape[0]
    size = q_ref.shape[1] // heads
    last = norm is not None
    if last:
        hot_ref, attn_ref, dq_ref = rest
    else:
        attn_ref, dq_ref, lev_ref = rest
    lane = lax.broadcasted_iota(jnp.int32, lev_in.shape, 1)
    lev = lev_in[...]
    for h in range(heads):
        cols = slice(h * size, (h + 1) * size)
        q, g = q_ref[:, cols], g_ref[:, cols]
        qf = q.astype(F32)
        attn = attn_in[:, cols]
        dq = dq_in[:, cols]
        for n, l in enumerate(which):
            owned = ((me >> (l - local_levels)) & 1).astype(F32)
            state = states[n][h * size : (h + 1) * size, :]
            coef = coef_ref[:, l * heads + h : l * heads + h + 1] * owned
            attn = attn + coef * nn(q, state)
            back = nt(g, state)
            dq = dq + coef * back
            part = jnp.sum(qf * back, axis=1, keepdims=True) * (owned * scales[l])
            lev = jnp.where(lane == l * heads + h, part, lev)
        attn_ref[:tokens, cols] = attn.astype(attn_ref.dtype)
        dq_ref[:, cols] = dq.astype(dq_ref.dtype)
    if not last:
        lev_ref[...] = lev
        return
    codes = attn_ref.shape[0] - tokens
    high = lev.astype(BF16)
    low = (lev - high.astype(F32)).astype(BF16)
    total = jnp.zeros((codes, heads), F32)
    for l in range(levels):
        hot = hot_ref[l * codes : (l + 1) * codes, :]
        pick = slice(l * heads, (l + 1) * heads)
        total = total + nn(hot, high[:, pick]) + nn(hot, low[:, pick])
    total = total * norm
    high = total.astype(BF16)
    low = total - high.astype(F32)
    attn_ref[tokens:, :] = jnp.zeros((codes, attn_ref.shape[1]), BF16)
    attn_ref[tokens:, :heads] = high
    attn_ref[tokens:, heads : 2 * heads] = low.astype(BF16)


def weight_body(masks, scale, group_bits, heads, seq_ref, *refs):
    count = 1 << group_bits
    picked, attns = refs[:count], refs[count : 2 * count]
    out_ref, table_ref = refs[2 * count : 2 * count + 2]
    scratch = refs[2 * count + 2 :]
    me = seq_ref[0] >> group_bits
    rows = out_ref.shape[1]
    tokens = picked[0].shape[0]
    codes = table_ref.shape[0]

    def product(cols):
        total = None
        for m in range(count):
            part = tn(picked[m][:, cols], attns[m][:tokens, :])
            total = part if total is None else total + part
        return total * scale

    if scratch:
        scratch[0][...] = product(slice(None))
    for n, m in enumerate(masks):
        start = pl.multiple_of((me ^ m) * rows, rows)
        total = scratch[0][pl.ds(start, rows), :] if scratch else product(pl.ds(start, rows))
        out_ref[n] = total.astype(out_ref.dtype)
    table = jnp.zeros((codes, heads), F32)
    for m in range(count):
        both = attns[m][tokens:, : 2 * heads].astype(F32)
        table = table + both[:, :heads] + both[:, heads:]
    table_ref[...] = table


def mixed_body(masks, head_ref, attn_ref, w_ref, send_ref, keep_ref):
    me = head_ref[0]
    tokens, width = send_ref.shape[1:]
    attn = attn_ref[:tokens, :]
    half = len(masks) // 2
    for n, m in enumerate(masks[half:] + masks[:half]):
        start = pl.multiple_of((me ^ m) * width, width)
        out_ref = send_ref if n < half else keep_ref
        out_ref[n % half] = nn(attn, w_ref[:, pl.ds(start, width)]).astype(BF16)


def final_body(heads, count, seq_ref, k_ref, v_ref, dk_in, dv_in, *rest):
    terms = rest[:count]
    dk_ref, dv_ref = rest[count:]
    me = seq_ref[0]
    size = k_ref.shape[1] // heads
    for h in range(heads):
        cols = slice(h * size, (h + 1) * size)
        u = jnp.zeros((size, size), F32)
        for b in range(count):
            owned = (1 - ((me >> b) & 1)).astype(F32)
            u = u + owned * terms[b][0, h * size : (h + 1) * size, :].astype(F32)
        u = u.astype(BF16)
        dk_ref[:, cols] = (dk_in[:, cols] + nt(v_ref[:, cols], u)).astype(BF16)
        dv_ref[:, cols] = (dv_in[:, cols] + nn(k_ref[:, cols], u)).astype(BF16)


def swap(value, axis, mask):
    pairs = [(i, i ^ mask) for i in range(lax.axis_size(axis))]
    return lax.ppermute(value, axis, pairs)


def one_way(value, axis, mask, up):
    n = lax.axis_size(axis)
    pairs = [(i, i ^ mask) for i in range(n) if (i & mask == 0) == up]
    return lax.ppermute(value, axis, pairs)


def reduce_blocks(send, keep, axis, bits, name):
    parts = [keep]
    for n, bit in enumerate(bits):
        if n > 0:
            half = parts[0].shape[0] // 2
            send = sum(part[half:].astype(F32) for part in parts).astype(BF16)
            parts = [part[:half] for part in parts]
        with jax.named_scope(f"{name}_{n}"):
            parts.append(swap(send, axis, 1 << bit))
    return sum(part[0].astype(F32) for part in parts)


def bit_order(bits):
    masks = [0]
    for bit in reversed(range(bits)):
        masks = masks + [m | (1 << bit) for m in masks]
    return masks


def per_device(queries, keys, values, level_table, level_code, out_weight, cotangent):
    tokens, cols = queries.shape
    heads = level_table.shape[1]
    codes = level_table.shape[0]
    size = cols // heads
    width = out_weight.shape[1]
    spans = tokens // SPAN
    local_bits = spans.bit_length() - 1
    seq_count = lax.axis_size("seq")
    seq_bits = seq_count.bit_length() - 1
    head_count = lax.axis_size("head")
    head_bits = head_count.bit_length() - 1
    local_levels = 1 + local_bits
    levels = local_levels + seq_bits
    group_bits = min(2, seq_bits - 1)
    group = 1 << group_bits
    high_bits = seq_bits - group_bits
    rows = width // seq_count
    scales = [1.0 / math.sqrt(SPAN * 2 ** max(l - 1, 0)) for l in range(levels)]
    seq_me = lax.axis_index("seq").astype(jnp.int32)
    head_me = lax.axis_index("head").astype(jnp.int32)
    seq_one = seq_me.reshape(1)
    head_one = head_me.reshape(1)

    blocks = {0: cotangent}
    for bit in reversed(range(head_bits)):
        for m in list(blocks):
            with jax.named_scope(f"gather_{m | (1 << bit)}"):
                blocks[m | (1 << bit)] = swap(blocks[m], "head", 1 << bit)

    (state,) = local_call(
        functools.partial(state_body, heads),
        [shaped((cols, size), BF16)],
        [keys, values],
        flops=2 * tokens * cols * size,
        name="state",
    )
    coef, hot = local_call(
        functools.partial(coef_body, levels, scales),
        [shaped((tokens, levels * heads), F32), shaped((levels * codes, tokens), BF16)],
        [level_code.T, level_table.T],
        flops=4 * tokens * levels * codes * heads,
        name="coef",
    )
    found = []
    block_state = state
    for bit in range(seq_bits):
        with jax.named_scope(f"state_{bit}"):
            if bit == seq_bits - 1:
                found.append(one_way(block_state, "seq", 1 << bit, True))
            else:
                got = swap(block_state, "seq", 1 << bit)
                found.append(got)
        if bit < seq_bits - 1:
            block_state = (block_state.astype(F32) + got.astype(F32)).astype(BF16)

    aligned = rows % 128 == 0
    kept = [shaped((tokens, width // group), BF16)] * group if aligned else [shaped((tokens, width), BF16)]
    g, terms, *picked = local_call(
        functools.partial(grad_body, heads, local_levels, levels, head_count, group, rows),
        [shaped((tokens, cols), BF16), shaped((seq_bits, cols, size), BF16)] + kept,
        [head_one, seq_one] + [blocks[m] for m in range(head_count)] + [out_weight, queries, coef],
        scalars=2,
        flops=2 * tokens * cols * width,
        scratch=[pltpu.VMEM((tokens, width), BF16)],
        name="grad",
    )
    if not aligned:
        split = picked[0].reshape(tokens, seq_count // group, group, rows)
        picked = [
            lax.dynamic_index_in_dim(split, (seq_me & (group - 1)) ^ m, 2, False).reshape(tokens, width // group)
            for m in range(group)
        ]
    term_parts = []
    for bit in range(seq_bits):
        with jax.named_scope(f"terms_{bit}"):
            if bit == seq_bits - 1:
                got = one_way(terms, "seq", 1 << bit, False)
            else:
                got = swap(terms, "seq", 1 << bit)
        term_parts.append(got)
        if bit < seq_bits - 1:
            terms = (terms[1:].astype(F32) + got[1:].astype(F32)).astype(BF16)
    for m in range(1, group):
        with jax.named_scope(f"rows_{m}"):
            picked[m] = swap(picked[m], "seq", m)

    lev_shape = shaped((tokens, 128 * pl.cdiv(levels * heads, 128)), F32)
    attn_in, dq_in, dk_in, dv_in, lev = local_call(
        functools.partial(inner_body, heads, local_levels, scales),
        [shaped((tokens, cols), F32)] * 4 + [lev_shape],
        [queries, keys, values, g, coef],
        flops=12 * tokens * tokens * cols,
        name="inner",
    )
    table_norm = 1.0 / math.sqrt(tokens * seq_count * levels)
    if levels - 1 > local_levels:
        attn_in, dq_in, lev = local_call(
            functools.partial(outer_body, heads, local_levels, range(local_levels, levels - 1), levels, scales, None),
            [shaped((tokens, cols), F32)] * 2 + [lev_shape],
            [seq_one, queries, g, coef, attn_in, dq_in, lev] + found[:-1],
            scalars=1,
            flops=4 * tokens * cols * size * (seq_bits - 1),
            name="middle",
        )
    attn, query_grad = local_call(
        functools.partial(outer_body, heads, local_levels, [levels - 1], levels, scales, table_norm),
        [shaped((tokens + codes, cols), BF16), shaped((tokens, cols), BF16)],
        [seq_one, queries, g, coef, attn_in, dq_in, lev, found[-1], hot],
        scalars=1,
        flops=4 * tokens * cols * size,
        name="outer",
    )
    attns = [attn]
    for m in range(1, group):
        with jax.named_scope(f"attn_{m}"):
            attns.append(swap(attn, "seq", m))

    masks_m = bit_order(head_bits)
    send_shape = shaped((head_count // 2, tokens, width // head_count), BF16)
    send, keep = local_call(
        functools.partial(mixed_body, masks_m),
        [send_shape, send_shape],
        [head_one, attn, out_weight],
        scalars=1,
        flops=2 * tokens * cols * width,
        name="mixed",
    )
    mixed = reduce_blocks(send, keep, "head", range(head_bits), "mixed").astype(BF16)

    weight_norm = 1.0 / math.sqrt(tokens * seq_count)
    masks_w = bit_order(high_bits)
    half = len(masks_w) // 2

    def weight_part(masks, dtype, name):
        return local_call(
            functools.partial(weight_body, masks, weight_norm, group_bits, heads),
            [shaped((half, rows, cols), dtype), shaped((codes, heads), F32)],
            [seq_one] + picked + attns,
            scalars=1,
            flops=tokens * cols * width,
            scratch=[] if aligned else [pltpu.VMEM((width // group, cols), F32)],
            name=name,
        )

    weight_send, table_grad = weight_part(masks_w[half:], BF16, "weight_send")
    weight_keep, _ = weight_part(masks_w[:half], F32, "weight_keep")
    out_weight_grad = reduce_blocks(weight_send, weight_keep, "seq", range(group_bits, seq_bits), "weight")
    for bit in range(group_bits, seq_bits):
        with jax.named_scope(f"table_{bit}"):
            table_grad = table_grad + swap(table_grad, "seq", 1 << bit)

    key_grad, value_grad = local_call(
        functools.partial(final_body, heads, seq_bits),
        [shaped((tokens, cols), BF16)] * 2,
        [seq_one, keys, values, dk_in, dv_in] + term_parts,
        scalars=1,
        flops=4 * tokens * cols * size,
        name="final",
    )
    return mixed, out_weight_grad, query_grad, key_grad, value_grad, table_grad


def solution(mesh):
    placed = (
        P("seq", "head"),
        P("seq", "head"),
        P("seq", "head"),
        P(None, "head"),
        P("seq", None),
        P("head", None),
        P("seq", "head"),
    )
    return jax.shard_map(
        per_device,
        mesh=mesh,
        in_specs=placed,
        out_specs=(
            P("seq", "head"),
            P("seq", "head"),
            P("seq", "head"),
            P("seq", "head"),
            P("seq", "head"),
            P(None, "head"),
        ),
        check_vma=False,
    )
```

time: 101 us -> 91.4 us (0.905)
  Pallas kernels: 11.6 us -> 30.4 us
  local copies, waits for them, and re-layouts: 21 us -> 3.44 us
  starting transfers between devices: 35.7 us -> 23.6 us
  waiting for transfers between devices: 24.3 us -> 28.7 us
  other arithmetic: 7.09 us -> 3.92 us
    pallas_call x9 -> x10, Pallas kernels: 11.6 us -> 30.4 us  [local_call(): pl.pallas_call(body, out_shape=tuple(outs), in_specs=[SMEM_SPEC] * scalar...]
    unnamed x59 -> x37, local copies, waits for them, and re-layouts: 20 us -> 3.44 us
    ppermute x18 -> x17, starting transfers between devices: 29.1 us -> 17.8 us  [swap(): return lax.ppermute(value, axis, pairs)]
    ppermute x2, waiting for transfers between devices: 0.88 us -> 6.47 us  [one_way(): return lax.ppermute(value, axis, pairs)]
    add x9 -> x2, other arithmetic: 3.54 us -> 1.91 us  [the longest x1 1.91 us: reduce_blocks(): return sum((part[0].astype(F32) for part in parts))]
    ppermute x18 -> x17, waiting for transfers between devices: 23.4 us -> 22.3 us  [swap(): return lax.ppermute(value, axis, pairs)]
    convert_element_type x2, other arithmetic: 1.14 us -> 0.11 us  [per_device(): terms = (terms[1:].astype(F32) + got[1:].astype(F32)).astype(BF16)]
  transfers between devices with their start and end apart: 20 -> 19, of which waited for: 11 -> 9; matrix products, arithmetic and copies ran while one was open for 8% -> 5% of each run, Pallas kernels for 11% -> 30%
where the time goes in v2:
time: 91.4 us; the launch traced here: 90.9 us
  Pallas kernels  30.4 us (33%)
  waiting for transfers between devices  28.7 us (31%)
  starting transfers between devices  23.6 us (26%)
  other arithmetic  3.92 us (4%)
  local copies, waits for them, and re-layouts  3.44 us (4%)
    pallas_call x10, Pallas kernels, local_call(): pl.pallas_call(body, out_shape=tuple(outs), in_specs=[SMEM_SPEC] * scalar...  30.4 us
    ppermute x17, waiting for transfers between devices, swap(): return lax.ppermute(value, axis, pairs)  22.3 us
    ppermute x17, starting transfers between devices, swap(): return lax.ppermute(value, axis, pairs)  17.8 us
    ppermute x2, waiting for transfers between devices, one_way(): return lax.ppermute(value, axis, pairs)  6.47 us
    ppermute x2, starting transfers between devices, one_way(): return lax.ppermute(value, axis, pairs)  5.8 us
    unnamed x37, local copies, waits for them, and re-layouts  3.44 us
    add x1, other arithmetic, reduce_blocks(): return sum((part[0].astype(F32) for part in parts))  1.91 us
  transfers between devices with their start and end apart: 19, of which 9 were waited for; matrix products, arithmetic and copies ran while one was open for 5% of the time, Pallas kernels for 30%

profile of v2, /device:TPU:0, one launch (start us, length us, event | category | flops | bytes accessed | tf_op | source)
XLA Modules:
  0.0 90.9 jit_solution(7563933926176800340)
XLA Ops:
  0.6 3.1 %collective-permute-start.1 = (bf16[256,512]{1,0:T(8,128)(2,1)}, bf16[256,512]{1,0:T(8,128)(2,1)S(1)}, u32[]{:S(2)}, u32[]{:S(2)}) collective-permute-start(bf16[256,512]{1,0:T(8,128)(2,1)} %refs_2_.1), channel_id=1, source_target_pairs={{0,2},{1,3},{2,0},{3,1},{4,6},{5,7},{6,4},{7,5},{8,10},{9,11},{10,... | collective-permute-start | bytes 786440 | tf_op jit(solution)/shard_map/gather_2/ppermute | solution.py:254
  3.7 2.0 %state.1 = bf16[512,128]{1,0:T(8,128)(2,1)} custom-call(bf16[256,512]{1,0:T(8,128)(2,1)} %k_ref.5, bf16[256,512]{1,0:T(8,128)(2,1)} %v_ref.5), custom_call_target="tpu_custom_call" | custom-call | flops 33554432 | bytes 655360 | tf_op jit(solution)/shard_map/state/pallas_call | solution.py:35
  5.6 1.5 %collective-permute-start.3 = (bf16[512,128]{1,0:T(8,128)(2,1)}, bf16[512,128]{1,0:T(8,128)(2,1)S(1)}, u32[]{:S(2)}, u32[]{:S(2)}) collective-permute-start(bf16[512,128]{1,0:T(8,128)(2,1)} %state.1), channel_id=1, source_target_pairs={{0,4},{4,0},{8,12},{12,8},{16,20},{20,16},{24,28},{28,24},{1,5},{5... | collective-permute-start | bytes 393224 | tf_op jit(solution)/shard_map/state_0/ppermute | solution.py:254
  7.1 3.1 %collective-permute-done.1.refs_4_ = bf16[256,512]{1,0:T(8,128)(2,1)S(1)} collective-permute-done((bf16[256,512]{1,0:T(8,128)(2,1)}, bf16[256,512]{1,0:T(8,128)(2,1)S(1)}, u32[]{:S(2)}, u32[]{:S(2)}) %collective-permute-start.1) | collective-permute-done | bytes 262176 | tf_op jit(solution)/shard_map/gather_2/ppermute | solution.py:254
  10.2 0.0 collective-permute-start.2
  10.2 0.6 collective-permute-done.3.rest_0_
  10.8 1.0 %add_convert_fusion.5 = bf16[512,128]{1,0:T(8,128)(2,1)S(1)} fusion(bf16[512,128]{1,0:T(8,128)(2,1)S(1)} %collective-permute-done.3.rest_0_, bf16[512,128]{1,0:T(8,128)(2,1)} %state.1), kind=kLoop, calls=%fused_computation.7 | loop fusion | flops 262144 | bytes 393216 | tf_op jit(solution)/shard_map/convert_element_type | solution.py:336
  11.8 1.6 %collective-permute-start.4 = (bf16[512,128]{1,0:T(8,128)(2,1)S(1)}, bf16[512,128]{1,0:T(8,128)(2,1)S(1)}, u32[]{:S(2)}, u32[]{:S(2)}) collective-permute-start(bf16[512,128]{1,0:T(8,128)(2,1)S(1)} %add_convert_fusion.5), channel_id=1, source_target_pairs={{0,8},{4,12},{8,0},{12,4},{16,24},{20,28},{24,16},{28,20},{1,9},{5... | collective-permute-start | bytes 393224 | tf_op jit(solution)/shard_map/state_1/ppermute | solution.py:254
  13.5 1.9 %coef.1 = (f32[256,24]{1,0:T(8,128)}, bf16[96,256]{1,0:T(8,128)(2,1)}) custom-call(s32[6,256]{1,0:T(8,128)} %bitcast.8, f32[4,16]{1,0:T(4,128)} %bitcast.9), custom_call_target="tpu_custom_call" | custom-call | flops 393216 | bytes 80128 | tf_op jit(solution)/shard_map/coef/pallas_call | solution.py:35
  15.3 0.0 copy-start.13
  15.4 0.7 copy-done.12
  16.0 0.1 copy-done.13
  16.1 4.3 %grad.1 = (bf16[256,512]{1,0:T(8,128)(2,1)}, bf16[3,512,128]{2,1,0:T(8,128)(2,1)}, bf16[256,512]{1,0:T(8,128)(2,1)}, bf16[256,512]{1,0:T(8,128)(2,1)}, bf16[256,...) custom-call(s32[1]{0:T(128)} %bitcast.refs_0_.head_ref, s32[1]{0:T(128)} %bitcast.1.refs_1_.seq_ref, bf16[256,512]{1,0:T(8,128)(2,1)} %refs_2_.1, ...), custom_call_target="tpu_custom_call" | custom-call | flops 536870912 | bytes 5136392 | tf_op jit(solution)/shard_map/grad/pallas_call | solution.py:35
  20.4 1.5 %collective-permute-start.8 = (bf16[256,512]{1,0:T(8,128)(2,1)}, bf16[256,512]{1,0:T(8,128)(2,1)S(1)}, u32[]{:S(2)}, u32[]{:S(2)}) collective-permute-start(bf16[256,512]{1,0:T(8,128)(2,1)} %get-tuple-element.44), channel_id=1, source_target_pairs={{0,4},{4,0},{8,12},{12,8},{16,20},{20,16},{24,28},{28,24},{1,5},{5... | collective-permute-start | bytes 786440 | tf_op jit(solution)/shard_map/rows_1/ppermute | solution.py:254
  21.9 0.5 collective-permute-start.9
  22.3 1.5 %collective-permute-start.10 = (bf16[256,512]{1,0:T(8,128)(2,1)}, bf16[256,512]{1,0:T(8,128)(2,1)S(1)}, u32[]{:S(2)}, u32[]{:S(2)}) collective-permute-start(bf16[256,512]{1,0:T(8,128)(2,1)} %get-tuple-element.46), channel_id=1, source_target_pairs={{0,12},{4,8},{8,4},{12,0},{16,28},{20,24},{24,20},{28,16},{1,13},{... | collective-permute-start | bytes 786440 | tf_op jit(solution)/shard_map/rows_3/ppermute | solution.py:254
  23.9 4.5 %collective-permute-start.5 = (bf16[512,128]{1,0:T(8,128)(2,1)S(1)}, bf16[512,128]{1,0:T(8,128)(2,1)S(1)}, u32[]{:S(2)}, u32[]{:S(2)}) collective-permute-start(bf16[512,128]{1,0:T(8,128)(2,1)S(1)} %add_convert_fusion.4), channel_id=1, source_target_pairs={{0,16},{4,20},{8,24},{12,28},{1,17},{5,21},{9,25},{13,29},{2,18},{... | collective-permute-start | bytes 393224 | tf_op jit(solution)/shard_map/state_2/ppermute | solution.py:260
  28.4 1.6 %collective-permute-start.15 = (bf16[3,512,128]{2,1,0:T(8,128)(2,1)}, bf16[3,512,128]{2,1,0:T(8,128)(2,1)S(1)}, u32[]{:S(2)}, u32[]{:S(2)}) collective-permute-start(bf16[3,512,128]{2,1,0:T(8,128)(2,1)} %get-tuple-element.52), channel_id=1, source_target_pairs={{0,4},{4,0},{8,12},{12,8},{16,20},{20,16},{24,28},{28,24},{1,5},{5... | collective-permute-start | bytes 1179656 | tf_op jit(solution)/shard_map/terms_0/ppermute | solution.py:254
  30.0 4.4 %inner.1 = (f32[256,512]{1,0:T(8,128)}, f32[256,512]{1,0:T(8,128)}, f32[256,512]{1,0:T(8,128)}, f32[256,512]{1,0:T(8,128)}, f32[256,128]{1,0:T(8,128)}) custom-call(bf16[256,512]{1,0:T(8,128)(2,1)} %q_ref.5, bf16[256,512]{1,0:T(8,128)(2,1)} %k_ref.5, bf16[256,512]{1,0:T(8,128)(2,1)} %v_ref.5, bf16[256,512]{1,0:T(8,128)(2,1)} %get-tuple-element.32.g_ref, ...), custom_call_target="tpu_custom_call" | custom-call | flops 402653184 | bytes 3301376 | tf_op jit(solution)/shard_map/inner/pallas_call | solution.py:35
  34.4 3.4 %middle.1 = (f32[256,512]{1,0:T(8,128)}, f32[256,512]{1,0:T(8,128)}, f32[256,128]{1,0:T(8,128)}) custom-call(s32[1]{0:T(128)} %bitcast.1.refs_1_.seq_ref, bf16[256,512]{1,0:T(8,128)(2,1)} %q_ref.5, bf16[256,512]{1,0:T(8,128)(2,1)} %get-tuple-element.32.g_ref, f32[256,24]{1,0:T(8,128)} %get-tuple-element.31.refs_8_.coef_ref, ...), custom_call_target="tpu_custom_call" | custom-call | flops 134217728 | bytes 3170308 | tf_op jit(solution)/shard_map/middle/pallas_call | solution.py:35
  37.8 0.7 copy-done.15
  38.5 3.0 %outer.1 = (bf16[272,512]{1,0:T(8,128)(2,1)}, bf16[256,512]{1,0:T(8,128)(2,1)}) custom-call(s32[1]{0:T(128)} %bitcast.1.refs_1_.seq_ref, bf16[256,512]{1,0:T(8,128)(2,1)} %q_ref.5, bf16[256,512]{1,0:T(8,128)(2,1)} %get-tuple-element.32.g_ref, f32[256,24]{1,0:T(8,128)} %get-tuple-element.31.refs_8_.coef_ref, f32[256,512]{1,0:T(8,128)} %get-tuple-element.36.attn_in, ...), custom_call_target="tpu_custom_call" | custom-call | flops 67108864 | bytes 2449412 | tf_op jit(solution)/shard_map/outer/pallas_call | solution.py:35
  41.5 0.4 collective-permute-start.13
  41.9 1.6 %collective-permute-start.12 = (bf16[272,512]{1,0:T(8,128)(2,1)}, bf16[272,512]{1,0:T(8,128)(2,1)S(1)}, u32[]{:S(2)}, u32[]{:S(2)}) collective-permute-start(bf16[272,512]{1,0:T(8,128)(2,1)} %get-tuple-element.40.attn_ref.refs_4_), channel_id=1, source_target_pairs={{0,8},{4,12},{8,0},{12,4},{16,24},{20,28},{24,16},{28,20},{1,9},{5... | collective-permute-start | bytes 835592 | tf_op jit(solution)/shard_map/attn_2/ppermute | solution.py:254
  43.5 1.5 %collective-permute-start.11 = (bf16[272,512]{1,0:T(8,128)(2,1)}, bf16[272,512]{1,0:T(8,128)(2,1)S(1)}, u32[]{:S(2)}, u32[]{:S(2)}) collective-permute-start(bf16[272,512]{1,0:T(8,128)(2,1)} %get-tuple-element.40.attn_ref.refs_4_), channel_id=1, source_target_pairs={{0,4},{4,0},{8,12},{12,8},{16,20},{20,16},{24,28},{28,24},{1,5},{5... | collective-permute-start | bytes 835592 | tf_op jit(solution)/shard_map/attn_1/ppermute | solution.py:254
  45.0 3.2 %mixed.1 = (bf16[2,256,512]{2,1,0:T(8,128)(2,1)}, bf16[2,256,512]{2,1,0:T(8,128)(2,1)}) custom-call(s32[1]{0:T(128)} %bitcast.refs_0_.head_ref, bf16[272,512]{1,0:T(8,128)(2,1)} %get-tuple-element.40.attn_ref.refs_4_, bf16[512,2048]{1,0:T(8,128)(2,1)} %w_ref.1), custom_call_target="tpu_custom_call" | custom-call | flops 536870912 | bytes 3424260 | tf_op jit(solution)/shard_map/mixed/pallas_call | solution.py:35
  48.2 3.9 %collective-permute-done.13.refs_7_ = bf16[272,512]{1,0:T(8,128)(2,1)S(1)} collective-permute-done((bf16[272,512]{1,0:T(8,128)(2,1)}, bf16[272,512]{1,0:T(8,128)(2,1)S(1)}, u32[]{:S(2)}, u32[]{:S(2)}) %collective-permute-start.13) | collective-permute-done | bytes 278560 | tf_op jit(solution)/shard_map/attn_3/ppermute | solution.py:254
  52.1 2.6 %collective-permute-done.12.refs_6_ = bf16[272,512]{1,0:T(8,128)(2,1)S(1)} collective-permute-done((bf16[272,512]{1,0:T(8,128)(2,1)}, bf16[272,512]{1,0:T(8,128)(2,1)S(1)}, u32[]{:S(2)}, u32[]{:S(2)}) %collective-permute-start.12) | collective-permute-done | bytes 278560 | tf_op jit(solution)/shard_map/attn_2/ppermute | solution.py:254
  54.7 0.9 collective-permute-done.11.refs_5_
  55.6 0.7 copy-done.2
  56.3 2.8 %weight_send.1 = (bf16[1,256,512]{2,1,0:T(8,128)(2,1)}, f32[16,4]{1,0:T(8,128)}) custom-call(s32[1]{0:T(128)} %bitcast.1.refs_1_.seq_ref, bf16[256,512]{1,0:T(8,128)(2,1)} %get-tuple-element.43.refs_0_, bf16[256,512]{1,0:T(8,128)(2,1)} %copy-done.4, bf16[256,512]{1,0:T(8,128)(2,1)} %copy-done.5, bf16[256,512]{1,0:T(8,128)(2,1)} %copy-done.6, ...), custom_call_target="tpu_custom_call" | custom-call | flops 268435456 | bytes 2425092 | tf_op jit(solution)/shard_map/weight_send/pallas_call | solution.py:35
  59.1 1.9 %collective-permute-start.18 = (f32[16,4]{1,0:T(8,128)}, f32[16,4]{1,0:T(8,128)S(1)}, u32[]{:S(2)}, u32[]{:S(2)}) collective-permute-start(f32[16,4]{1,0:T(8,128)} %get-tuple-element.55), channel_id=1, source_target_pairs={{0,16},{4,20},{8,24},{12,28},{16,0},{20,4},{24,8},{28,12},{1,17},{... | collective-permute-start | bytes 776 | tf_op jit(solution)/shard_map/table_2/ppermute | solution.py:254
  61.0 1.0 %collective-permute-start.14 = (bf16[1,256,512]{2,1,0:T(8,128)(2,1)}, bf16[1,256,512]{2,1,0:T(8,128)(2,1)S(1)}, u32[]{:S(2)}, u32[]{:S(2)}) collective-permute-start(bf16[1,256,512]{2,1,0:T(8,128)(2,1)} %get-tuple-element.48), channel_id=1, source_target_pairs={{0,16},{4,20},{8,24},{12,28},{16,0},{20,4},{24,8},{28,12},{1,17},{... | collective-permute-start | bytes 786440 | tf_op jit(solution)/shard_map/weight_0/ppermute | solution.py:254
  62.0 2.8 %weight_keep.1 = (f32[1,256,512]{2,1,0:T(8,128)}, f32[16,4]{1,0:T(8,128)}) custom-call(s32[1]{0:T(128)} %bitcast.1.refs_1_.seq_ref, bf16[256,512]{1,0:T(8,128)(2,1)} %get-tuple-element.43.refs_0_, bf16[256,512]{1,0:T(8,128)(2,1)} %copy-done.4, bf16[256,512]{1,0:T(8,128)(2,1)} %copy-done.5, bf16[256,512]{1,0:T(8,128)(2,1)} %copy-done.6, ...), custom_call_target="tpu_custom_call" | custom-call | flops 268435456 | bytes 2687236 | tf_op jit(solution)/shard_map/weight_keep/pallas_call | solution.py:35
  64.8 4.3 %collective-permute-done.18 = f32[16,4]{1,0:T(8,128)S(1)} collective-permute-done((f32[16,4]{1,0:T(8,128)}, f32[16,4]{1,0:T(8,128)S(1)}, u32[]{:S(2)}, u32[]{:S(2)}) %collective-permute-start.18) | collective-permute-done | bytes 288 | tf_op jit(solution)/shard_map/table_2/ppermute | solution.py:254
  69.1 0.7 copy.13
  69.8 0.1 add_convert_fusion
  69.9 0.1 collective-permute-start.16
  70.0 0.1 add_convert_fusion.2
  70.0 0.1 collective-permute-start.7
  70.1 4.7 %collective-permute-done.14 = bf16[1,256,512]{2,1,0:T(8,128)(2,1)S(1)} collective-permute-done((bf16[1,256,512]{2,1,0:T(8,128)(2,1)}, bf16[1,256,512]{2,1,0:T(8,128)(2,1)S(1)}, u32[]{:S(2)}, u32[]{:S(2)}) %collective-permute-start.14) | collective-permute-done | bytes 262176 | tf_op jit(solution)/shard_map/weight_0/ppermute | solution.py:254
  74.8 1.9 %add_bitcast_fusion = f32[256,512]{1,0:T(8,128)} fusion(f32[1,256,512]{2,1,0:T(8,128)} %get-tuple-element.47, bf16[1,256,512]{2,1,0:T(8,128)(2,1)S(1)} %collective-permute-done.14), kind=kLoop, calls=%fused_computation.1 | loop fusion | flops 262144 | bytes 1310720 | tf_op jit(solution)/shard_map/add | solution.py:272
  76.7 2.2 %collective-permute-done.16.rest_1_ = bf16[2,512,128]{2,1,0:T(8,128)(2,1)S(1)} collective-permute-done((bf16[2,512,128]{2,1,0:T(8,128)(2,1)S(1)}, bf16[2,512,128]{2,1,0:T(8,128)(2,1)S(1)}, u32[]{:S(2)}, u32[]{:S(2)}) %collective-permute-start.16) | collective-permute-done | bytes 262176 | tf_op jit(solution)/shard_map/terms_1/ppermute | solution.py:254
  79.0 1.3 %collective-permute-start.17 = (bf16[1,512,128]{2,1,0:T(8,128)(2,1)S(1)}, bf16[1,512,128]{2,1,0:T(8,128)(2,1)S(1)}, u32[]{:S(2)}, u32[]{:S(2)}) collective-permute-start(bf16[1,512,128]{2,1,0:T(8,128)(2,1)S(1)} %add_convert_fusion.3), channel_id=1, source_target_pairs={{16,0},{20,4},{24,8},{28,12},{17,1},{21,5},{25,9},{29,13},{18,2},{... | collective-permute-start | bytes 393224 | tf_op jit(solution)/shard_map/terms_2/ppermute | solution.py:260
  80.3 0.8 fusion
  81.1 6.5 %collective-permute-done.17.rest_2_ = bf16[1,512,128]{2,1,0:T(8,128)(2,1)S(1)} collective-permute-done((bf16[1,512,128]{2,1,0:T(8,128)(2,1)S(1)}, bf16[1,512,128]{2,1,0:T(8,128)(2,1)S(1)}, u32[]{:S(2)}, u32[]{:S(2)}) %collective-permute-start.17) | collective-permute-done | bytes 131104 | tf_op jit(solution)/shard_map/terms_2/ppermute | solution.py:260
  87.6 0.6 copy-done.16
  88.2 2.7 %final.1 = (bf16[256,512]{1,0:T(8,128)(2,1)}, bf16[256,512]{1,0:T(8,128)(2,1)}) custom-call(s32[1]{0:T(128)} %bitcast.1.refs_1_.seq_ref, bf16[256,512]{1,0:T(8,128)(2,1)} %k_ref.5, bf16[256,512]{1,0:T(8,128)(2,1)} %v_ref.5, f32[256,512]{1,0:T(8,128)} %get-tuple-element.50.dk_in, f32[256,512]{1,0:T(8,128)} %get-tuple-element.51.dv_in, ...), custom_call_target="tpu_custom_call" | custom-call | flops 67108864 | bytes 2883588 | tf_op jit(solution)/shard_map/final/pallas_call | solution.py:35
  (45 shorter events, 0.2 us)
Async XLA Ops:
  0.6 9.6 %collective-permute-start.1 = (bf16[256,512]{1,0:T(8,128)(2,1)}, bf16[256,512]{1,0:T(8,128)(2,1)S(1)}, u32[]{:S(2)}, u32[]{:S(2)}) collective-permute-start(bf16[256,512]{1,0:T(8,128)(2,1)} %refs_2_.1), channel_id=1, source_target_pairs={{0,2},{1,3},{2,0},{3,1},{4,6},{5,7},{6,4},{7,5},{8,10},{9,11},{10,... | collective-permute-start | bytes 786440 | tf_op jit(solution)/shard_map/gather_2/ppermute | solution.py:254
  5.6 5.2 %collective-permute-start.3 = (bf16[512,128]{1,0:T(8,128)(2,1)}, bf16[512,128]{1,0:T(8,128)(2,1)S(1)}, u32[]{:S(2)}, u32[]{:S(2)}) collective-permute-start(bf16[512,128]{1,0:T(8,128)(2,1)} %state.1), channel_id=1, source_target_pairs={{0,4},{4,0},{8,12},{12,8},{16,20},{20,16},{24,28},{28,24},{1,5},{5... | collective-permute-start | bytes 393224 | tf_op jit(solution)/shard_map/state_0/ppermute | solution.py:254
  7.1 8.2 %collective-permute-start = (bf16[256,512]{1,0:T(8,128)(2,1)}, bf16[256,512]{1,0:T(8,128)(2,1)S(1)}, u32[]{:S(2)}, u32[]{:S(2)}) collective-permute-start(bf16[256,512]{1,0:T(8,128)(2,1)} %refs_2_.1), channel_id=1, source_target_pairs={{0,1},{1,0},{2,3},{3,2},{4,5},{5,4},{6,7},{7,6},{8,9},{9,8},{10,11... | collective-permute-start | bytes 786440 | tf_op jit(solution)/shard_map/gather_1/ppermute | solution.py:254
  10.2 5.1 %copy-start.11 = (bf16[256,512]{1,0:T(8,128)(2,1)}, bf16[256,512]{1,0:T(8,128)(2,1)S(1)}, u32[]{:S(2)}) copy-start(bf16[256,512]{1,0:T(8,128)(2,1)S(1)} %collective-permute-done.1.refs_4_) | copy-start | bytes 786436
  10.2 5.1 %collective-permute-start.2 = (bf16[256,512]{1,0:T(8,128)(2,1)S(1)}, bf16[256,512]{1,0:T(8,128)(2,1)S(1)}, u32[]{:S(2)}, u32[]{:S(2)}) collective-permute-start(bf16[256,512]{1,0:T(8,128)(2,1)S(1)} %collective-permute-done.1.refs_4_), channel_id=1, source_target_pairs={{0,1},{1,0},{2,3},{3,2},{4,5},{5,4},{6,7},{7,6},{8,9},{9,8},{10,11... | collective-permute-start | bytes 786440 | tf_op jit(solution)/shard_map/gather_3/ppermute | solution.py:254
  10.8 13.1 %copy-start.8 = (bf16[512,128]{1,0:T(8,128)(2,1)}, bf16[512,128]{1,0:T(8,128)(2,1)S(1)}, u32[]{:S(2)}) copy-start(bf16[512,128]{1,0:T(8,128)(2,1)S(1)} %collective-permute-done.3.rest_0_) | copy-start | bytes 393220
  11.8 12.1 %collective-permute-start.4 = (bf16[512,128]{1,0:T(8,128)(2,1)S(1)}, bf16[512,128]{1,0:T(8,128)(2,1)S(1)}, u32[]{:S(2)}, u32[]{:S(2)}) collective-permute-start(bf16[512,128]{1,0:T(8,128)(2,1)S(1)} %add_convert_fusion.5), channel_id=1, source_target_pairs={{0,8},{4,12},{8,0},{12,4},{16,24},{20,28},{24,16},{28,20},{1,9},{5... | collective-permute-start | bytes 393224 | tf_op jit(solution)/shard_map/state_1/ppermute | solution.py:254
  15.3 0.7 copy-start.12
  15.3 0.8 copy-start.13
  20.4 21.5 %collective-permute-start.8 = (bf16[256,512]{1,0:T(8,128)(2,1)}, bf16[256,512]{1,0:T(8,128)(2,1)S(1)}, u32[]{:S(2)}, u32[]{:S(2)}) collective-permute-start(bf16[256,512]{1,0:T(8,128)(2,1)} %get-tuple-element.44), channel_id=1, source_target_pairs={{0,4},{4,0},{8,12},{12,8},{16,20},{20,16},{24,28},{28,24},{1,5},{5... | collective-permute-start | bytes 786440 | tf_op jit(solution)/shard_map/rows_1/ppermute | solution.py:254
  21.9 21.6 %collective-permute-start.9 = (bf16[256,512]{1,0:T(8,128)(2,1)}, bf16[256,512]{1,0:T(8,128)(2,1)S(1)}, u32[]{:S(2)}, u32[]{:S(2)}) collective-permute-start(bf16[256,512]{1,0:T(8,128)(2,1)} %get-tuple-element.45), channel_id=1, source_target_pairs={{0,8},{4,12},{8,0},{12,4},{16,24},{20,28},{24,16},{28,20},{1,9},{5... | collective-permute-start | bytes 786440 | tf_op jit(solution)/shard_map/rows_2/ppermute | solution.py:254
  22.3 25.9 %collective-permute-start.10 = (bf16[256,512]{1,0:T(8,128)(2,1)}, bf16[256,512]{1,0:T(8,128)(2,1)S(1)}, u32[]{:S(2)}, u32[]{:S(2)}) collective-permute-start(bf16[256,512]{1,0:T(8,128)(2,1)} %get-tuple-element.46), channel_id=1, source_target_pairs={{0,12},{4,8},{8,4},{12,0},{16,28},{20,24},{24,20},{28,16},{1,13},{... | collective-permute-start | bytes 786440 | tf_op jit(solution)/shard_map/rows_3/ppermute | solution.py:254
  23.9 10.6 %copy-start.9 = (bf16[512,128]{1,0:T(8,128)(2,1)}, bf16[512,128]{1,0:T(8,128)(2,1)S(1)}, u32[]{:S(2)}) copy-start(bf16[512,128]{1,0:T(8,128)(2,1)S(1)} %collective-permute-done.4.rest_1_) | copy-start | bytes 393220
  23.9 13.9 %collective-permute-start.5 = (bf16[512,128]{1,0:T(8,128)(2,1)S(1)}, bf16[512,128]{1,0:T(8,128)(2,1)S(1)}, u32[]{:S(2)}, u32[]{:S(2)}) collective-permute-start(bf16[512,128]{1,0:T(8,128)(2,1)S(1)} %add_convert_fusion.4), channel_id=1, source_target_pairs={{0,16},{4,20},{8,24},{12,28},{1,17},{5,21},{9,25},{13,29},{2,18},{... | collective-permute-start | bytes 393224 | tf_op jit(solution)/shard_map/state_2/ppermute | solution.py:260
  28.4 41.4 %collective-permute-start.15 = (bf16[3,512,128]{2,1,0:T(8,128)(2,1)}, bf16[3,512,128]{2,1,0:T(8,128)(2,1)S(1)}, u32[]{:S(2)}, u32[]{:S(2)}) collective-permute-start(bf16[3,512,128]{2,1,0:T(8,128)(2,1)} %get-tuple-element.52), channel_id=1, source_target_pairs={{0,4},{4,0},{8,12},{12,8},{16,20},{20,16},{24,28},{28,24},{1,5},{5... | collective-permute-start | bytes 1179656 | tf_op jit(solution)/shard_map/terms_0/ppermute | solution.py:254
  37.8 0.7 copy-start.15
  41.5 10.6 %collective-permute-start.13 = (bf16[272,512]{1,0:T(8,128)(2,1)}, bf16[272,512]{1,0:T(8,128)(2,1)S(1)}, u32[]{:S(2)}, u32[]{:S(2)}) collective-permute-start(bf16[272,512]{1,0:T(8,128)(2,1)} %get-tuple-element.40.attn_ref.refs_4_), channel_id=1, source_target_pairs={{0,12},{4,8},{8,4},{12,0},{16,28},{20,24},{24,20},{28,16},{1,13},{... | collective-permute-start | bytes 835592 | tf_op jit(solution)/shard_map/attn_3/ppermute | solution.py:254
  41.9 13.7 %copy-start.4 = (bf16[256,512]{1,0:T(8,128)(2,1)}, bf16[256,512]{1,0:T(8,128)(2,1)S(1)}, u32[]{:S(2)}) copy-start(bf16[256,512]{1,0:T(8,128)(2,1)S(1)} %collective-permute-done.8.refs_1_) | copy-start | bytes 786436
  41.9 12.8 %collective-permute-start.12 = (bf16[272,512]{1,0:T(8,128)(2,1)}, bf16[272,512]{1,0:T(8,128)(2,1)S(1)}, u32[]{:S(2)}, u32[]{:S(2)}) collective-permute-start(bf16[272,512]{1,0:T(8,128)(2,1)} %get-tuple-element.40.attn_ref.refs_4_), channel_id=1, source_target_pairs={{0,8},{4,12},{8,0},{12,4},{16,24},{20,28},{24,16},{28,20},{1,9},{5... | collective-permute-start | bytes 835592 | tf_op jit(solution)/shard_map/attn_2/ppermute | solution.py:254
  43.5 12.1 %copy-start.5 = (bf16[256,512]{1,0:T(8,128)(2,1)}, bf16[256,512]{1,0:T(8,128)(2,1)S(1)}, u32[]{:S(2)}) copy-start(bf16[256,512]{1,0:T(8,128)(2,1)S(1)} %collective-permute-done.9.refs_2_) | copy-start | bytes 786436
  43.5 12.1 %collective-permute-start.11 = (bf16[272,512]{1,0:T(8,128)(2,1)}, bf16[272,512]{1,0:T(8,128)(2,1)S(1)}, u32[]{:S(2)}, u32[]{:S(2)}) collective-permute-start(bf16[272,512]{1,0:T(8,128)(2,1)} %get-tuple-element.40.attn_ref.refs_4_), channel_id=1, source_target_pairs={{0,4},{4,0},{8,12},{12,8},{16,20},{20,16},{24,28},{28,24},{1,5},{5... | collective-permute-start | bytes 835592 | tf_op jit(solution)/shard_map/attn_1/ppermute | solution.py:254
  48.2 7.4 %copy-start.6 = (bf16[256,512]{1,0:T(8,128)(2,1)}, bf16[256,512]{1,0:T(8,128)(2,1)S(1)}, u32[]{:S(2)}) copy-start(bf16[256,512]{1,0:T(8,128)(2,1)S(1)} %collective-permute-done.10.refs_3_) | copy-start | bytes 786436
  48.2 21.8 %collective-permute-start.6 = (bf16[2,256,512]{2,1,0:T(8,128)(2,1)}, bf16[2,256,512]{2,1,0:T(8,128)(2,1)S(1)}, u32[]{:S(2)}, u32[]{:S(2)}) collective-permute-start(bf16[2,256,512]{2,1,0:T(8,128)(2,1)} %get-tuple-element.42), channel_id=1, source_target_pairs={{0,1},{1,0},{2,3},{3,2},{4,5},{5,4},{6,7},{7,6},{8,9},{9,8},{10,11... | collective-permute-start | bytes 1572872 | tf_op jit(solution)/shard_map/mixed_0/ppermute | solution.py:254
  52.1 3.5 %copy-start = (bf16[272,512]{1,0:T(8,128)(2,1)}, bf16[272,512]{1,0:T(8,128)(2,1)S(1)}, u32[]{:S(2)}) copy-start(bf16[272,512]{1,0:T(8,128)(2,1)S(1)} %collective-permute-done.13.refs_7_) | copy-start | bytes 835588
  54.7 0.9 %copy-start.1 = (bf16[272,512]{1,0:T(8,128)(2,1)}, bf16[272,512]{1,0:T(8,128)(2,1)S(1)}, u32[]{:S(2)}) copy-start(bf16[272,512]{1,0:T(8,128)(2,1)S(1)} %collective-permute-done.12.refs_6_) | copy-start | bytes 835588
  55.6 0.7 copy-start.2
  56.3 13.5 %copy-start.14 = (bf16[3,512,128]{2,1,0:T(8,128)(2,1)S(1)}, bf16[3,512,128]{2,1,0:T(8,128)(2,1)}, u32[]{:S(2)}) copy-start(bf16[3,512,128]{2,1,0:T(8,128)(2,1)} %get-tuple-element.52) | copy-start | bytes 1179652
  56.3 13.7 %copy-start.10 = (bf16[2,256,512]{2,1,0:T(8,128)(2,1)S(1)}, bf16[2,256,512]{2,1,0:T(8,128)(2,1)}, u32[]{:S(2)}) copy-start(bf16[2,256,512]{2,1,0:T(8,128)(2,1)} %get-tuple-element.41) | copy-start | bytes 1572868
  59.1 10.0 %copy-start.17 = (f32[16,4]{1,0:T(8,128)S(1)}, f32[16,4]{1,0:T(8,128)}, u32[]{:S(2)}) copy-start(f32[16,4]{1,0:T(8,128)} %get-tuple-element.55) | copy-start | bytes 772
  59.1 10.0 %collective-permute-start.18 = (f32[16,4]{1,0:T(8,128)}, f32[16,4]{1,0:T(8,128)S(1)}, u32[]{:S(2)}, u32[]{:S(2)}) collective-permute-start(f32[16,4]{1,0:T(8,128)} %get-tuple-element.55), channel_id=1, source_target_pairs={{0,16},{4,20},{8,24},{12,28},{16,0},{20,4},{24,8},{28,12},{1,17},{... | collective-permute-start | bytes 776 | tf_op jit(solution)/shard_map/table_2/ppermute | solution.py:254
  61.0 13.8 %collective-permute-start.14 = (bf16[1,256,512]{2,1,0:T(8,128)(2,1)}, bf16[1,256,512]{2,1,0:T(8,128)(2,1)S(1)}, u32[]{:S(2)}, u32[]{:S(2)}) collective-permute-start(bf16[1,256,512]{2,1,0:T(8,128)(2,1)} %get-tuple-element.48), channel_id=1, source_target_pairs={{0,16},{4,20},{8,24},{12,28},{16,0},{20,4},{24,8},{28,12},{1,17},{... | collective-permute-start | bytes 786440 | tf_op jit(solution)/shard_map/weight_0/ppermute | solution.py:254
  69.8 11.3 %copy-start.3 = (bf16[3,512,128]{2,1,0:T(8,128)(2,1)}, bf16[3,512,128]{2,1,0:T(8,128)(2,1)S(1)}, u32[]{:S(2)}) copy-start(bf16[3,512,128]{2,1,0:T(8,128)(2,1)S(1)} %collective-permute-done.15.rest_0_) | copy-start | bytes 1179652
  69.9 9.0 %collective-permute-start.16 = (bf16[2,512,128]{2,1,0:T(8,128)(2,1)S(1)}, bf16[2,512,128]{2,1,0:T(8,128)(2,1)S(1)}, u32[]{:S(2)}, u32[]{:S(2)}) collective-permute-start(bf16[2,512,128]{2,1,0:T(8,128)(2,1)S(1)} %add_convert_fusion), channel_id=1, source_target_pairs={{0,8},{4,12},{8,0},{12,4},{16,24},{20,28},{24,16},{28,20},{1,9},{5... | collective-permute-start | bytes 786440 | tf_op jit(solution)/shard_map/terms_1/ppermute | solution.py:254
  70.0 10.2 %collective-permute-start.7 = (bf16[1,256,512]{2,1,0:T(8,128)(2,1)S(1)}, bf16[1,256,512]{2,1,0:T(8,128)(2,1)S(1)}, u32[]{:S(2)}, u32[]{:S(2)}) collective-permute-start(bf16[1,256,512]{2,1,0:T(8,128)(2,1)S(1)} %add_convert_fusion.2), channel_id=1, source_target_pairs={{0,2},{1,3},{2,0},{3,1},{4,6},{5,7},{6,4},{7,5},{8,10},{9,11},{10,... | collective-permute-start | bytes 786440 | tf_op jit(solution)/shard_map/mixed_1/ppermute | solution.py:254
  78.9 8.6 %copy-start.7 = (bf16[2,512,128]{2,1,0:T(8,128)(2,1)}, bf16[2,512,128]{2,1,0:T(8,128)(2,1)S(1)}, u32[]{:S(2)}) copy-start(bf16[2,512,128]{2,1,0:T(8,128)(2,1)S(1)} %collective-permute-done.16.rest_1_) | copy-start | bytes 786436
  79.0 8.6 %collective-permute-start.17 = (bf16[1,512,128]{2,1,0:T(8,128)(2,1)S(1)}, bf16[1,512,128]{2,1,0:T(8,128)(2,1)S(1)}, u32[]{:S(2)}, u32[]{:S(2)}) collective-permute-start(bf16[1,512,128]{2,1,0:T(8,128)(2,1)S(1)} %add_convert_fusion.3), channel_id=1, source_target_pairs={{16,0},{20,4},{24,8},{28,12},{17,1},{21,5},{25,9},{29,13},{18,2},{... | collective-permute-start | bytes 393224 | tf_op jit(solution)/shard_map/terms_2/ppermute | solution.py:260
  87.5 0.7 copy-start.16

commit v3 on v2

v3 whole, which is shorter than its diff:
```python
import functools
import math

import jax
import jax.numpy as jnp
from jax import lax
from jax.experimental import pallas as pl
from jax.experimental.pallas import tpu as pltpu
from jax.sharding import PartitionSpec as P


SPAN = 64
F32 = jnp.float32
BF16 = jnp.bfloat16

VMEM_SPEC = pl.BlockSpec(memory_space=pltpu.VMEM)
SMEM_SPEC = pl.BlockSpec(memory_space=pltpu.SMEM)


def nn(left, right):
    return lax.dot_general(left, right, (((1,), (0,)), ((), ())), preferred_element_type=F32)


def nt(left, right):
    return lax.dot_general(left, right, (((1,), (1,)), ((), ())), preferred_element_type=F32)


def tn(left, right):
    return lax.dot_general(left, right, (((0,), (0,)), ((), ())), preferred_element_type=F32)


def local_call(body, outs, ins, scalars=0, flops=0, scratch=()):
    moved = sum(math.prod(o.shape) * o.dtype.itemsize for o in outs)
    moved += sum(math.prod(a.shape) * a.dtype.itemsize for a in ins)
    return pl.pallas_call(
        body,
        out_shape=tuple(outs),
        in_specs=[SMEM_SPEC] * scalars + [VMEM_SPEC] * (len(ins) - scalars),
        out_specs=tuple(VMEM_SPEC for _ in outs),
        scratch_shapes=scratch,
        cost_estimate=pl.CostEstimate(flops=flops, bytes_accessed=moved, transcendentals=0),
    )(*ins)


def shaped(shape, dtype):
    return jax.ShapeDtypeStruct(shape, dtype)


def state_body(heads, k_ref, v_ref, d_ref):
    size = k_ref.shape[1] // heads
    for h in range(heads):
        cols = slice(h * size, (h + 1) * size)
        d_ref[h * size : (h + 1) * size, :] = tn(k_ref[:, cols], v_ref[:, cols]).astype(BF16)


def level_masks(tokens, local_levels):
    row = lax.broadcasted_iota(jnp.int32, (tokens, tokens), 0)
    col = lax.broadcasted_iota(jnp.int32, (tokens, tokens), 1)
    apart = (row // SPAN) ^ (col // SPAN)
    causal = col <= row
    masks = [causal & (apart == 0)]
    for l in range(1, local_levels):
        masks.append(causal & ((apart >> (l - 1)) == 1))
    return masks


def level_weight(masks, coef_ref, heads, h):
    weight = jnp.zeros(masks[0].shape, F32)
    for l, mask in enumerate(masks):
        weight = jnp.where(mask, coef_ref[:, l * heads + h : l * heads + h + 1], weight)
    return weight


def inner_body(local_levels, scales, q_ref, k_ref, v_ref, code_ref, table_ref, attn_ref, coef_ref, hot_ref):
    heads, codes = table_ref.shape
    table = table_ref[...]
    high = table.astype(BF16)
    low = (table - high.astype(F32)).astype(BF16)
    tokens = code_ref.shape[1]
    size = q_ref.shape[1] // heads
    row = lax.broadcasted_iota(jnp.int32, (codes, tokens), 0)
    for l in range(len(scales)):
        hot = jnp.where(row == code_ref[l : l + 1, :], 1.0, 0.0).astype(BF16)
        hot_ref[l * codes : (l + 1) * codes, :] = hot
        lam = lax.dot_general(hot, high, (((0,), (1,)), ((), ())), preferred_element_type=F32)
        lam = lam + lax.dot_general(hot, low, (((0,), (1,)), ((), ())), preferred_element_type=F32)
        coef_ref[:, l * heads : (l + 1) * heads] = lam * scales[l]
    masks = level_masks(tokens, local_levels)
    for h in range(heads):
        cols = slice(h * size, (h + 1) * size)
        scores = nt(q_ref[:, cols], k_ref[:, cols]) * level_weight(masks, coef_ref, heads, h)
        attn_ref[:, cols] = nn(scores.astype(BF16), v_ref[:, cols])


def grad_body(heads, local_levels, levels, count, group, rows, *refs):
    head_ref, seq_ref = refs[:2]
    blocks = refs[2 : 2 + count]
    w_ref, q_ref, coef_ref, g_ref, t_ref = refs[2 + count : 7 + count]
    picked = refs[7 + count : -1]
    full_ref = refs[-1]
    me = head_ref[0]
    width = blocks[0].shape[1]
    size = q_ref.shape[1] // heads
    total = None
    for m in range(count):
        start = pl.multiple_of((me ^ m) * width, width)
        block = blocks[m][...]
        full_ref[:, pl.ds(start, width)] = block
        part = nt(block, w_ref[:, pl.ds(start, width)])
        total = part if total is None else total + part
    g = total.astype(BF16)
    g_ref[...] = g
    for l in range(local_levels, levels):
        for h in range(heads):
            cols = slice(h * size, (h + 1) * size)
            scaled = (g[:, cols].astype(F32) * coef_ref[:, l * heads + h : l * heads + h + 1]).astype(BF16)
            t_ref[l - local_levels, h * size : (h + 1) * size, :] = tn(q_ref[:, cols], scaled).astype(BF16)
    if len(picked) == 1:
        picked[0][...] = full_ref[...]
        return
    low = seq_ref[0] & (group - 1)
    for m in range(group):
        for n in range(picked[m].shape[1] // rows):
            start = pl.multiple_of((n * group + (low ^ m)) * rows, rows)
            picked[m][:, n * rows : (n + 1) * rows] = full_ref[:, pl.ds(start, rows)]


def outer_body(heads, local_levels, seq_ref, q_ref, coef_ref, attn_in, *rest):
    states, attn_ref = rest[:-1], rest[-1]
    me = seq_ref[0]
    size = q_ref.shape[1] // heads
    for h in range(heads):
        cols = slice(h * size, (h + 1) * size)
        q = q_ref[:, cols]
        attn = attn_in[:, cols]
        for b, state_ref in enumerate(states):
            owned = ((me >> b) & 1).astype(F32)
            place = (local_levels + b) * heads + h
            state = state_ref[h * size : (h + 1) * size, :]
            attn = attn + coef_ref[:, place : place + 1] * owned * nn(q, state)
        attn_ref[:, cols] = attn.astype(BF16)


def back_body(heads, local_levels, scales, norm, seq_ref, q_ref, k_ref, v_ref, g_ref, coef_ref, hot_ref, *rest):
    states = rest[: len(scales) - local_levels]
    dq_ref, dk_ref, dv_ref, table_ref = rest[len(scales) - local_levels :]
    me = seq_ref[0]
    tokens = q_ref.shape[0]
    size = q_ref.shape[1] // heads
    codes = table_ref.shape[0]
    masks = level_masks(tokens, local_levels)
    lanes = 128 * pl.cdiv(len(scales) * heads, 128)
    lane = lax.broadcasted_iota(jnp.int32, (tokens, lanes), 1)
    lev = jnp.zeros((tokens, lanes), F32)
    for h in range(heads):
        cols = slice(h * size, (h + 1) * size)
        q, k, v, g = q_ref[:, cols], k_ref[:, cols], v_ref[:, cols], g_ref[:, cols]
        weight = level_weight(masks, coef_ref, heads, h)
        scores = nt(q, k)
        grads = nt(g, v)
        both = scores * grads
        for l in range(local_levels):
            part = jnp.sum(jnp.where(masks[l], both, 0.0), axis=1, keepdims=True) * scales[l]
            lev = jnp.where(lane == l * heads + h, part, lev)
        scores = (scores * weight).astype(BF16)
        grads = (grads * weight).astype(BF16)
        dk_ref[:, cols] = tn(grads, q)
        dv_ref[:, cols] = tn(scores, g)
        dq = nn(grads, k)
        qf = q.astype(F32)
        for b, state_ref in enumerate(states):
            owned = ((me >> b) & 1).astype(F32)
            place = (local_levels + b) * heads + h
            back = nt(g, state_ref[h * size : (h + 1) * size, :])
            dq = dq + coef_ref[:, place : place + 1] * owned * back
            part = jnp.sum(qf * back, axis=1, keepdims=True) * (owned * scales[local_levels + b])
            lev = jnp.where(lane == place, part, lev)
        dq_ref[:, cols] = dq.astype(BF16)
    high = lev.astype(BF16)
    low = (lev - high.astype(F32)).astype(BF16)
    total = jnp.zeros((codes, heads), F32)
    for l in range(len(scales)):
        hot = hot_ref[l * codes : (l + 1) * codes, :]
        pick = slice(l * heads, (l + 1) * heads)
        total = total + nn(hot, high[:, pick]) + nn(hot, low[:, pick])
    table_ref[...] = total * norm


def weight_body(masks, scale, group_bits, seq_ref, *refs):
    count = 1 << group_bits
    picked, attns, out_ref = refs[:count], refs[count : 2 * count], refs[2 * count]
    scratch = refs[2 * count + 1 :]
    me = seq_ref[0] >> group_bits
    rows = out_ref.shape[1]

    def product(cols):
        total = None
        for m in range(count):
            part = tn(picked[m][:, cols], attns[m][...])
            total = part if total is None else total + part
        return total * scale

    if scratch:
        scratch[0][...] = product(slice(None))
    for n, m in enumerate(masks):
        start = pl.multiple_of((me ^ m) * rows, rows)
        total = scratch[0][pl.ds(start, rows), :] if scratch else product(pl.ds(start, rows))
        out_ref[n] = total.astype(out_ref.dtype)


def mixed_body(masks, head_ref, attn_ref, w_ref, send_ref, keep_ref):
    me = head_ref[0]
    width = send_ref.shape[2]
    attn = attn_ref[...]
    half = len(masks) // 2
    for n, m in enumerate(masks[half:] + masks[:half]):
        start = pl.multiple_of((me ^ m) * width, width)
        out_ref = send_ref if n < half else keep_ref
        out_ref[n % half] = nn(attn, w_ref[:, pl.ds(start, width)]).astype(BF16)


def final_body(heads, count, seq_ref, k_ref, v_ref, dk_in, dv_in, *rest):
    terms = rest[:count]
    dk_ref, dv_ref = rest[count:]
    me = seq_ref[0]
    size = k_ref.shape[1] // heads
    for h in range(heads):
        cols = slice(h * size, (h + 1) * size)
        u = jnp.zeros((size, size), F32)
        for b in range(count):
            owned = (1 - ((me >> b) & 1)).astype(F32)
            u = u + owned * terms[b][0, h * size : (h + 1) * size, :].astype(F32)
        u = u.astype(BF16)
        dk_ref[:, cols] = (dk_in[:, cols] + nt(v_ref[:, cols], u)).astype(BF16)
        dv_ref[:, cols] = (dv_in[:, cols] + nn(k_ref[:, cols], u)).astype(BF16)


def swap(value, axis, mask):
    pairs = [(i, i ^ mask) for i in range(lax.axis_size(axis))]
    return lax.ppermute(value, axis, pairs)


def one_way(value, axis, mask, up):
    n = lax.axis_size(axis)
    pairs = [(i, i ^ mask) for i in range(n) if (i & mask == 0) == up]
    return lax.ppermute(value, axis, pairs)


def reduce_blocks(send, keep, axis, bits):
    parts = [keep]
    for n, bit in enumerate(bits):
        if n > 0:
            half = parts[0].shape[0] // 2
            send = sum(part[half:].astype(F32) for part in parts).astype(BF16)
            parts = [part[:half] for part in parts]
        parts.append(swap(send, axis, 1 << bit))
    return sum(part[0].astype(F32) for part in parts)


def bit_order(bits):
    masks = [0]
    for bit in reversed(range(bits)):
        masks = masks + [m | (1 << bit) for m in masks]
    return masks


def per_device(queries, keys, values, level_table, level_code, out_weight, cotangent):
    tokens, cols = queries.shape
    heads = level_table.shape[1]
    codes = level_table.shape[0]
    size = cols // heads
    width = out_weight.shape[1]
    spans = tokens // SPAN
    local_bits = spans.bit_length() - 1
    seq_count = lax.axis_size("seq")
    seq_bits = seq_count.bit_length() - 1
    head_count = lax.axis_size("head")
    head_bits = head_count.bit_length() - 1
    local_levels = 1 + local_bits
    levels = local_levels + seq_bits
    group_bits = min(2, seq_bits - 1)
    group = 1 << group_bits
    high_bits = seq_bits - group_bits
    rows = width // seq_count
    scales = [1.0 / math.sqrt(SPAN * 2 ** max(l - 1, 0)) for l in range(levels)]
    seq_me = lax.axis_index("seq").astype(jnp.int32)
    head_me = lax.axis_index("head").astype(jnp.int32)
    seq_one = seq_me.reshape(1)
    head_one = head_me.reshape(1)

    blocks = {0: cotangent}
    for bit in reversed(range(head_bits)):
        for m in list(blocks):
            blocks[m | (1 << bit)] = swap(blocks[m], "head", 1 << bit)

    (state,) = local_call(
        functools.partial(state_body, heads),
        [shaped((cols, size), BF16)],
        [keys, values],
        flops=2 * tokens * cols * size,
    )
    attn_in, coef, hot = local_call(
        functools.partial(inner_body, local_levels, scales),
        [
            shaped((tokens, cols), F32),
            shaped((tokens, levels * heads), F32),
            shaped((levels * codes, tokens), BF16),
        ],
        [queries, keys, values, level_code.T, level_table.T],
        flops=4 * tokens * tokens * cols,
    )
    found = []
    block_state = state
    for bit in range(seq_bits):
        if bit == seq_bits - 1:
            found.append(one_way(block_state, "seq", 1 << bit, True))
        else:
            got = swap(block_state, "seq", 1 << bit)
            found.append(got)
        if bit < seq_bits - 1:
            block_state = (block_state.astype(F32) + got.astype(F32)).astype(BF16)

    aligned = rows % 128 == 0
    kept = [shaped((tokens, width // group), BF16)] * group if aligned else [shaped((tokens, width), BF16)]
    g, terms, *picked = local_call(
        functools.partial(grad_body, heads, local_levels, levels, head_count, group, rows),
        [shaped((tokens, cols), BF16), shaped((seq_bits, cols, size), BF16)] + kept,
        [head_one, seq_one] + [blocks[m] for m in range(head_count)] + [out_weight, queries, coef],
        scalars=2,
        flops=2 * tokens * cols * width,
        scratch=[pltpu.VMEM((tokens, width), BF16)],
    )
    if not aligned:
        split = picked[0].reshape(tokens, seq_count // group, group, rows)
        picked = [
            lax.dynamic_index_in_dim(split, (seq_me & (group - 1)) ^ m, 2, False).reshape(tokens, width // group)
            for m in range(group)
        ]
    term_parts = []
    for bit in range(seq_bits):
        if bit == seq_bits - 1:
            got = one_way(terms, "seq", 1 << bit, False)
        else:
            got = swap(terms, "seq", 1 << bit)
        term_parts.append(got)
        if bit < seq_bits - 1:
            terms = (terms[1:].astype(F32) + got[1:].astype(F32)).astype(BF16)
    for m in range(1, group):
        picked[m] = swap(picked[m], "seq", m)

    (attn,) = local_call(
        functools.partial(outer_body, heads, local_levels),
        [shaped((tokens, cols), BF16)],
        [seq_one, queries, coef, attn_in] + found,
        scalars=1,
        flops=2 * tokens * cols * size * seq_bits,
    )
    table_norm = 1.0 / math.sqrt(tokens * seq_count * levels)
    query_grad, dk_in, dv_in, table_grad = local_call(
        functools.partial(back_body, heads, local_levels, scales, table_norm),
        [shaped((tokens, cols), BF16)] + [shaped((tokens, cols), F32)] * 2 + [shaped((codes, heads), F32)],
        [seq_one, queries, keys, values, g, coef, hot] + found,
        scalars=1,
        flops=10 * tokens * tokens * cols,
    )
    for bit in range(seq_bits):
        table_grad = table_grad + swap(table_grad, "seq", 1 << bit)
    attns = [attn]
    for m in range(1, group):
        attns.append(swap(attn, "seq", m))

    masks_m = bit_order(head_bits)
    send_shape = shaped((head_count // 2, tokens, width // head_count), BF16)
    send, keep = local_call(
        functools.partial(mixed_body, masks_m),
        [send_shape, send_shape],
        [head_one, attn, out_weight],
        scalars=1,
        flops=2 * tokens * cols * width,
    )
    mixed = reduce_blocks(send, keep, "head", range(head_bits)).astype(BF16)

    weight_norm = 1.0 / math.sqrt(tokens * seq_count)
    masks_w = bit_order(high_bits)
    half = len(masks_w) // 2

    def weight_part(masks, dtype):
        return local_call(
            functools.partial(weight_body, masks, weight_norm, group_bits),
            [shaped((half, rows, cols), dtype)],
            [seq_one] + picked + attns,
            scalars=1,
            flops=tokens * cols * width,
            scratch=[] if aligned else [pltpu.VMEM((width // group, cols), F32)],
        )

    (weight_send,) = weight_part(masks_w[half:], BF16)
    (weight_keep,) = weight_part(masks_w[:half], F32)
    out_weight_grad = reduce_blocks(weight_send, weight_keep, "seq", range(group_bits, seq_bits))

    key_grad, value_grad = local_call(
        functools.partial(final_body, heads, seq_bits),
        [shaped((tokens, cols), BF16)] * 2,
        [seq_one, keys, values, dk_in, dv_in] + term_parts,
        scalars=1,
        flops=4 * tokens * cols * size,
    )
    return mixed, out_weight_grad, query_grad, key_grad, value_grad, table_grad


def solution(mesh):
    placed = (
        P("seq", "head"),
        P("seq", "head"),
        P("seq", "head"),
        P(None, "head"),
        P("seq", None),
        P("head", None),
        P("seq", "head"),
    )

    return jax.shard_map(
        per_device,
        mesh=mesh,
        in_specs=placed,
        out_specs=(
            P("seq", "head"),
            P("seq", "head"),
            P("seq", "head"),
            P("seq", "head"),
            P("seq", "head"),
            P(None, "head"),
        ),
        check_vma=False,
    )
```

time: 91.4 us -> 101 us (1.11)
  starting transfers between devices: 23.6 us -> 28.6 us
  waiting for transfers between devices: 28.7 us -> 33.5 us
  Pallas kernels: 30.4 us -> 29.3 us
    ppermute x17 -> x19, waiting for transfers between devices: 22.3 us -> 27.9 us  [swap(): return lax.ppermute(value, axis, pairs)]
    ppermute x17 -> x19, starting transfers between devices: 17.8 us -> 22.6 us  [swap(): return lax.ppermute(value, axis, pairs)]
    pallas_call x10 -> x9, Pallas kernels: 30.4 us -> 29.3 us  [local_call(): pl.pallas_call(body, out_shape=tuple(outs), in_specs=[SMEM_SPEC] * scalar...]
    unnamed x37 -> x35, local copies, waits for them, and re-layouts: 3.44 us -> 3.43 us
  transfers between devices with their start and end apart: 19 -> 21, of which waited for: 9 -> 10; matrix products, arithmetic and copies ran while one was open for 5% -> 4% of each run, Pallas kernels for 30% -> 25%
where the time goes in v3:
time: 101 us; the launch traced here: 100 us
  waiting for transfers between devices  33.5 us (33%)
  Pallas kernels  29.3 us (29%)
  starting transfers between devices  28.6 us (28%)
  other arithmetic  4.62 us (5%)
  local copies, waits for them, and re-layouts  3.43 us (3%)
    pallas_call x9, Pallas kernels, local_call(): pl.pallas_call(body, out_shape=tuple(outs), in_specs=[SMEM_SPEC] * scalar...  29.3 us
    ppermute x19, waiting for transfers between devices, swap(): return lax.ppermute(value, axis, pairs)  27.9 us
    ppermute x19, starting transfers between devices, swap(): return lax.ppermute(value, axis, pairs)  22.6 us
    ppermute x2, starting transfers between devices, one_way(): return lax.ppermute(value, axis, pairs)  6.04 us
    ppermute x2, waiting for transfers between devices, one_way(): return lax.ppermute(value, axis, pairs)  5.65 us
    unnamed x35, local copies, waits for them, and re-layouts  3.43 us
  transfers between devices with their start and end apart: 21, of which 10 were waited for; matrix products, arithmetic and copies ran while one was open for 4% of the time, Pallas kernels for 25%

profile of v3, /device:TPU:0, one launch (start us, length us, event | category | flops | bytes accessed | tf_op | source)
XLA Modules:
  0.0 100.3 jit_solution(5452360891190962995)
XLA Ops:
  0.6 2.0 %shard_map.119 = bf16[512,128]{1,0:T(8,128)(2,1)} custom-call(bf16[256,512]{1,0:T(8,128)(2,1)} %k_ref.7, bf16[256,512]{1,0:T(8,128)(2,1)} %v_ref.7), custom_call_target="tpu_custom_call" | custom-call | flops 33554432 | bytes 655360 | tf_op jit(solution)/shard_map/pallas_call | solution.py:35
  2.6 3.0 %collective-permute-start = (bf16[512,128]{1,0:T(8,128)(2,1)}, bf16[512,128]{1,0:T(8,128)(2,1)S(1)}, u32[]{:S(2)}, u32[]{:S(2)}) collective-permute-start(bf16[512,128]{1,0:T(8,128)(2,1)} %shard_map.119), channel_id=1, source_target_pairs={{0,4},{4,0},{8,12},{12,8},{16,20},{20,16},{24,28},{28,24},{1,5},{5... | collective-permute-start | bytes 393224 | tf_op jit(solution)/shard_map/ppermute | solution.py:240
  5.6 3.7 %collective-permute-done.rest_0_ = bf16[512,128]{1,0:T(8,128)(2,1)S(1)} collective-permute-done((bf16[512,128]{1,0:T(8,128)(2,1)}, bf16[512,128]{1,0:T(8,128)(2,1)S(1)}, u32[]{:S(2)}, u32[]{:S(2)}) %collective-permute-start) | collective-permute-done | bytes 131104 | tf_op jit(solution)/shard_map/ppermute | solution.py:240
  9.3 1.0 add_convert_fusion.5
  10.3 1.9 %collective-permute-start.1 = (bf16[512,128]{1,0:T(8,128)(2,1)S(1)}, bf16[512,128]{1,0:T(8,128)(2,1)S(1)}, u32[]{:S(2)}, u32[]{:S(2)}) collective-permute-start(bf16[512,128]{1,0:T(8,128)(2,1)S(1)} %add_convert_fusion.5), channel_id=1, source_target_pairs={{0,8},{4,12},{8,0},{12,4},{16,24},{20,28},{24,16},{28,20},{1,9},{5... | collective-permute-start | bytes 393224 | tf_op jit(solution)/shard_map/ppermute | solution.py:240
  12.1 1.5 %collective-permute-start.6 = (bf16[256,512]{1,0:T(8,128)(2,1)}, bf16[256,512]{1,0:T(8,128)(2,1)S(1)}, u32[]{:S(2)}, u32[]{:S(2)}) collective-permute-start(bf16[256,512]{1,0:T(8,128)(2,1)} %refs_2_.1), channel_id=1, source_target_pairs={{0,2},{1,3},{2,0},{3,1},{4,6},{5,7},{6,4},{7,5},{8,10},{9,11},{10,... | collective-permute-start | bytes 786440 | tf_op jit(solution)/shard_map/ppermute | solution.py:240
  13.7 1.6 %collective-permute-done.1.rest_1_ = bf16[512,128]{1,0:T(8,128)(2,1)S(1)} collective-permute-done((bf16[512,128]{1,0:T(8,128)(2,1)S(1)}, bf16[512,128]{1,0:T(8,128)(2,1)S(1)}, u32[]{:S(2)}, u32[]{:S(2)}) %collective-permute-start.1) | collective-permute-done | bytes 131104 | tf_op jit(solution)/shard_map/ppermute | solution.py:240
  15.3 4.8 %collective-permute-start.2 = (bf16[512,128]{1,0:T(8,128)(2,1)S(1)}, bf16[512,128]{1,0:T(8,128)(2,1)S(1)}, u32[]{:S(2)}, u32[]{:S(2)}) collective-permute-start(bf16[512,128]{1,0:T(8,128)(2,1)S(1)} %add_convert_fusion.4), channel_id=1, source_target_pairs={{0,16},{4,20},{8,24},{12,28},{1,17},{5,21},{9,25},{13,29},{2,18},{... | collective-permute-start | bytes 393224 | tf_op jit(solution)/shard_map/ppermute | solution.py:246
  20.2 0.5 collective-permute-start.7
  20.7 3.1 %shard_map.118 = (f32[256,512]{1,0:T(8,128)}, f32[256,24]{1,0:T(8,128)}, bf16[96,256]{1,0:T(8,128)(2,1)}) custom-call(bf16[256,512]{1,0:T(8,128)(2,1)} %q_ref.5, bf16[256,512]{1,0:T(8,128)(2,1)} %k_ref.7, bf16[256,512]{1,0:T(8,128)(2,1)} %v_ref.7, s32[6,256]{1,0:T(8,128)} %bitcast.8, f32[4,16]{1,0:T(4,128)} %bitcast.9), custom_call_target="tpu_custom_call" | custom-call | flops 134217728 | bytes 1390848 | tf_op jit(solution)/shard_map/pallas_call | solution.py:35
  23.8 0.6 copy-done.10
  24.5 2.5 %shard_map.120.attn_ref.refs_4_ = bf16[256,512]{1,0:T(8,128)(2,1)} custom-call(s32[1]{0:T(128)} %bitcast.1.seq_ref.refs_1_, bf16[256,512]{1,0:T(8,128)(2,1)} %q_ref.5, f32[256,24]{1,0:T(8,128)} %get-tuple-element.23.coef_ref.refs_8_, f32[256,512]{1,0:T(8,128)} %get-tuple-element.24.attn_in, bf16[512,128]{1,0:T(8,128)(2,1)} %copy-done, ...), custom_call_target="tpu_custom_call" | custom-call | flops 100663296 | bytes 1466372 | tf_op jit(solution)/shard_map/pallas_call | solution.py:35
  27.0 2.6 %collective-permute-start.13 = (bf16[256,512]{1,0:T(8,128)(2,1)}, bf16[256,512]{1,0:T(8,128)(2,1)S(1)}, u32[]{:S(2)}, u32[]{:S(2)}) collective-permute-start(bf16[256,512]{1,0:T(8,128)(2,1)} %shard_map.120.attn_ref.refs_4_), channel_id=1, source_target_pairs={{0,12},{4,8},{8,4},{12,0},{16,28},{20,24},{24,20},{28,16},{1,13},{... | collective-permute-start | bytes 786440 | tf_op jit(solution)/shard_map/ppermute | solution.py:240
  29.5 0.4 collective-permute-start.12
  29.9 0.5 collective-permute-start.11
  30.5 0.7 copy-done.13
  31.2 0.1 copy-done.14
  31.3 4.3 %shard_map.122 = (bf16[256,512]{1,0:T(8,128)(2,1)}, bf16[3,512,128]{2,1,0:T(8,128)(2,1)}, bf16[256,512]{1,0:T(8,128)(2,1)}, bf16[256,512]{1,0:T(8,128)(2,1)}, bf...) custom-call(s32[1]{0:T(128)} %bitcast.head_ref.refs_0_, s32[1]{0:T(128)} %bitcast.1.seq_ref.refs_1_, ...), custom_call_target="tpu_custom_call" | custom-call | flops 536870912 | bytes 5136392 | tf_op jit(solution)/shard_map/pallas_call | solution.py:35
  35.5 1.5 %collective-permute-start.15 = (bf16[3,512,128]{2,1,0:T(8,128)(2,1)}, bf16[3,512,128]{2,1,0:T(8,128)(2,1)S(1)}, u32[]{:S(2)}, u32[]{:S(2)}) collective-permute-start(bf16[3,512,128]{2,1,0:T(8,128)(2,1)} %get-tuple-element.36), channel_id=1, source_target_pairs={{0,4},{4,0},{8,12},{12,8},{16,20},{20,16},{24,28},{28,24},{1,5},{5... | collective-permute-start | bytes 1179656 | tf_op jit(solution)/shard_map/ppermute | solution.py:240
  37.0 6.1 %shard_map.125 = (bf16[256,512]{1,0:T(8,128)(2,1)}, f32[256,512]{1,0:T(8,128)}, f32[256,512]{1,0:T(8,128)}, f32[16,4]{1,0:T(8,128)}) custom-call(s32[1]{0:T(128)} %bitcast.1.seq_ref.refs_1_, bf16[256,512]{1,0:T(8,128)(2,1)} %q_ref.5, bf16[256,512]{1,0:T(8,128)(2,1)} %k_ref.7, bf16[256,512]{1,0:T(8,128)(2,1)} %v_ref.7, ...), custom_call_target="tpu_custom_call" | custom-call | flops 335544320 | bytes 2826500 | tf_op jit(solution)/shard_map/pallas_call | solution.py:35
  43.1 0.5 collective-permute-start.18
  43.6 7.0 %collective-permute-done.18 = f32[16,4]{1,0:T(8,128)S(1)} collective-permute-done((f32[16,4]{1,0:T(8,128)}, f32[16,4]{1,0:T(8,128)S(1)}, u32[]{:S(2)}, u32[]{:S(2)}) %collective-permute-start.18) | collective-permute-done | bytes 288 | tf_op jit(solution)/shard_map/ppermute | solution.py:240
  50.6 0.7 add.47
  51.3 1.6 %collective-permute-start.19 = (f32[16,4]{1,0:T(8,128)S(1)}, f32[16,4]{1,0:T(8,128)S(1)}, u32[]{:S(2)}, u32[]{:S(2)}) collective-permute-start(f32[16,4]{1,0:T(8,128)S(1)} %add.47), channel_id=1, source_target_pairs={{0,8},{4,12},{8,0},{12,4},{16,24},{20,28},{24,16},{28,20},{1,9},{5... | collective-permute-start | bytes 776 | tf_op jit(solution)/shard_map/ppermute | solution.py:240
  52.9 2.1 %collective-permute-done.19 = f32[16,4]{1,0:T(8,128)S(1)} collective-permute-done((f32[16,4]{1,0:T(8,128)S(1)}, f32[16,4]{1,0:T(8,128)S(1)}, u32[]{:S(2)}, u32[]{:S(2)}) %collective-permute-start.19) | collective-permute-done | bytes 288 | tf_op jit(solution)/shard_map/ppermute | solution.py:240
  55.0 1.6 %collective-permute-start.20 = (f32[16,4]{1,0:T(8,128)S(1)}, f32[16,4]{1,0:T(8,128)S(1)}, u32[]{:S(2)}, u32[]{:S(2)}) collective-permute-start(f32[16,4]{1,0:T(8,128)S(1)} %add.48), channel_id=1, source_target_pairs={{0,16},{4,20},{8,24},{12,28},{16,0},{20,4},{24,8},{28,12},{1,17},{... | collective-permute-start | bytes 776 | tf_op jit(solution)/shard_map/ppermute | solution.py:240
  56.6 3.0 %collective-permute-done.20 = f32[16,4]{1,0:T(8,128)S(1)} collective-permute-done((f32[16,4]{1,0:T(8,128)S(1)}, f32[16,4]{1,0:T(8,128)S(1)}, u32[]{:S(2)}, u32[]{:S(2)}) %collective-permute-start.20) | collective-permute-done | bytes 288 | tf_op jit(solution)/shard_map/ppermute | solution.py:240
  59.5 1.5 %collective-permute-start.8 = (bf16[256,512]{1,0:T(8,128)(2,1)}, bf16[256,512]{1,0:T(8,128)(2,1)S(1)}, u32[]{:S(2)}, u32[]{:S(2)}) collective-permute-start(bf16[256,512]{1,0:T(8,128)(2,1)} %get-tuple-element.28), channel_id=1, source_target_pairs={{0,4},{4,0},{8,12},{12,8},{16,20},{20,16},{24,28},{28,24},{1,5},{5... | collective-permute-start | bytes 786440 | tf_op jit(solution)/shard_map/ppermute | solution.py:240
  61.0 1.6 %collective-permute-start.9 = (bf16[256,512]{1,0:T(8,128)(2,1)}, bf16[256,512]{1,0:T(8,128)(2,1)S(1)}, u32[]{:S(2)}, u32[]{:S(2)}) collective-permute-start(bf16[256,512]{1,0:T(8,128)(2,1)} %get-tuple-element.29), channel_id=1, source_target_pairs={{0,8},{4,12},{8,0},{12,4},{16,24},{20,28},{24,16},{28,20},{1,9},{5... | collective-permute-start | bytes 786440 | tf_op jit(solution)/shard_map/ppermute | solution.py:240
  62.6 0.4 collective-permute-start.10
  63.0 3.2 %shard_map.121 = (bf16[2,256,512]{2,1,0:T(8,128)(2,1)}, bf16[2,256,512]{2,1,0:T(8,128)(2,1)}) custom-call(s32[1]{0:T(128)} %bitcast.head_ref.refs_0_, bf16[256,512]{1,0:T(8,128)(2,1)} %shard_map.120.attn_ref.refs_4_, bf16[512,2048]{1,0:T(8,128)(2,1)} %refs_6_.1), custom_call_target="tpu_custom_call" | custom-call | flops 536870912 | bytes 3407876 | tf_op jit(solution)/shard_map/pallas_call | solution.py:35
  66.3 0.7 copy.13
  66.9 2.0 %collective-permute-done.8.refs_1_ = bf16[256,512]{1,0:T(8,128)(2,1)S(1)} collective-permute-done((bf16[256,512]{1,0:T(8,128)(2,1)}, bf16[256,512]{1,0:T(8,128)(2,1)S(1)}, u32[]{:S(2)}, u32[]{:S(2)}) %collective-permute-start.8) | collective-permute-done | bytes 262176 | tf_op jit(solution)/shard_map/ppermute | solution.py:240
  68.9 0.8 collective-permute-done.9.refs_2_
  69.7 2.8 %collective-permute-done.10.refs_3_ = bf16[256,512]{1,0:T(8,128)(2,1)S(1)} collective-permute-done((bf16[256,512]{1,0:T(8,128)(2,1)}, bf16[256,512]{1,0:T(8,128)(2,1)S(1)}, u32[]{:S(2)}, u32[]{:S(2)}) %collective-permute-start.10) | collective-permute-done | bytes 262176 | tf_op jit(solution)/shard_map/ppermute | solution.py:240
  72.5 0.7 copy-done.8
  73.2 2.8 %shard_map.124 = bf16[1,256,512]{2,1,0:T(8,128)(2,1)} custom-call(s32[1]{0:T(128)} %bitcast.1.seq_ref.refs_1_, bf16[256,512]{1,0:T(8,128)(2,1)} %get-tuple-element.27.refs_0_, bf16[256,512]{1,0:T(8,128)(2,1)} %copy-done.6, bf16[256,512]{1,0:T(8,128)(2,1)} %copy-done.7, bf16[256,512]{1,0:T(8,128)(2,1)} %copy-done.8, ...), custom_call_target="tpu_custom_call" | custom-call | flops 268435456 | bytes 2359300 | tf_op jit(solution)/shard_map/pallas_call | solution.py:35
  76.0 1.4 %collective-permute-start.14 = (bf16[1,256,512]{2,1,0:T(8,128)(2,1)}, bf16[1,256,512]{2,1,0:T(8,128)(2,1)S(1)}, u32[]{:S(2)}, u32[]{:S(2)}) collective-permute-start(bf16[1,256,512]{2,1,0:T(8,128)(2,1)} %shard_map.124), channel_id=1, source_target_pairs={{0,16},{4,20},{8,24},{12,28},{16,0},{20,4},{24,8},{28,12},{1,17},{... | collective-permute-start | bytes 786440 | tf_op jit(solution)/shard_map/ppermute | solution.py:240
  77.4 2.8 %shard_map.123 = f32[1,256,512]{2,1,0:T(8,128)} custom-call(s32[1]{0:T(128)} %bitcast.1.seq_ref.refs_1_, bf16[256,512]{1,0:T(8,128)(2,1)} %get-tuple-element.27.refs_0_, bf16[256,512]{1,0:T(8,128)(2,1)} %copy-done.6, bf16[256,512]{1,0:T(8,128)(2,1)} %copy-done.7, bf16[256,512]{1,0:T(8,128)(2,1)} %copy-done.8, bf16[256,512]{1,0:T(8,128)(2,1)} %shard_map.120.attn_ref.refs_4_, ...), custom_call_target="tpu_custom_call" | custom-call | flops 268435456 | bytes 2621444 | tf_op jit(solution)/shard_map/pallas_call | solution.py:35
  80.2 0.5 collective-permute-start.16
  80.8 1.6 %collective-permute-start.4 = (bf16[1,256,512]{2,1,0:T(8,128)(2,1)S(1)}, bf16[1,256,512]{2,1,0:T(8,128)(2,1)S(1)}, u32[]{:S(2)}, u32[]{:S(2)}) collective-permute-start(bf16[1,256,512]{2,1,0:T(8,128)(2,1)S(1)} %add_convert_fusion.2), channel_id=1, source_target_pairs={{0,2},{1,3},{2,0},{3,1},{4,6},{5,7},{6,4},{7,5},{8,10},{9,11},{10,... | collective-permute-start | bytes 786440 | tf_op jit(solution)/shard_map/ppermute | solution.py:240
  82.4 4.9 %collective-permute-done.14 = bf16[1,256,512]{2,1,0:T(8,128)(2,1)S(1)} collective-permute-done((bf16[1,256,512]{2,1,0:T(8,128)(2,1)}, bf16[1,256,512]{2,1,0:T(8,128)(2,1)S(1)}, u32[]{:S(2)}, u32[]{:S(2)}) %collective-permute-start.14) | collective-permute-done | bytes 262176 | tf_op jit(solution)/shard_map/ppermute | solution.py:240
  87.3 1.9 %add_bitcast_fusion = f32[256,512]{1,0:T(8,128)} fusion(f32[1,256,512]{2,1,0:T(8,128)} %shard_map.123, bf16[1,256,512]{2,1,0:T(8,128)(2,1)S(1)} %collective-permute-done.14), kind=kLoop, calls=%fused_computation.1 | loop fusion | flops 262144 | bytes 1310720 | tf_op jit(solution)/shard_map/add | solution.py:257
  89.3 1.3 %collective-permute-start.17 = (bf16[1,512,128]{2,1,0:T(8,128)(2,1)S(1)}, bf16[1,512,128]{2,1,0:T(8,128)(2,1)S(1)}, u32[]{:S(2)}, u32[]{:S(2)}) collective-permute-start(bf16[1,512,128]{2,1,0:T(8,128)(2,1)S(1)} %add_convert_fusion.3), channel_id=1, source_target_pairs={{16,0},{20,4},{24,8},{28,12},{17,1},{21,5},{25,9},{29,13},{18,2},{... | collective-permute-start | bytes 393224 | tf_op jit(solution)/shard_map/ppermute | solution.py:246
  90.6 0.8 fusion
  91.4 5.6 %collective-permute-done.17.rest_2_ = bf16[1,512,128]{2,1,0:T(8,128)(2,1)S(1)} collective-permute-done((bf16[1,512,128]{2,1,0:T(8,128)(2,1)S(1)}, bf16[1,512,128]{2,1,0:T(8,128)(2,1)S(1)}, u32[]{:S(2)}, u32[]{:S(2)}) %collective-permute-start.17) | collective-permute-done | bytes 131104 | tf_op jit(solution)/shard_map/ppermute | solution.py:246
  97.0 0.6 copy-done.16
  97.7 2.7 %shard_map.126 = (bf16[256,512]{1,0:T(8,128)(2,1)}, bf16[256,512]{1,0:T(8,128)(2,1)}) custom-call(s32[1]{0:T(128)} %bitcast.1.seq_ref.refs_1_, bf16[256,512]{1,0:T(8,128)(2,1)} %k_ref.7, bf16[256,512]{1,0:T(8,128)(2,1)} %v_ref.7, f32[256,512]{1,0:T(8,128)} %get-tuple-element.34.dk_in, f32[256,512]{1,0:T(8,128)} %get-tuple-element.35.dv_in, ...), custom_call_target="tpu_custom_call" | custom-call | flops 67108864 | bytes 2883588 | tf_op jit(solution)/shard_map/pallas_call | solution.py:35
  (48 shorter events, 0.4 us)
Async XLA Ops:
  2.6 6.7 %collective-permute-start = (bf16[512,128]{1,0:T(8,128)(2,1)}, bf16[512,128]{1,0:T(8,128)(2,1)S(1)}, u32[]{:S(2)}, u32[]{:S(2)}) collective-permute-start(bf16[512,128]{1,0:T(8,128)(2,1)} %shard_map.119), channel_id=1, source_target_pairs={{0,4},{4,0},{8,12},{12,8},{16,20},{20,16},{24,28},{28,24},{1,5},{5... | collective-permute-start | bytes 393224 | tf_op jit(solution)/shard_map/ppermute | solution.py:240
  9.3 14.5 %copy-start = (bf16[512,128]{1,0:T(8,128)(2,1)}, bf16[512,128]{1,0:T(8,128)(2,1)S(1)}, u32[]{:S(2)}) copy-start(bf16[512,128]{1,0:T(8,128)(2,1)S(1)} %collective-permute-done.rest_0_) | copy-start | bytes 393220
  10.3 5.0 %collective-permute-start.1 = (bf16[512,128]{1,0:T(8,128)(2,1)S(1)}, bf16[512,128]{1,0:T(8,128)(2,1)S(1)}, u32[]{:S(2)}, u32[]{:S(2)}) collective-permute-start(bf16[512,128]{1,0:T(8,128)(2,1)S(1)} %add_convert_fusion.5), channel_id=1, source_target_pairs={{0,8},{4,12},{8,0},{12,4},{16,24},{20,28},{24,16},{28,20},{1,9},{5... | collective-permute-start | bytes 393224 | tf_op jit(solution)/shard_map/ppermute | solution.py:240
  12.1 8.0 %collective-permute-start.6 = (bf16[256,512]{1,0:T(8,128)(2,1)}, bf16[256,512]{1,0:T(8,128)(2,1)S(1)}, u32[]{:S(2)}, u32[]{:S(2)}) collective-permute-start(bf16[256,512]{1,0:T(8,128)(2,1)} %refs_2_.1), channel_id=1, source_target_pairs={{0,2},{1,3},{2,0},{3,1},{4,6},{5,7},{6,4},{7,5},{8,10},{9,11},{10,... | collective-permute-start | bytes 786440 | tf_op jit(solution)/shard_map/ppermute | solution.py:240
  15.3 8.5 %copy-start.1 = (bf16[512,128]{1,0:T(8,128)(2,1)}, bf16[512,128]{1,0:T(8,128)(2,1)S(1)}, u32[]{:S(2)}) copy-start(bf16[512,128]{1,0:T(8,128)(2,1)S(1)} %collective-permute-done.1.rest_1_) | copy-start | bytes 393220
  15.3 8.5 %collective-permute-start.2 = (bf16[512,128]{1,0:T(8,128)(2,1)S(1)}, bf16[512,128]{1,0:T(8,128)(2,1)S(1)}, u32[]{:S(2)}, u32[]{:S(2)}) collective-permute-start(bf16[512,128]{1,0:T(8,128)(2,1)S(1)} %add_convert_fusion.4), channel_id=1, source_target_pairs={{0,16},{4,20},{8,24},{12,28},{1,17},{5,21},{9,25},{13,29},{2,18},{... | collective-permute-start | bytes 393224 | tf_op jit(solution)/shard_map/ppermute | solution.py:246
  20.1 10.4 %collective-permute-start.5 = (bf16[256,512]{1,0:T(8,128)(2,1)}, bf16[256,512]{1,0:T(8,128)(2,1)S(1)}, u32[]{:S(2)}, u32[]{:S(2)}) collective-permute-start(bf16[256,512]{1,0:T(8,128)(2,1)} %refs_2_.1), channel_id=1, source_target_pairs={{0,1},{1,0},{2,3},{3,2},{4,5},{5,4},{6,7},{7,6},{8,9},{9,8},{10,11... | collective-permute-start | bytes 786440 | tf_op jit(solution)/shard_map/ppermute | solution.py:240
  20.2 10.3 %copy-start.12 = (bf16[256,512]{1,0:T(8,128)(2,1)}, bf16[256,512]{1,0:T(8,128)(2,1)S(1)}, u32[]{:S(2)}) copy-start(bf16[256,512]{1,0:T(8,128)(2,1)S(1)} %collective-permute-done.6.refs_4_) | copy-start | bytes 786436
  20.2 10.3 %collective-permute-start.7 = (bf16[256,512]{1,0:T(8,128)(2,1)S(1)}, bf16[256,512]{1,0:T(8,128)(2,1)S(1)}, u32[]{:S(2)}, u32[]{:S(2)}) collective-permute-start(bf16[256,512]{1,0:T(8,128)(2,1)S(1)} %collective-permute-done.6.refs_4_), channel_id=1, source_target_pairs={{0,1},{1,0},{2,3},{3,2},{4,5},{5,4},{6,7},{7,6},{8,9},{9,8},{10,11... | collective-permute-start | bytes 786440 | tf_op jit(solution)/shard_map/ppermute | solution.py:240
  23.8 0.7 copy-start.10
  27.0 34.0 %collective-permute-start.13 = (bf16[256,512]{1,0:T(8,128)(2,1)}, bf16[256,512]{1,0:T(8,128)(2,1)S(1)}, u32[]{:S(2)}, u32[]{:S(2)}) collective-permute-start(bf16[256,512]{1,0:T(8,128)(2,1)} %shard_map.120.attn_ref.refs_4_), channel_id=1, source_target_pairs={{0,12},{4,8},{8,4},{12,0},{16,28},{20,24},{24,20},{28,16},{1,13},{... | collective-permute-start | bytes 786440 | tf_op jit(solution)/shard_map/ppermute | solution.py:240
  29.5 33.1 %collective-permute-start.12 = (bf16[256,512]{1,0:T(8,128)(2,1)}, bf16[256,512]{1,0:T(8,128)(2,1)S(1)}, u32[]{:S(2)}, u32[]{:S(2)}) collective-permute-start(bf16[256,512]{1,0:T(8,128)(2,1)} %shard_map.120.attn_ref.refs_4_), channel_id=1, source_target_pairs={{0,8},{4,12},{8,0},{12,4},{16,24},{20,28},{24,16},{28,20},{1,9},{5... | collective-permute-start | bytes 786440 | tf_op jit(solution)/shard_map/ppermute | solution.py:240
  29.9 36.3 %collective-permute-start.11 = (bf16[256,512]{1,0:T(8,128)(2,1)}, bf16[256,512]{1,0:T(8,128)(2,1)S(1)}, u32[]{:S(2)}, u32[]{:S(2)}) collective-permute-start(bf16[256,512]{1,0:T(8,128)(2,1)} %shard_map.120.attn_ref.refs_4_), channel_id=1, source_target_pairs={{0,4},{4,0},{8,12},{12,8},{16,20},{20,16},{24,28},{28,24},{1,5},{5... | collective-permute-start | bytes 786440 | tf_op jit(solution)/shard_map/ppermute | solution.py:240
  30.5 0.7 copy-start.13
  30.5 0.8 copy-start.14
  35.5 44.6 %collective-permute-start.15 = (bf16[3,512,128]{2,1,0:T(8,128)(2,1)}, bf16[3,512,128]{2,1,0:T(8,128)(2,1)S(1)}, u32[]{:S(2)}, u32[]{:S(2)}) collective-permute-start(bf16[3,512,128]{2,1,0:T(8,128)(2,1)} %get-tuple-element.36), channel_id=1, source_target_pairs={{0,4},{4,0},{8,12},{12,8},{16,20},{20,16},{24,28},{28,24},{1,5},{5... | collective-permute-start | bytes 1179656 | tf_op jit(solution)/shard_map/ppermute | solution.py:240
  43.1 7.5 %collective-permute-start.18 = (f32[16,4]{1,0:T(8,128)}, f32[16,4]{1,0:T(8,128)S(1)}, u32[]{:S(2)}, u32[]{:S(2)}) collective-permute-start(f32[16,4]{1,0:T(8,128)} %get-tuple-element.39), channel_id=1, source_target_pairs={{0,4},{4,0},{8,12},{12,8},{16,20},{20,16},{24,28},{28,24},{1,5},{5... | collective-permute-start | bytes 776 | tf_op jit(solution)/shard_map/ppermute | solution.py:240
  51.3 3.7 %collective-permute-start.19 = (f32[16,4]{1,0:T(8,128)S(1)}, f32[16,4]{1,0:T(8,128)S(1)}, u32[]{:S(2)}, u32[]{:S(2)}) collective-permute-start(f32[16,4]{1,0:T(8,128)S(1)} %add.47), channel_id=1, source_target_pairs={{0,8},{4,12},{8,0},{12,4},{16,24},{20,28},{24,16},{28,20},{1,9},{5... | collective-permute-start | bytes 776 | tf_op jit(solution)/shard_map/ppermute | solution.py:240
  55.0 4.5 %collective-permute-start.20 = (f32[16,4]{1,0:T(8,128)S(1)}, f32[16,4]{1,0:T(8,128)S(1)}, u32[]{:S(2)}, u32[]{:S(2)}) collective-permute-start(f32[16,4]{1,0:T(8,128)S(1)} %add.48), channel_id=1, source_target_pairs={{0,16},{4,20},{8,24},{12,28},{16,0},{20,4},{24,8},{28,12},{1,17},{... | collective-permute-start | bytes 776 | tf_op jit(solution)/shard_map/ppermute | solution.py:240
  59.5 9.4 %collective-permute-start.8 = (bf16[256,512]{1,0:T(8,128)(2,1)}, bf16[256,512]{1,0:T(8,128)(2,1)S(1)}, u32[]{:S(2)}, u32[]{:S(2)}) collective-permute-start(bf16[256,512]{1,0:T(8,128)(2,1)} %get-tuple-element.28), channel_id=1, source_target_pairs={{0,4},{4,0},{8,12},{12,8},{16,20},{20,16},{24,28},{28,24},{1,5},{5... | collective-permute-start | bytes 786440 | tf_op jit(solution)/shard_map/ppermute | solution.py:240
  61.0 11.5 %copy-start.3 = (bf16[256,512]{1,0:T(8,128)(2,1)}, bf16[256,512]{1,0:T(8,128)(2,1)S(1)}, u32[]{:S(2)}) copy-start(bf16[256,512]{1,0:T(8,128)(2,1)S(1)} %collective-permute-done.13.refs_7_) | copy-start | bytes 786436
  61.0 8.7 %collective-permute-start.9 = (bf16[256,512]{1,0:T(8,128)(2,1)}, bf16[256,512]{1,0:T(8,128)(2,1)S(1)}, u32[]{:S(2)}, u32[]{:S(2)}) collective-permute-start(bf16[256,512]{1,0:T(8,128)(2,1)} %get-tuple-element.29), channel_id=1, source_target_pairs={{0,8},{4,12},{8,0},{12,4},{16,24},{20,28},{24,16},{28,20},{1,9},{5... | collective-permute-start | bytes 786440 | tf_op jit(solution)/shard_map/ppermute | solution.py:240
  62.6 9.9 %copy-start.4 = (bf16[256,512]{1,0:T(8,128)(2,1)}, bf16[256,512]{1,0:T(8,128)(2,1)S(1)}, u32[]{:S(2)}) copy-start(bf16[256,512]{1,0:T(8,128)(2,1)S(1)} %collective-permute-done.12.refs_6_) | copy-start | bytes 786436
  62.6 9.9 %collective-permute-start.10 = (bf16[256,512]{1,0:T(8,128)(2,1)}, bf16[256,512]{1,0:T(8,128)(2,1)S(1)}, u32[]{:S(2)}, u32[]{:S(2)}) collective-permute-start(bf16[256,512]{1,0:T(8,128)(2,1)} %get-tuple-element.30), channel_id=1, source_target_pairs={{0,12},{4,8},{8,4},{12,0},{16,28},{20,24},{24,20},{28,16},{1,13},{... | collective-permute-start | bytes 786440 | tf_op jit(solution)/shard_map/ppermute | solution.py:240
  66.3 6.2 %copy-start.5 = (bf16[256,512]{1,0:T(8,128)(2,1)}, bf16[256,512]{1,0:T(8,128)(2,1)S(1)}, u32[]{:S(2)}) copy-start(bf16[256,512]{1,0:T(8,128)(2,1)S(1)} %collective-permute-done.11.refs_5_) | copy-start | bytes 786436
  66.3 14.5 %collective-permute-start.3 = (bf16[2,256,512]{2,1,0:T(8,128)(2,1)}, bf16[2,256,512]{2,1,0:T(8,128)(2,1)S(1)}, u32[]{:S(2)}, u32[]{:S(2)}) collective-permute-start(bf16[2,256,512]{2,1,0:T(8,128)(2,1)} %get-tuple-element.26), channel_id=1, source_target_pairs={{0,1},{1,0},{2,3},{3,2},{4,5},{5,4},{6,7},{7,6},{8,9},{9,8},{10,11... | collective-permute-start | bytes 1572872 | tf_op jit(solution)/shard_map/ppermute | solution.py:240
  68.9 3.6 %copy-start.6 = (bf16[256,512]{1,0:T(8,128)(2,1)}, bf16[256,512]{1,0:T(8,128)(2,1)S(1)}, u32[]{:S(2)}) copy-start(bf16[256,512]{1,0:T(8,128)(2,1)S(1)} %collective-permute-done.8.refs_1_) | copy-start | bytes 786436
  69.7 2.8 %copy-start.7 = (bf16[256,512]{1,0:T(8,128)(2,1)}, bf16[256,512]{1,0:T(8,128)(2,1)S(1)}, u32[]{:S(2)}) copy-start(bf16[256,512]{1,0:T(8,128)(2,1)S(1)} %collective-permute-done.9.refs_2_) | copy-start | bytes 786436
  72.5 0.7 copy-start.8
  73.2 6.9 %copy-start.15 = (bf16[3,512,128]{2,1,0:T(8,128)(2,1)S(1)}, bf16[3,512,128]{2,1,0:T(8,128)(2,1)}, u32[]{:S(2)}) copy-start(bf16[3,512,128]{2,1,0:T(8,128)(2,1)} %get-tuple-element.36) | copy-start | bytes 1179652
  76.0 4.8 %copy-start.11 = (bf16[2,256,512]{2,1,0:T(8,128)(2,1)S(1)}, bf16[2,256,512]{2,1,0:T(8,128)(2,1)}, u32[]{:S(2)}) copy-start(bf16[2,256,512]{2,1,0:T(8,128)(2,1)} %get-tuple-element.25) | copy-start | bytes 1572868
  76.0 11.4 %collective-permute-start.14 = (bf16[1,256,512]{2,1,0:T(8,128)(2,1)}, bf16[1,256,512]{2,1,0:T(8,128)(2,1)S(1)}, u32[]{:S(2)}, u32[]{:S(2)}) collective-permute-start(bf16[1,256,512]{2,1,0:T(8,128)(2,1)} %shard_map.124), channel_id=1, source_target_pairs={{0,16},{4,20},{8,24},{12,28},{16,0},{20,4},{24,8},{28,12},{1,17},{... | collective-permute-start | bytes 786440 | tf_op jit(solution)/shard_map/ppermute | solution.py:240
  80.1 11.2 %copy-start.2 = (bf16[3,512,128]{2,1,0:T(8,128)(2,1)}, bf16[3,512,128]{2,1,0:T(8,128)(2,1)S(1)}, u32[]{:S(2)}) copy-start(bf16[3,512,128]{2,1,0:T(8,128)(2,1)S(1)} %collective-permute-done.15.rest_0_) | copy-start | bytes 1179652
  80.2 9.0 %collective-permute-start.16 = (bf16[2,512,128]{2,1,0:T(8,128)(2,1)S(1)}, bf16[2,512,128]{2,1,0:T(8,128)(2,1)S(1)}, u32[]{:S(2)}, u32[]{:S(2)}) collective-permute-start(bf16[2,512,128]{2,1,0:T(8,128)(2,1)S(1)} %add_convert_fusion), channel_id=1, source_target_pairs={{0,8},{4,12},{8,0},{12,4},{16,24},{20,28},{24,16},{28,20},{1,9},{5... | collective-permute-start | bytes 786440 | tf_op jit(solution)/shard_map/ppermute | solution.py:240
  80.8 9.8 %collective-permute-start.4 = (bf16[1,256,512]{2,1,0:T(8,128)(2,1)S(1)}, bf16[1,256,512]{2,1,0:T(8,128)(2,1)S(1)}, u32[]{:S(2)}, u32[]{:S(2)}) collective-permute-start(bf16[1,256,512]{2,1,0:T(8,128)(2,1)S(1)} %add_convert_fusion.2), channel_id=1, source_target_pairs={{0,2},{1,3},{2,0},{3,1},{4,6},{5,7},{6,4},{7,5},{8,10},{9,11},{10,... | collective-permute-start | bytes 786440 | tf_op jit(solution)/shard_map/ppermute | solution.py:240
  89.2 7.8 %copy-start.9 = (bf16[2,512,128]{2,1,0:T(8,128)(2,1)}, bf16[2,512,128]{2,1,0:T(8,128)(2,1)S(1)}, u32[]{:S(2)}) copy-start(bf16[2,512,128]{2,1,0:T(8,128)(2,1)S(1)} %collective-permute-done.16.rest_1_) | copy-start | bytes 786436
  89.3 7.8 %collective-permute-start.17 = (bf16[1,512,128]{2,1,0:T(8,128)(2,1)S(1)}, bf16[1,512,128]{2,1,0:T(8,128)(2,1)S(1)}, u32[]{:S(2)}, u32[]{:S(2)}) collective-permute-start(bf16[1,512,128]{2,1,0:T(8,128)(2,1)S(1)} %add_convert_fusion.3), channel_id=1, source_target_pairs={{16,0},{20,4},{24,8},{28,12},{17,1},{21,5},{25,9},{29,13},{18,2},{... | collective-permute-start | bytes 393224 | tf_op jit(solution)/shard_map/ppermute | solution.py:246
  97.0 0.6 copy-start.16

commit v4 on v3

--- a/solution.py
+++ b/solution.py
@@ -240,12 +240,6 @@
     return lax.ppermute(value, axis, pairs)
 
 
-def one_way(value, axis, mask, up):
-    n = lax.axis_size(axis)
-    pairs = [(i, i ^ mask) for i in range(n) if (i & mask == 0) == up]
-    return lax.ppermute(value, axis, pairs)
-
-
 def reduce_blocks(send, keep, axis, bits):
     parts = [keep]
     for n, bit in enumerate(bits):
@@ -312,11 +306,8 @@
     found = []
     block_state = state
     for bit in range(seq_bits):
-        if bit == seq_bits - 1:
-            found.append(one_way(block_state, "seq", 1 << bit, True))
-        else:
-            got = swap(block_state, "seq", 1 << bit)
-            found.append(got)
+        got = swap(block_state, "seq", 1 << bit)
+        found.append(got)
         if bit < seq_bits - 1:
             block_state = (block_state.astype(F32) + got.astype(F32)).astype(BF16)
 
@@ -338,10 +329,7 @@
         ]
     term_parts = []
     for bit in range(seq_bits):
-        if bit == seq_bits - 1:
-            got = one_way(terms, "seq", 1 << bit, False)
-        else:
-            got = swap(terms, "seq", 1 << bit)
+        got = swap(terms, "seq", 1 << bit)
         term_parts.append(got)
         if bit < seq_bits - 1:
             terms = (terms[1:].astype(F32) + got[1:].astype(F32)).astype(BF16)

time: 101 us -> 99.1 us (0.981)
  starting transfers between devices: 28.6 us -> 26.1 us
    ppermute x19 -> x21, waiting for transfers between devices: 27.9 us -> 34.3 us  [swap(): return lax.ppermute(value, axis, pairs)]
    ppermute x2 -> x0, starting transfers between devices: 6.04 us -> none  [one_way(): return lax.ppermute(value, axis, pairs)]
    ppermute x2 -> x0, waiting for transfers between devices: 5.65 us -> none  [one_way(): return lax.ppermute(value, axis, pairs)]
    ppermute x19 -> x21, starting transfers between devices: 22.6 us -> 26.1 us  [swap(): return lax.ppermute(value, axis, pairs)]
  transfers between devices with their start and end apart: 21 -> 21, of which waited for: 10 -> 13; matrix products, arithmetic and copies ran while one was open for 4% -> 4% of each run, Pallas kernels for 25% -> 25%
where the time goes in v4:
time: 99.1 us; the launch traced here: 98.7 us
  waiting for transfers between devices  34.3 us (35%)
  Pallas kernels  29.4 us (30%)
  starting transfers between devices  26.1 us (26%)
  other arithmetic  4.62 us (5%)
  local copies, waits for them, and re-layouts  3.44 us (3%)
    ppermute x21, waiting for transfers between devices, swap(): return lax.ppermute(value, axis, pairs)  34.3 us
    pallas_call x9, Pallas kernels, local_call(): pl.pallas_call(body, out_shape=tuple(outs), in_specs=[SMEM_SPEC] * scalar...  29.4 us
    ppermute x21, starting transfers between devices, swap(): return lax.ppermute(value, axis, pairs)  26.1 us
    unnamed x35, local copies, waits for them, and re-layouts  3.44 us
  transfers between devices with their start and end apart: 21, of which 13 were waited for; matrix products, arithmetic and copies ran while one was open for 4% of the time, Pallas kernels for 25%

profile of v4, /device:TPU:0, one launch (start us, length us, event | category | flops | bytes accessed | tf_op | source)
XLA Modules:
  0.0 98.7 jit_solution(14045732799686757431)
XLA Ops:
  0.6 2.0 %shard_map.119 = bf16[512,128]{1,0:T(8,128)(2,1)} custom-call(bf16[256,512]{1,0:T(8,128)(2,1)} %k_ref.7, bf16[256,512]{1,0:T(8,128)(2,1)} %v_ref.7), custom_call_target="tpu_custom_call" | custom-call | flops 33554432 | bytes 655360 | tf_op jit(solution)/shard_map/pallas_call | solution.py:35
  2.6 3.0 %collective-permute-start = (bf16[512,128]{1,0:T(8,128)(2,1)}, bf16[512,128]{1,0:T(8,128)(2,1)S(1)}, u32[]{:S(2)}, u32[]{:S(2)}) collective-permute-start(bf16[512,128]{1,0:T(8,128)(2,1)} %shard_map.119), channel_id=1, source_target_pairs={{0,4},{4,0},{8,12},{12,8},{16,20},{20,16},{24,28},{28,24},{1,5},{5... | collective-permute-start | bytes 393224 | tf_op jit(solution)/shard_map/ppermute | solution.py:240
  5.6 3.7 %collective-permute-done.rest_0_ = bf16[512,128]{1,0:T(8,128)(2,1)S(1)} collective-permute-done((bf16[512,128]{1,0:T(8,128)(2,1)}, bf16[512,128]{1,0:T(8,128)(2,1)S(1)}, u32[]{:S(2)}, u32[]{:S(2)}) %collective-permute-start) | collective-permute-done | bytes 131104 | tf_op jit(solution)/shard_map/ppermute | solution.py:240
  9.3 1.0 %add_convert_fusion.5 = bf16[512,128]{1,0:T(8,128)(2,1)S(1)} fusion(bf16[512,128]{1,0:T(8,128)(2,1)S(1)} %collective-permute-done.rest_0_, bf16[512,128]{1,0:T(8,128)(2,1)} %shard_map.119), kind=kLoop, calls=%fused_computation.7 | loop fusion | flops 262144 | bytes 393216 | tf_op jit(solution)/shard_map/convert_element_type | solution.py:312
  10.3 1.9 %collective-permute-start.1 = (bf16[512,128]{1,0:T(8,128)(2,1)S(1)}, bf16[512,128]{1,0:T(8,128)(2,1)S(1)}, u32[]{:S(2)}, u32[]{:S(2)}) collective-permute-start(bf16[512,128]{1,0:T(8,128)(2,1)S(1)} %add_convert_fusion.5), channel_id=1, source_target_pairs={{0,8},{4,12},{8,0},{12,4},{16,24},{20,28},{24,16},{28,20},{1,9},{5... | collective-permute-start | bytes 393224 | tf_op jit(solution)/shard_map/ppermute | solution.py:240
  12.1 1.5 %collective-permute-start.6 = (bf16[256,512]{1,0:T(8,128)(2,1)}, bf16[256,512]{1,0:T(8,128)(2,1)S(1)}, u32[]{:S(2)}, u32[]{:S(2)}) collective-permute-start(bf16[256,512]{1,0:T(8,128)(2,1)} %refs_2_.1), channel_id=1, source_target_pairs={{0,2},{1,3},{2,0},{3,1},{4,6},{5,7},{6,4},{7,5},{8,10},{9,11},{10,... | collective-permute-start | bytes 786440 | tf_op jit(solution)/shard_map/ppermute | solution.py:240
  13.7 1.6 %collective-permute-done.1.rest_1_ = bf16[512,128]{1,0:T(8,128)(2,1)S(1)} collective-permute-done((bf16[512,128]{1,0:T(8,128)(2,1)S(1)}, bf16[512,128]{1,0:T(8,128)(2,1)S(1)}, u32[]{:S(2)}, u32[]{:S(2)}) %collective-permute-start.1) | collective-permute-done | bytes 131104 | tf_op jit(solution)/shard_map/ppermute | solution.py:240
  15.3 2.9 %collective-permute-start.2 = (bf16[512,128]{1,0:T(8,128)(2,1)S(1)}, bf16[512,128]{1,0:T(8,128)(2,1)S(1)}, u32[]{:S(2)}, u32[]{:S(2)}) collective-permute-start(bf16[512,128]{1,0:T(8,128)(2,1)S(1)} %add_convert_fusion.4), channel_id=1, source_target_pairs={{0,16},{4,20},{8,24},{12,28},{16,0},{20,4},{24,8},{28,12},{1,17},{... | collective-permute-start | bytes 393224 | tf_op jit(solution)/shard_map/ppermute | solution.py:240
  18.2 1.0 %collective-permute-done.6.refs_4_ = bf16[256,512]{1,0:T(8,128)(2,1)S(1)} collective-permute-done((bf16[256,512]{1,0:T(8,128)(2,1)}, bf16[256,512]{1,0:T(8,128)(2,1)S(1)}, u32[]{:S(2)}, u32[]{:S(2)}) %collective-permute-start.6) | collective-permute-done | bytes 262176 | tf_op jit(solution)/shard_map/ppermute | solution.py:240
  19.3 3.2 %shard_map.118 = (f32[256,512]{1,0:T(8,128)}, f32[256,24]{1,0:T(8,128)}, bf16[96,256]{1,0:T(8,128)(2,1)}) custom-call(bf16[256,512]{1,0:T(8,128)(2,1)} %q_ref.5, bf16[256,512]{1,0:T(8,128)(2,1)} %k_ref.7, bf16[256,512]{1,0:T(8,128)(2,1)} %v_ref.7, s32[6,256]{1,0:T(8,128)} %bitcast.8, f32[4,16]{1,0:T(4,128)} %bitcast.9), custom_call_target="tpu_custom_call" | custom-call | flops 134217728 | bytes 1390848 | tf_op jit(solution)/shard_map/pallas_call | solution.py:35
  22.5 0.2 collective-permute-done.2.rest_2_
  22.7 0.7 copy-done.10
  23.3 2.5 %shard_map.120.attn_ref.refs_4_ = bf16[256,512]{1,0:T(8,128)(2,1)} custom-call(s32[1]{0:T(128)} %bitcast.1.seq_ref.refs_1_, bf16[256,512]{1,0:T(8,128)(2,1)} %q_ref.5, f32[256,24]{1,0:T(8,128)} %get-tuple-element.23.coef_ref.refs_8_, f32[256,512]{1,0:T(8,128)} %get-tuple-element.24.attn_in, bf16[512,128]{1,0:T(8,128)(2,1)} %copy-done, ...), custom_call_target="tpu_custom_call" | custom-call | flops 100663296 | bytes 1466372 | tf_op jit(solution)/shard_map/pallas_call | solution.py:35
  25.9 1.9 %collective-permute-start.13 = (bf16[256,512]{1,0:T(8,128)(2,1)}, bf16[256,512]{1,0:T(8,128)(2,1)S(1)}, u32[]{:S(2)}, u32[]{:S(2)}) collective-permute-start(bf16[256,512]{1,0:T(8,128)(2,1)} %shard_map.120.attn_ref.refs_4_), channel_id=1, source_target_pairs={{0,12},{4,8},{8,4},{12,0},{16,28},{20,24},{24,20},{28,16},{1,13},{... | collective-permute-start | bytes 786440 | tf_op jit(solution)/shard_map/ppermute | solution.py:240
  27.7 1.4 %collective-permute-start.12 = (bf16[256,512]{1,0:T(8,128)(2,1)}, bf16[256,512]{1,0:T(8,128)(2,1)S(1)}, u32[]{:S(2)}, u32[]{:S(2)}) collective-permute-start(bf16[256,512]{1,0:T(8,128)(2,1)} %shard_map.120.attn_ref.refs_4_), channel_id=1, source_target_pairs={{0,8},{4,12},{8,0},{12,4},{16,24},{20,28},{24,16},{28,20},{1,9},{5... | collective-permute-start | bytes 786440 | tf_op jit(solution)/shard_map/ppermute | solution.py:240
  29.1 0.3 collective-permute-start.11
  29.4 0.7 copy-done.13
  30.2 4.3 %shard_map.122 = (bf16[256,512]{1,0:T(8,128)(2,1)}, bf16[3,512,128]{2,1,0:T(8,128)(2,1)}, bf16[256,512]{1,0:T(8,128)(2,1)}, bf16[256,512]{1,0:T(8,128)(2,1)}, bf...) custom-call(s32[1]{0:T(128)} %bitcast.head_ref.refs_0_, s32[1]{0:T(128)} %bitcast.1.seq_ref.refs_1_, ...), custom_call_target="tpu_custom_call" | custom-call | flops 536870912 | bytes 5136392 | tf_op jit(solution)/shard_map/pallas_call | solution.py:35
  34.4 1.7 %collective-permute-start.15 = (bf16[3,512,128]{2,1,0:T(8,128)(2,1)}, bf16[3,512,128]{2,1,0:T(8,128)(2,1)S(1)}, u32[]{:S(2)}, u32[]{:S(2)}) collective-permute-start(bf16[3,512,128]{2,1,0:T(8,128)(2,1)} %get-tuple-element.36), channel_id=1, source_target_pairs={{0,4},{4,0},{8,12},{12,8},{16,20},{20,16},{24,28},{28,24},{1,5},{5... | collective-permute-start | bytes 1179656 | tf_op jit(solution)/shard_map/ppermute | solution.py:240
  36.2 6.1 %shard_map.125 = (bf16[256,512]{1,0:T(8,128)(2,1)}, f32[256,512]{1,0:T(8,128)}, f32[256,512]{1,0:T(8,128)}, f32[16,4]{1,0:T(8,128)}) custom-call(s32[1]{0:T(128)} %bitcast.1.seq_ref.refs_1_, bf16[256,512]{1,0:T(8,128)(2,1)} %q_ref.5, bf16[256,512]{1,0:T(8,128)(2,1)} %k_ref.7, bf16[256,512]{1,0:T(8,128)(2,1)} %v_ref.7, ...), custom_call_target="tpu_custom_call" | custom-call | flops 335544320 | bytes 2826500 | tf_op jit(solution)/shard_map/pallas_call | solution.py:35
  42.2 0.3 collective-permute-start.18
  42.5 7.1 %collective-permute-done.18 = f32[16,4]{1,0:T(8,128)S(1)} collective-permute-done((f32[16,4]{1,0:T(8,128)}, f32[16,4]{1,0:T(8,128)S(1)}, u32[]{:S(2)}, u32[]{:S(2)}) %collective-permute-start.18) | collective-permute-done | bytes 288 | tf_op jit(solution)/shard_map/ppermute | solution.py:240
  49.6 0.7 add.47
  50.3 0.7 collective-permute-start.19
  51.0 3.0 %collective-permute-done.19 = f32[16,4]{1,0:T(8,128)S(1)} collective-permute-done((f32[16,4]{1,0:T(8,128)S(1)}, f32[16,4]{1,0:T(8,128)S(1)}, u32[]{:S(2)}, u32[]{:S(2)}) %collective-permute-start.19) | collective-permute-done | bytes 288 | tf_op jit(solution)/shard_map/ppermute | solution.py:240
  54.0 2.6 %collective-permute-start.20 = (f32[16,4]{1,0:T(8,128)S(1)}, f32[16,4]{1,0:T(8,128)S(1)}, u32[]{:S(2)}, u32[]{:S(2)}) collective-permute-start(f32[16,4]{1,0:T(8,128)S(1)} %add.48), channel_id=1, source_target_pairs={{0,16},{4,20},{8,24},{12,28},{16,0},{20,4},{24,8},{28,12},{1,17},{... | collective-permute-start | bytes 776 | tf_op jit(solution)/shard_map/ppermute | solution.py:240
  56.6 2.0 %collective-permute-done.20 = f32[16,4]{1,0:T(8,128)S(1)} collective-permute-done((f32[16,4]{1,0:T(8,128)S(1)}, f32[16,4]{1,0:T(8,128)S(1)}, u32[]{:S(2)}, u32[]{:S(2)}) %collective-permute-start.20) | collective-permute-done | bytes 288 | tf_op jit(solution)/shard_map/ppermute | solution.py:240
  58.5 1.5 %collective-permute-start.8 = (bf16[256,512]{1,0:T(8,128)(2,1)}, bf16[256,512]{1,0:T(8,128)(2,1)S(1)}, u32[]{:S(2)}, u32[]{:S(2)}) collective-permute-start(bf16[256,512]{1,0:T(8,128)(2,1)} %get-tuple-element.28), channel_id=1, source_target_pairs={{0,4},{4,0},{8,12},{12,8},{16,20},{20,16},{24,28},{28,24},{1,5},{5... | collective-permute-start | bytes 786440 | tf_op jit(solution)/shard_map/ppermute | solution.py:240
  60.0 0.7 collective-permute-start.9
  60.7 1.3 %collective-permute-start.10 = (bf16[256,512]{1,0:T(8,128)(2,1)}, bf16[256,512]{1,0:T(8,128)(2,1)S(1)}, u32[]{:S(2)}, u32[]{:S(2)}) collective-permute-start(bf16[256,512]{1,0:T(8,128)(2,1)} %get-tuple-element.30), channel_id=1, source_target_pairs={{0,12},{4,8},{8,4},{12,0},{16,28},{20,24},{24,20},{28,16},{1,13},{... | collective-permute-start | bytes 786440 | tf_op jit(solution)/shard_map/ppermute | solution.py:240
  62.0 3.2 %shard_map.121 = (bf16[2,256,512]{2,1,0:T(8,128)(2,1)}, bf16[2,256,512]{2,1,0:T(8,128)(2,1)}) custom-call(s32[1]{0:T(128)} %bitcast.head_ref.refs_0_, bf16[256,512]{1,0:T(8,128)(2,1)} %shard_map.120.attn_ref.refs_4_, bf16[512,2048]{1,0:T(8,128)(2,1)} %refs_6_.1), custom_call_target="tpu_custom_call" | custom-call | flops 536870912 | bytes 3407876 | tf_op jit(solution)/shard_map/pallas_call | solution.py:35
  65.3 0.7 copy.13
  65.9 2.0 %collective-permute-done.8.refs_1_ = bf16[256,512]{1,0:T(8,128)(2,1)S(1)} collective-permute-done((bf16[256,512]{1,0:T(8,128)(2,1)}, bf16[256,512]{1,0:T(8,128)(2,1)S(1)}, u32[]{:S(2)}, u32[]{:S(2)}) %collective-permute-start.8) | collective-permute-done | bytes 262176 | tf_op jit(solution)/shard_map/ppermute | solution.py:240
  67.9 0.8 collective-permute-done.9.refs_2_
  68.7 2.8 %collective-permute-done.10.refs_3_ = bf16[256,512]{1,0:T(8,128)(2,1)S(1)} collective-permute-done((bf16[256,512]{1,0:T(8,128)(2,1)}, bf16[256,512]{1,0:T(8,128)(2,1)S(1)}, u32[]{:S(2)}, u32[]{:S(2)}) %collective-permute-start.10) | collective-permute-done | bytes 262176 | tf_op jit(solution)/shard_map/ppermute | solution.py:240
  71.5 0.7 copy-done.8
  72.2 2.7 %shard_map.124 = bf16[1,256,512]{2,1,0:T(8,128)(2,1)} custom-call(s32[1]{0:T(128)} %bitcast.1.seq_ref.refs_1_, bf16[256,512]{1,0:T(8,128)(2,1)} %get-tuple-element.27.refs_0_, bf16[256,512]{1,0:T(8,128)(2,1)} %copy-done.6, bf16[256,512]{1,0:T(8,128)(2,1)} %copy-done.7, bf16[256,512]{1,0:T(8,128)(2,1)} %copy-done.8, ...), custom_call_target="tpu_custom_call" | custom-call | flops 268435456 | bytes 2359300 | tf_op jit(solution)/shard_map/pallas_call | solution.py:35
  75.0 2.6 %collective-permute-start.14 = (bf16[1,256,512]{2,1,0:T(8,128)(2,1)}, bf16[1,256,512]{2,1,0:T(8,128)(2,1)S(1)}, u32[]{:S(2)}, u32[]{:S(2)}) collective-permute-start(bf16[1,256,512]{2,1,0:T(8,128)(2,1)} %shard_map.124), channel_id=1, source_target_pairs={{0,16},{4,20},{8,24},{12,28},{16,0},{20,4},{24,8},{28,12},{1,17},{... | collective-permute-start | bytes 786440 | tf_op jit(solution)/shard_map/ppermute | solution.py:240
  77.5 2.8 %shard_map.123 = f32[1,256,512]{2,1,0:T(8,128)} custom-call(s32[1]{0:T(128)} %bitcast.1.seq_ref.refs_1_, bf16[256,512]{1,0:T(8,128)(2,1)} %get-tuple-element.27.refs_0_, bf16[256,512]{1,0:T(8,128)(2,1)} %copy-done.6, bf16[256,512]{1,0:T(8,128)(2,1)} %copy-done.7, bf16[256,512]{1,0:T(8,128)(2,1)} %copy-done.8, bf16[256,512]{1,0:T(8,128)(2,1)} %shard_map.120.attn_ref.refs_4_, ...), custom_call_target="tpu_custom_call" | custom-call | flops 268435456 | bytes 2621444 | tf_op jit(solution)/shard_map/pallas_call | solution.py:35
  80.4 0.4 collective-permute-start.16
  80.8 1.6 %collective-permute-start.4 = (bf16[1,256,512]{2,1,0:T(8,128)(2,1)S(1)}, bf16[1,256,512]{2,1,0:T(8,128)(2,1)S(1)}, u32[]{:S(2)}, u32[]{:S(2)}) collective-permute-start(bf16[1,256,512]{2,1,0:T(8,128)(2,1)S(1)} %add_convert_fusion.2), channel_id=1, source_target_pairs={{0,2},{1,3},{2,0},{3,1},{4,6},{5,7},{6,4},{7,5},{8,10},{9,11},{10,... | collective-permute-start | bytes 786440 | tf_op jit(solution)/shard_map/ppermute | solution.py:240
  82.4 3.8 %collective-permute-done.14 = bf16[1,256,512]{2,1,0:T(8,128)(2,1)S(1)} collective-permute-done((bf16[1,256,512]{2,1,0:T(8,128)(2,1)}, bf16[1,256,512]{2,1,0:T(8,128)(2,1)S(1)}, u32[]{:S(2)}, u32[]{:S(2)}) %collective-permute-start.14) | collective-permute-done | bytes 262176 | tf_op jit(solution)/shard_map/ppermute | solution.py:240
  86.3 1.9 %add_bitcast_fusion = f32[256,512]{1,0:T(8,128)} fusion(f32[1,256,512]{2,1,0:T(8,128)} %shard_map.123, bf16[1,256,512]{2,1,0:T(8,128)(2,1)S(1)} %collective-permute-done.14), kind=kLoop, calls=%fused_computation.1 | loop fusion | flops 262144 | bytes 1310720 | tf_op jit(solution)/shard_map/add | solution.py:251
  88.2 0.8 collective-permute-done.16.rest_1_
  89.1 0.8 fusion
  89.9 5.4 %collective-permute-done.17.rest_2_ = bf16[1,512,128]{2,1,0:T(8,128)(2,1)S(1)} collective-permute-done((bf16[1,512,128]{2,1,0:T(8,128)(2,1)S(1)}, bf16[1,512,128]{2,1,0:T(8,128)(2,1)S(1)}, u32[]{:S(2)}, u32[]{:S(2)}) %collective-permute-start.17) | collective-permute-done | bytes 131104 | tf_op jit(solution)/shard_map/ppermute | solution.py:240
  95.4 0.6 copy-done.16
  96.0 2.7 %shard_map.126 = (bf16[256,512]{1,0:T(8,128)(2,1)}, bf16[256,512]{1,0:T(8,128)(2,1)}) custom-call(s32[1]{0:T(128)} %bitcast.1.seq_ref.refs_1_, bf16[256,512]{1,0:T(8,128)(2,1)} %k_ref.7, bf16[256,512]{1,0:T(8,128)(2,1)} %v_ref.7, f32[256,512]{1,0:T(8,128)} %get-tuple-element.34.dk_in, f32[256,512]{1,0:T(8,128)} %get-tuple-element.35.dv_in, ...), custom_call_target="tpu_custom_call" | custom-call | flops 67108864 | bytes 2883588 | tf_op jit(solution)/shard_map/pallas_call | solution.py:35
  (48 shorter events, 0.5 us)
Async XLA Ops:
  2.6 6.7 %collective-permute-start = (bf16[512,128]{1,0:T(8,128)(2,1)}, bf16[512,128]{1,0:T(8,128)(2,1)S(1)}, u32[]{:S(2)}, u32[]{:S(2)}) collective-permute-start(bf16[512,128]{1,0:T(8,128)(2,1)} %shard_map.119), channel_id=1, source_target_pairs={{0,4},{4,0},{8,12},{12,8},{16,20},{20,16},{24,28},{28,24},{1,5},{5... | collective-permute-start | bytes 393224 | tf_op jit(solution)/shard_map/ppermute | solution.py:240
  9.3 13.4 %copy-start = (bf16[512,128]{1,0:T(8,128)(2,1)}, bf16[512,128]{1,0:T(8,128)(2,1)S(1)}, u32[]{:S(2)}) copy-start(bf16[512,128]{1,0:T(8,128)(2,1)S(1)} %collective-permute-done.rest_0_) | copy-start | bytes 393220
  10.3 5.0 %collective-permute-start.1 = (bf16[512,128]{1,0:T(8,128)(2,1)S(1)}, bf16[512,128]{1,0:T(8,128)(2,1)S(1)}, u32[]{:S(2)}, u32[]{:S(2)}) collective-permute-start(bf16[512,128]{1,0:T(8,128)(2,1)S(1)} %add_convert_fusion.5), channel_id=1, source_target_pairs={{0,8},{4,12},{8,0},{12,4},{16,24},{20,28},{24,16},{28,20},{1,9},{5... | collective-permute-start | bytes 393224 | tf_op jit(solution)/shard_map/ppermute | solution.py:240
  12.1 7.1 %collective-permute-start.6 = (bf16[256,512]{1,0:T(8,128)(2,1)}, bf16[256,512]{1,0:T(8,128)(2,1)S(1)}, u32[]{:S(2)}, u32[]{:S(2)}) collective-permute-start(bf16[256,512]{1,0:T(8,128)(2,1)} %refs_2_.1), channel_id=1, source_target_pairs={{0,2},{1,3},{2,0},{3,1},{4,6},{5,7},{6,4},{7,5},{8,10},{9,11},{10,... | collective-permute-start | bytes 786440 | tf_op jit(solution)/shard_map/ppermute | solution.py:240
  15.3 7.4 %copy-start.1 = (bf16[512,128]{1,0:T(8,128)(2,1)}, bf16[512,128]{1,0:T(8,128)(2,1)S(1)}, u32[]{:S(2)}) copy-start(bf16[512,128]{1,0:T(8,128)(2,1)S(1)} %collective-permute-done.1.rest_1_) | copy-start | bytes 393220
  15.3 7.3 %collective-permute-start.2 = (bf16[512,128]{1,0:T(8,128)(2,1)S(1)}, bf16[512,128]{1,0:T(8,128)(2,1)S(1)}, u32[]{:S(2)}, u32[]{:S(2)}) collective-permute-start(bf16[512,128]{1,0:T(8,128)(2,1)S(1)} %add_convert_fusion.4), channel_id=1, source_target_pairs={{0,16},{4,20},{8,24},{12,28},{16,0},{20,4},{24,8},{28,12},{1,17},{... | collective-permute-start | bytes 393224 | tf_op jit(solution)/shard_map/ppermute | solution.py:240
  18.2 11.1 %collective-permute-start.5 = (bf16[256,512]{1,0:T(8,128)(2,1)}, bf16[256,512]{1,0:T(8,128)(2,1)S(1)}, u32[]{:S(2)}, u32[]{:S(2)}) collective-permute-start(bf16[256,512]{1,0:T(8,128)(2,1)} %refs_2_.1), channel_id=1, source_target_pairs={{0,1},{1,0},{2,3},{3,2},{4,5},{5,4},{6,7},{7,6},{8,9},{9,8},{10,11... | collective-permute-start | bytes 786440 | tf_op jit(solution)/shard_map/ppermute | solution.py:240
  19.3 10.1 %copy-start.12 = (bf16[256,512]{1,0:T(8,128)(2,1)}, bf16[256,512]{1,0:T(8,128)(2,1)S(1)}, u32[]{:S(2)}) copy-start(bf16[256,512]{1,0:T(8,128)(2,1)S(1)} %collective-permute-done.6.refs_4_) | copy-start | bytes 786436
  19.3 10.1 %collective-permute-start.7 = (bf16[256,512]{1,0:T(8,128)(2,1)S(1)}, bf16[256,512]{1,0:T(8,128)(2,1)S(1)}, u32[]{:S(2)}, u32[]{:S(2)}) collective-permute-start(bf16[256,512]{1,0:T(8,128)(2,1)S(1)} %collective-permute-done.6.refs_4_), channel_id=1, source_target_pairs={{0,1},{1,0},{2,3},{3,2},{4,5},{5,4},{6,7},{7,6},{8,9},{9,8},{10,11... | collective-permute-start | bytes 786440 | tf_op jit(solution)/shard_map/ppermute | solution.py:240
  22.7 0.7 copy-start.10
  25.9 34.2 %collective-permute-start.13 = (bf16[256,512]{1,0:T(8,128)(2,1)}, bf16[256,512]{1,0:T(8,128)(2,1)S(1)}, u32[]{:S(2)}, u32[]{:S(2)}) collective-permute-start(bf16[256,512]{1,0:T(8,128)(2,1)} %shard_map.120.attn_ref.refs_4_), channel_id=1, source_target_pairs={{0,12},{4,8},{8,4},{12,0},{16,28},{20,24},{24,20},{28,16},{1,13},{... | collective-permute-start | bytes 786440 | tf_op jit(solution)/shard_map/ppermute | solution.py:240
  27.7 33.0 %collective-permute-start.12 = (bf16[256,512]{1,0:T(8,128)(2,1)}, bf16[256,512]{1,0:T(8,128)(2,1)S(1)}, u32[]{:S(2)}, u32[]{:S(2)}) collective-permute-start(bf16[256,512]{1,0:T(8,128)(2,1)} %shard_map.120.attn_ref.refs_4_), channel_id=1, source_target_pairs={{0,8},{4,12},{8,0},{12,4},{16,24},{20,28},{24,16},{28,20},{1,9},{5... | collective-permute-start | bytes 786440 | tf_op jit(solution)/shard_map/ppermute | solution.py:240
  29.1 36.2 %collective-permute-start.11 = (bf16[256,512]{1,0:T(8,128)(2,1)}, bf16[256,512]{1,0:T(8,128)(2,1)S(1)}, u32[]{:S(2)}, u32[]{:S(2)}) collective-permute-start(bf16[256,512]{1,0:T(8,128)(2,1)} %shard_map.120.attn_ref.refs_4_), channel_id=1, source_target_pairs={{0,4},{4,0},{8,12},{12,8},{16,20},{20,16},{24,28},{28,24},{1,5},{5... | collective-permute-start | bytes 786440 | tf_op jit(solution)/shard_map/ppermute | solution.py:240
  29.4 0.7 copy-start.13
  29.4 0.8 copy-start.14
  34.4 45.9 %collective-permute-start.15 = (bf16[3,512,128]{2,1,0:T(8,128)(2,1)}, bf16[3,512,128]{2,1,0:T(8,128)(2,1)S(1)}, u32[]{:S(2)}, u32[]{:S(2)}) collective-permute-start(bf16[3,512,128]{2,1,0:T(8,128)(2,1)} %get-tuple-element.36), channel_id=1, source_target_pairs={{0,4},{4,0},{8,12},{12,8},{16,20},{20,16},{24,28},{28,24},{1,5},{5... | collective-permute-start | bytes 1179656 | tf_op jit(solution)/shard_map/ppermute | solution.py:240
  42.2 7.4 %collective-permute-start.18 = (f32[16,4]{1,0:T(8,128)}, f32[16,4]{1,0:T(8,128)S(1)}, u32[]{:S(2)}, u32[]{:S(2)}) collective-permute-start(f32[16,4]{1,0:T(8,128)} %get-tuple-element.39), channel_id=1, source_target_pairs={{0,4},{4,0},{8,12},{12,8},{16,20},{20,16},{24,28},{28,24},{1,5},{5... | collective-permute-start | bytes 776 | tf_op jit(solution)/shard_map/ppermute | solution.py:240
  50.3 3.7 %collective-permute-start.19 = (f32[16,4]{1,0:T(8,128)S(1)}, f32[16,4]{1,0:T(8,128)S(1)}, u32[]{:S(2)}, u32[]{:S(2)}) collective-permute-start(f32[16,4]{1,0:T(8,128)S(1)} %add.47), channel_id=1, source_target_pairs={{0,8},{4,12},{8,0},{12,4},{16,24},{20,28},{24,16},{28,20},{1,9},{5... | collective-permute-start | bytes 776 | tf_op jit(solution)/shard_map/ppermute | solution.py:240
  54.0 4.5 %collective-permute-start.20 = (f32[16,4]{1,0:T(8,128)S(1)}, f32[16,4]{1,0:T(8,128)S(1)}, u32[]{:S(2)}, u32[]{:S(2)}) collective-permute-start(f32[16,4]{1,0:T(8,128)S(1)} %add.48), channel_id=1, source_target_pairs={{0,16},{4,20},{8,24},{12,28},{16,0},{20,4},{24,8},{28,12},{1,17},{... | collective-permute-start | bytes 776 | tf_op jit(solution)/shard_map/ppermute | solution.py:240
  58.5 9.4 %collective-permute-start.8 = (bf16[256,512]{1,0:T(8,128)(2,1)}, bf16[256,512]{1,0:T(8,128)(2,1)S(1)}, u32[]{:S(2)}, u32[]{:S(2)}) collective-permute-start(bf16[256,512]{1,0:T(8,128)(2,1)} %get-tuple-element.28), channel_id=1, source_target_pairs={{0,4},{4,0},{8,12},{12,8},{16,20},{20,16},{24,28},{28,24},{1,5},{5... | collective-permute-start | bytes 786440 | tf_op jit(solution)/shard_map/ppermute | solution.py:240
  60.0 11.5 %copy-start.3 = (bf16[256,512]{1,0:T(8,128)(2,1)}, bf16[256,512]{1,0:T(8,128)(2,1)S(1)}, u32[]{:S(2)}) copy-start(bf16[256,512]{1,0:T(8,128)(2,1)S(1)} %collective-permute-done.13.refs_7_) | copy-start | bytes 786436
  60.0 8.7 %collective-permute-start.9 = (bf16[256,512]{1,0:T(8,128)(2,1)}, bf16[256,512]{1,0:T(8,128)(2,1)S(1)}, u32[]{:S(2)}, u32[]{:S(2)}) collective-permute-start(bf16[256,512]{1,0:T(8,128)(2,1)} %get-tuple-element.29), channel_id=1, source_target_pairs={{0,8},{4,12},{8,0},{12,4},{16,24},{20,28},{24,16},{28,20},{1,9},{5... | collective-permute-start | bytes 786440 | tf_op jit(solution)/shard_map/ppermute | solution.py:240
  60.7 10.8 %copy-start.4 = (bf16[256,512]{1,0:T(8,128)(2,1)}, bf16[256,512]{1,0:T(8,128)(2,1)S(1)}, u32[]{:S(2)}) copy-start(bf16[256,512]{1,0:T(8,128)(2,1)S(1)} %collective-permute-done.12.refs_6_) | copy-start | bytes 786436
  60.7 10.8 %collective-permute-start.10 = (bf16[256,512]{1,0:T(8,128)(2,1)}, bf16[256,512]{1,0:T(8,128)(2,1)S(1)}, u32[]{:S(2)}, u32[]{:S(2)}) collective-permute-start(bf16[256,512]{1,0:T(8,128)(2,1)} %get-tuple-element.30), channel_id=1, source_target_pairs={{0,12},{4,8},{8,4},{12,0},{16,28},{20,24},{24,20},{28,16},{1,13},{... | collective-permute-start | bytes 786440 | tf_op jit(solution)/shard_map/ppermute | solution.py:240
  65.3 6.2 %copy-start.5 = (bf16[256,512]{1,0:T(8,128)(2,1)}, bf16[256,512]{1,0:T(8,128)(2,1)S(1)}, u32[]{:S(2)}) copy-start(bf16[256,512]{1,0:T(8,128)(2,1)S(1)} %collective-permute-done.11.refs_5_) | copy-start | bytes 786436
  65.3 15.5 %collective-permute-start.3 = (bf16[2,256,512]{2,1,0:T(8,128)(2,1)}, bf16[2,256,512]{2,1,0:T(8,128)(2,1)S(1)}, u32[]{:S(2)}, u32[]{:S(2)}) collective-permute-start(bf16[2,256,512]{2,1,0:T(8,128)(2,1)} %get-tuple-element.26), channel_id=1, source_target_pairs={{0,1},{1,0},{2,3},{3,2},{4,5},{5,4},{6,7},{7,6},{8,9},{9,8},{10,11... | collective-permute-start | bytes 1572872 | tf_op jit(solution)/shard_map/ppermute | solution.py:240
  67.9 3.6 %copy-start.6 = (bf16[256,512]{1,0:T(8,128)(2,1)}, bf16[256,512]{1,0:T(8,128)(2,1)S(1)}, u32[]{:S(2)}) copy-start(bf16[256,512]{1,0:T(8,128)(2,1)S(1)} %collective-permute-done.8.refs_1_) | copy-start | bytes 786436
  68.7 2.8 %copy-start.7 = (bf16[256,512]{1,0:T(8,128)(2,1)}, bf16[256,512]{1,0:T(8,128)(2,1)S(1)}, u32[]{:S(2)}) copy-start(bf16[256,512]{1,0:T(8,128)(2,1)S(1)} %collective-permute-done.9.refs_2_) | copy-start | bytes 786436
  71.5 0.7 copy-start.8
  72.2 8.1 %copy-start.15 = (bf16[3,512,128]{2,1,0:T(8,128)(2,1)S(1)}, bf16[3,512,128]{2,1,0:T(8,128)(2,1)}, u32[]{:S(2)}) copy-start(bf16[3,512,128]{2,1,0:T(8,128)(2,1)} %get-tuple-element.36) | copy-start | bytes 1179652
  75.0 5.8 %copy-start.11 = (bf16[2,256,512]{2,1,0:T(8,128)(2,1)S(1)}, bf16[2,256,512]{2,1,0:T(8,128)(2,1)}, u32[]{:S(2)}) copy-start(bf16[2,256,512]{2,1,0:T(8,128)(2,1)} %get-tuple-element.25) | copy-start | bytes 1572868
  75.0 11.3 %collective-permute-start.14 = (bf16[1,256,512]{2,1,0:T(8,128)(2,1)}, bf16[1,256,512]{2,1,0:T(8,128)(2,1)S(1)}, u32[]{:S(2)}, u32[]{:S(2)}) collective-permute-start(bf16[1,256,512]{2,1,0:T(8,128)(2,1)} %shard_map.124), channel_id=1, source_target_pairs={{0,16},{4,20},{8,24},{12,28},{16,0},{20,4},{24,8},{28,12},{1,17},{... | collective-permute-start | bytes 786440 | tf_op jit(solution)/shard_map/ppermute | solution.py:240
  80.3 9.6 %copy-start.2 = (bf16[3,512,128]{2,1,0:T(8,128)(2,1)}, bf16[3,512,128]{2,1,0:T(8,128)(2,1)S(1)}, u32[]{:S(2)}) copy-start(bf16[3,512,128]{2,1,0:T(8,128)(2,1)S(1)} %collective-permute-done.15.rest_0_) | copy-start | bytes 1179652
  80.4 8.6 %collective-permute-start.16 = (bf16[2,512,128]{2,1,0:T(8,128)(2,1)S(1)}, bf16[2,512,128]{2,1,0:T(8,128)(2,1)S(1)}, u32[]{:S(2)}, u32[]{:S(2)}) collective-permute-start(bf16[2,512,128]{2,1,0:T(8,128)(2,1)S(1)} %add_convert_fusion), channel_id=1, source_target_pairs={{0,8},{4,12},{8,0},{12,4},{16,24},{20,28},{24,16},{28,20},{1,9},{5... | collective-permute-start | bytes 786440 | tf_op jit(solution)/shard_map/ppermute | solution.py:240
  80.8 8.3 %collective-permute-start.4 = (bf16[1,256,512]{2,1,0:T(8,128)(2,1)S(1)}, bf16[1,256,512]{2,1,0:T(8,128)(2,1)S(1)}, u32[]{:S(2)}, u32[]{:S(2)}) collective-permute-start(bf16[1,256,512]{2,1,0:T(8,128)(2,1)S(1)} %add_convert_fusion.2), channel_id=1, source_target_pairs={{0,2},{1,3},{2,0},{3,1},{4,6},{5,7},{6,4},{7,5},{8,10},{9,11},{10,... | collective-permute-start | bytes 786440 | tf_op jit(solution)/shard_map/ppermute | solution.py:240
  89.0 6.4 %copy-start.9 = (bf16[2,512,128]{2,1,0:T(8,128)(2,1)}, bf16[2,512,128]{2,1,0:T(8,128)(2,1)S(1)}, u32[]{:S(2)}) copy-start(bf16[2,512,128]{2,1,0:T(8,128)(2,1)S(1)} %collective-permute-done.16.rest_1_) | copy-start | bytes 786436
  89.0 6.3 %collective-permute-start.17 = (bf16[1,512,128]{2,1,0:T(8,128)(2,1)S(1)}, bf16[1,512,128]{2,1,0:T(8,128)(2,1)S(1)}, u32[]{:S(2)}, u32[]{:S(2)}) collective-permute-start(bf16[1,512,128]{2,1,0:T(8,128)(2,1)S(1)} %add_convert_fusion.3), channel_id=1, source_target_pairs={{0,16},{4,20},{8,24},{12,28},{16,0},{20,4},{24,8},{28,12},{1,17},{... | collective-permute-start | bytes 393224 | tf_op jit(solution)/shard_map/ppermute | solution.py:240
  95.4 0.6 copy-start.16
